TPU v7x, 256 devices: a whole 4x4x8 slice. The times are simulated.
256 devices in a mesh: band: 32 (over x_hi, z, core), fft: 8 (over x_lo, y).
Axes of the slice: x: 4 (x_hi: 2, x_lo: 2; x = x_hi * 2 + x_lo), y: 4, z: 8, core: 2. Of those that a mesh axis runs over, the one named last changes fastest.
Arguments:
- orbitals: float32 [64, 64, 4096], P('band', 'fft'), may hold values from -5 to 5
Outputs:
- exchange: float32 [64, 64, 4096], P('band', 'fft')
All inputs are finite; a program needn't handle non-finite values.
Results may differ from a plain program's by a relative error of at most 0.00018.
Values sent between devices are 32-bit elements; how exact they have to be, the bound alone decides.
No kernel may reach another device: no remote copies, remote signals or barrier semaphores. Data moves between devices by JAX's collectives and lax.ppermute only.
A program may use at most 64 MiB of HBM per device.

v0:
```python
import math

import jax
import jax.numpy as jnp
from jax import lax
from jax.experimental import pallas as pl
from jax.experimental.pallas import tpu as pltpu
from jax.sharding import PartitionSpec as P


GRID = 64
EXX_FRACTION = 0.25
SCREEN = 0.05
PLANES = 8
LANES = 128


ORDER = (6, 7, 5, 4, 2, 3, 1)
REACH = (4, 3, 5, 2, 6, 1, 7)


def split_table(table, axis):
    high = lax.reduce_precision(table, 8, 7)
    return jnp.concatenate([high, high, table - high], axis).astype(jnp.bfloat16)


def wave(rows, columns, direction):
    angles = (rows[:, None] * columns[None, :] % GRID).astype(jnp.float32) * (2.0 * math.pi / GRID)
    return jnp.cos(angles), direction * jnp.sin(angles)


def left_table(rows, columns, direction):
    cosine, sine = wave(rows, columns, direction)
    top = jnp.concatenate([cosine, -sine], 1)
    bottom = jnp.concatenate([sine, cosine], 1)
    return split_table(jnp.concatenate([top, bottom], 0), 1)


def right_table(direction):
    index = jnp.arange(GRID, dtype=jnp.int32)
    cosine, sine = wave(index, index, direction)
    zero = jnp.zeros_like(cosine)
    table = jnp.concatenate(
        [
            jnp.concatenate([cosine, zero, sine, zero], 1),
            jnp.concatenate([zero, cosine, zero, sine], 1),
            jnp.concatenate([-sine, zero, cosine, zero], 1),
            jnp.concatenate([zero, -sine, zero, cosine], 1),
        ],
        0,
    )
    return split_table(table, 0)


def filter_table(y_offset):
    indices = jnp.arange(GRID, dtype=jnp.int32)
    signed = jnp.where(indices < GRID // 2, indices, indices - GRID).astype(jnp.float32)
    wavenum = signed * (2.0 * math.pi / GRID)
    y_indices = y_offset + jnp.arange(PLANES, dtype=jnp.int32)
    y_signed = jnp.where(y_indices < GRID // 2, y_indices, y_indices - GRID).astype(jnp.float32)
    y_wavenum = y_signed * (2.0 * math.pi / GRID)
    wide = jnp.concatenate([wavenum, wavenum])
    squares = wavenum[None, :, None] ** 2 + y_wavenum[:, None, None] ** 2 + wide[None, None, :] ** 2
    guarded = jnp.where(squares > 0, squares, 1.0)
    kernel = jnp.where(
        squares > 0, (1.0 - jnp.exp(-guarded / (4.0 * SCREEN * SCREEN))) / guarded, 0.0
    )
    return kernel * (-EXX_FRACTION / float(GRID) ** 3)


def parts(values):
    high = values.astype(jnp.bfloat16)
    low = (values - high.astype(jnp.float32)).astype(jnp.bfloat16)
    return high, low


def times_left(table, values):
    high, low = parts(values)
    stacked = jnp.concatenate([high, low, high], 0)
    return jnp.dot(table, stacked, preferred_element_type=jnp.float32)


def times_right(values, table):
    high, low = parts(values)
    stacked = jnp.concatenate([high, low, high], 1)
    return jnp.dot(stacked, table, preferred_element_type=jnp.float32)


def pair_sources(own_refs, other_refs, part, y_half, low_lanes):
    columns = slice(y_half * LANES, (y_half + 1) * LANES)
    own, other = own_refs[part][:, columns], other_refs[part][:, columns]
    even = jnp.where(low_lanes, own, pltpu.roll(other, GRID, 1))
    odd = jnp.where(low_lanes, pltpu.roll(own, GRID, 1), other)
    return even, odd


def forward_kernel(orb_ref, *refs):
    own_refs, other_refs, (right_ref, left_ref) = refs[:2], refs[2:4], refs[4:6]
    out_refs, (pair_ref, work_ref) = refs[6:14], refs[14:]
    low_lanes = lax.broadcasted_iota(jnp.int32, (PLANES, LANES), 1) < GRID
    for y_half in range(GRID // 2):
        for part in range(2):
            even, odd = pair_sources(own_refs, other_refs, part, y_half, low_lanes)
            for i in range(2):
                tile = orb_ref[i, :, y_half * LANES : (y_half + 1) * LANES]
                turned = pltpu.roll(tile, GRID, 1)
                base = y_half * 2 * PLANES
                lanes = slice(part * LANES, (part + 1) * LANES)
                pair_ref[i, base : base + PLANES, lanes] = (
                    jnp.where(low_lanes, tile, turned) * even
                )
                pair_ref[i, base + PLANES : base + 2 * PLANES, lanes] = (
                    jnp.where(low_lanes, turned, tile) * odd
                )
    for i in range(2):
        result = times_right(pair_ref[i], right_ref[...])
        work_ref[0] = result[:, :LANES]
        work_ref[1] = result[:, LANES:]
        for x in range(0, PLANES, 2):
            columns = []
            for plane in (x, x + 1):
                rows = [work_ref[part, pl.ds(plane, GRID, stride=PLANES), :] for part in range(2)]
                columns.append(jnp.concatenate(rows, 0))
            result = times_left(left_ref[...], jnp.concatenate(columns, 1))
            for k in range(2):
                for part in range(2):
                    for block in range(8):
                        top = part * GRID + block * PLANES
                        out_refs[block][i, x + k, part] = result[
                            top : top + PLANES, k * LANES : (k + 1) * LANES
                        ]


def middle_kernel(*refs):
    in_refs, (forth_ref, back_ref, filter_ref), out_refs = refs[:8], refs[8:11], refs[11:]
    for i in range(2):
        for ky in range(0, PLANES, 2):
            columns = []
            for y in (ky, ky + 1):
                rows = []
                for part in range(2):
                    for block in range(8):
                        start = i * 128 + part * 8 + y
                        rows.append(in_refs[block][pl.ds(start, PLANES, stride=16), :])
                columns.append(jnp.concatenate(rows, 0))
            spectrum = times_left(forth_ref[...], jnp.concatenate(columns, 1))
            scale = jnp.concatenate([filter_ref[ky], filter_ref[ky + 1]], 1)
            spectrum = spectrum * jnp.concatenate([scale, scale], 0)
            result = times_left(back_ref[...], spectrum)
            for k in range(2):
                for part in range(2):
                    for block in range(8):
                        start = i * 128 + part * 8 + ky + k
                        top = part * GRID + block * PLANES
                        out_refs[block][pl.ds(start, PLANES, stride=16), :] = result[
                            top : top + PLANES, k * LANES : (k + 1) * LANES
                        ]


def inverse_kernel(*refs):
    in_refs, own_refs, other_refs = refs[:8], refs[8:10], refs[10:12]
    right_ref, left_ref, out_ref, work_ref = refs[12:]
    low_lanes = lax.broadcasted_iota(jnp.int32, (PLANES, LANES), 1) < GRID
    for i in range(2):
        for x in range(0, PLANES, 2):
            columns = []
            for plane in (x, x + 1):
                rows = [ref[i, plane, part] for part in range(2) for ref in in_refs]
                columns.append(jnp.concatenate(rows, 0))
            result = times_left(left_ref[...], jnp.concatenate(columns, 1))
            for k in range(2):
                for part in range(2):
                    work_ref[part, pl.ds(x + k, GRID, stride=PLANES), :] = result[
                        part * GRID : (part + 1) * GRID, k * LANES : (k + 1) * LANES
                    ]
        potential = times_right(jnp.concatenate([work_ref[0], work_ref[1]], 1), right_ref[...])
        for y_half in range(GRID // 2):
            sums = [0.0, 0.0]
            for part in range(2):
                pair = pair_sources(own_refs, other_refs, part, y_half, low_lanes)
                for odd in range(2):
                    base = (y_half * 2 + odd) * PLANES
                    values = potential[base : base + PLANES, part * LANES : (part + 1) * LANES]
                    sums[odd] = sums[odd] + values * pair[odd]
            even, odd = (s + pltpu.roll(s, GRID, 1) for s in sums)
            out_ref[i, :, y_half * LANES : (y_half + 1) * LANES] = jnp.where(low_lanes, even, odd)


def local_call(kernel, shapes, scratch):
    return pl.pallas_call(
        kernel,
        out_shape=[jax.ShapeDtypeStruct(shape, jnp.float32) for shape in shapes],
        scratch_shapes=scratch,
        compiler_params=pltpu.CompilerParams(vmem_limit_bytes=24 << 20),
    )


def band_of(x_half, z, core):
    return x_half * 16 + z * 2 + core


def fetch_sources(orbitals):
    cores = (0, 1)
    band = lax.axis_index("band")
    x_half, z = band // 16, band // 2 % 8
    handed = lax.ppermute(
        orbitals[1], "band", [(band_of(0, 0, c), band_of(1, 0, c)) for c in cores]
    )
    root = jnp.where(x_half == 1, handed, orbitals[0])
    first = root
    for step in REACH:
        pairs = [(band_of(h, 0, c), band_of(h, step, c)) for h in cores for c in cores]
        first = jnp.where(z == step, lax.ppermute(root, "band", pairs), first)
    second = lax.ppermute(first, "band", [(b, b ^ 16) for b in range(32)])
    own = (first, second)
    other = tuple(lax.ppermute(a, "band", [(b, b ^ 1) for b in range(32)]) for a in own)
    return own, other


def exchange(blocks):
    results = list(blocks)
    for d in ORDER:
        results[d] = lax.ppermute(blocks[d], "fft", [(p, p ^ d) for p in range(8)])
    return results


def apply_exchange(orbitals):
    own, other = fetch_sources(orbitals)
    here = lax.axis_index("fft")
    filters = filter_table(here * PLANES)
    index = jnp.arange(GRID, dtype=jnp.int32)
    mixed = (index // PLANES ^ here) * PLANES + index % PLANES
    right_forth, right_back = right_table(-1.0), right_table(1.0)
    rows = PLANES * GRID
    work = pltpu.VMEM((2, rows, LANES), jnp.float32)
    block = (2, PLANES, 2, PLANES, LANES)
    flat = (2 * PLANES * 2 * PLANES, LANES)
    spectrum = local_call(
        forward_kernel,
        [block] * 8,
        [pltpu.VMEM((2, rows, 2 * LANES), jnp.float32), work],
    )(orbitals, *own, *other, right_forth, left_table(mixed, index, -1.0))
    spectrum = [a.reshape(flat) for a in exchange(spectrum)]
    filtered = local_call(middle_kernel, [flat] * 8, [])(
        *spectrum, left_table(index, mixed, -1.0), left_table(mixed, index, 1.0), filters
    )
    returned = exchange([a.reshape(block) for a in filtered])
    return local_call(inverse_kernel, [(2, PLANES, GRID * GRID)], [work])(
        *returned, *own, *other, right_back, left_table(index, mixed, 1.0)
    )[0]


def solution(mesh):
    return jax.shard_map(
        apply_exchange,
        mesh=mesh,
        in_specs=(P("band", "fft", None),),
        out_specs=P("band", "fft", None),
        check_vma=False,
    )
```

profile of v0, /device:TPU:4, one launch (start us, length us, event | category | flops | bytes accessed | tf_op | source)
XLA Modules:
  0.0 73.8 jit_solution(15744176678485404532)
XLA Ops:
  0.0 0.9 %slice_bitcast_fusion = f32[8,4096]{1,0:T(8,128)S(1)} fusion(f32[2,8,4096]{2,1,0:T(8,128)} %orb_ref.1), kind=kLoop, calls=%fused_computation.43 | loop fusion | bytes 262144 | tf_op jit(solution)/shard_map/squeeze | solution.py:207
  0.9 1.3 %collective-permute-start = (f32[8,4096]{1,0:T(8,128)S(1)}, f32[8,4096]{1,0:T(8,128)S(1)}, u32[]{:S(2)}, u32[]{:S(2)}) collective-permute-start(f32[8,4096]{1,0:T(8,128)S(1)} %slice_bitcast_fusion), channel_id=1, source_target_pairs={{0,128},{8,136},{1,129},{9,137},{2,130},{10,138},{3,131},{11,139},... | collective-permute-start | bytes 393224 | tf_op jit(solution)/shard_map/ppermute | solution.py:206
  2.2 0.0 copy-start
  2.3 0.3 fusion.51
  2.6 0.1 broadcast_add_fusion
  2.6 0.1 reduce-precision_convert_fusion.3
  2.8 6.8 %collective-permute-done = f32[8,4096]{1,0:T(8,128)S(1)} collective-permute-done((f32[8,4096]{1,0:T(8,128)S(1)}, f32[8,4096]{1,0:T(8,128)S(1)}, u32[]{:S(2)}, u32[]{:S(2)}) %collective-permute-start) | collective-permute-done | bytes 131104 | tf_op jit(solution)/shard_map/ppermute | solution.py:206
  9.6 1.3 %collective-permute-start.1 = (f32[8,4096]{1,0:T(8,128)S(1)}, f32[8,4096]{1,0:T(8,128)S(1)}, u32[]{:S(2)}, u32[]{:S(2)}) collective-permute-start(f32[8,4096]{1,0:T(8,128)S(1)} %bitcast_select_fusion), channel_id=1, source_target_pairs={{0,112},{8,120},{128,240},{136,248},{1,113},{9,121},{129,241},{137... | collective-permute-start | bytes 393224 | tf_op jit(solution)/shard_map/ppermute | solution.py:213
  10.9 1.3 %collective-permute-start.2 = (f32[8,4096]{1,0:T(8,128)S(1)}, f32[8,4096]{1,0:T(8,128)S(1)}, u32[]{:S(2)}, u32[]{:S(2)}) collective-permute-start(f32[8,4096]{1,0:T(8,128)S(1)} %bitcast_select_fusion), channel_id=1, source_target_pairs={{0,16},{8,24},{128,144},{136,152},{1,17},{9,25},{129,145},{137,153... | collective-permute-start | bytes 393224 | tf_op jit(solution)/shard_map/ppermute | solution.py:213
  12.2 0.1 broadcast_multiply_fusion.2
  12.4 1.3 %collective-permute-start.3 = (f32[8,4096]{1,0:T(8,128)S(1)}, f32[8,4096]{1,0:T(8,128)S(1)}, u32[]{:S(2)}, u32[]{:S(2)}) collective-permute-start(f32[8,4096]{1,0:T(8,128)S(1)} %bitcast_select_fusion), channel_id=1, source_target_pairs={{0,96},{8,104},{128,224},{136,232},{1,97},{9,105},{129,225},{137,2... | collective-permute-start | bytes 393224 | tf_op jit(solution)/shard_map/ppermute | solution.py:213
  13.7 1.3 %collective-permute-start.4 = (f32[8,4096]{1,0:T(8,128)S(1)}, f32[8,4096]{1,0:T(8,128)S(1)}, u32[]{:S(2)}, u32[]{:S(2)}) collective-permute-start(f32[8,4096]{1,0:T(8,128)S(1)} %bitcast_select_fusion), channel_id=1, source_target_pairs={{0,32},{8,40},{128,160},{136,168},{1,33},{9,41},{129,161},{137,169... | collective-permute-start | bytes 393224 | tf_op jit(solution)/shard_map/ppermute | solution.py:213
  15.0 1.3 %collective-permute-start.5 = (f32[8,4096]{1,0:T(8,128)S(1)}, f32[8,4096]{1,0:T(8,128)S(1)}, u32[]{:S(2)}, u32[]{:S(2)}) collective-permute-start(f32[8,4096]{1,0:T(8,128)S(1)} %bitcast_select_fusion), channel_id=1, source_target_pairs={{0,80},{8,88},{128,208},{136,216},{1,81},{9,89},{129,209},{137,217... | collective-permute-start | bytes 393224 | tf_op jit(solution)/shard_map/ppermute | solution.py:213
  16.3 0.0 collective-permute-done.1
  16.3 1.3 %collective-permute-start.6 = (f32[8,4096]{1,0:T(8,128)S(1)}, f32[8,4096]{1,0:T(8,128)S(1)}, u32[]{:S(2)}, u32[]{:S(2)}) collective-permute-start(f32[8,4096]{1,0:T(8,128)S(1)} %bitcast_select_fusion), channel_id=1, source_target_pairs={{0,48},{8,56},{128,176},{136,184},{1,49},{9,57},{129,177},{137,185... | collective-permute-start | bytes 393224 | tf_op jit(solution)/shard_map/ppermute | solution.py:213
  17.6 0.0 collective-permute-done.2
  17.6 1.3 %collective-permute-start.7 = (f32[8,4096]{1,0:T(8,128)S(1)}, f32[8,4096]{1,0:T(8,128)S(1)}, u32[]{:S(2)}, u32[]{:S(2)}) collective-permute-start(f32[8,4096]{1,0:T(8,128)S(1)} %bitcast_select_fusion), channel_id=1, source_target_pairs={{0,64},{8,72},{128,192},{136,200},{1,65},{9,73},{129,193},{137,201... | collective-permute-start | bytes 393224 | tf_op jit(solution)/shard_map/ppermute | solution.py:213
  18.9 0.1 fusion.52
  19.1 0.2 fusion.9
  19.3 0.0 collective-permute-done.3
  19.3 0.0 collective-permute-done.4
  19.3 0.0 collective-permute-done.5
  19.3 2.1 %collective-permute-done.6 = f32[8,4096]{1,0:T(8,128)S(1)} collective-permute-done((f32[8,4096]{1,0:T(8,128)S(1)}, f32[8,4096]{1,0:T(8,128)S(1)}, u32[]{:S(2)}, u32[]{:S(2)}) %collective-permute-start.6) | collective-permute-done | bytes 131104 | tf_op jit(solution)/shard_map/ppermute | solution.py:213
  21.5 1.6 %collective-permute-done.7 = f32[8,4096]{1,0:T(8,128)S(1)} collective-permute-done((f32[8,4096]{1,0:T(8,128)S(1)}, f32[8,4096]{1,0:T(8,128)S(1)}, u32[]{:S(2)}, u32[]{:S(2)}) %collective-permute-start.7) | collective-permute-done | bytes 131104 | tf_op jit(solution)/shard_map/ppermute | solution.py:213
  23.1 0.4 collective-permute-start.8
  23.5 0.1 reduce-precision_convert_fusion.1
  23.6 0.1 collective-permute-start.9
  23.7 6.0 %collective-permute-done.8.refs_1_.refs_9_ = f32[8,4096]{1,0:T(8,128)S(1)} collective-permute-done((f32[8,4096]{1,0:T(8,128)S(1)}, f32[8,4096]{1,0:T(8,128)S(1)}, u32[]{:S(2)}, u32[]{:S(2)}) %collective-permute-start.8) | collective-permute-done | bytes 131104 | tf_op jit(solution)/shard_map/ppermute | solution.py:214
  29.7 0.0 collective-permute-start.10
  29.7 0.1 maximum_multiply_fusion
  29.8 0.0 collective-permute-done.9.refs_2_.refs_10_
  29.8 1.2 %collective-permute-done.10.refs_3_.refs_11_ = f32[8,4096]{1,0:T(8,128)S(1)} collective-permute-done((f32[8,4096]{1,0:T(8,128)S(1)}, f32[8,4096]{1,0:T(8,128)S(1)}, u32[]{:S(2)}, u32[]{:S(2)}) %collective-permute-start.10) | collective-permute-done | bytes 131104 | tf_op jit(solution)/shard_map/ppermute | solution.py:216
  31.0 1.9 %shard_map.17 = (f32[2,8,2,8,128]{4,3,2,1,0:T(8,128)S(1)}, f32[2,8,2,8,128]{4,3,2,1,0:T(8,128)S(1)}, f32[2,8,2,8,128]{4,3,2,1,0:T(8,128)S(1)}, f32[2,8,2,8,128]{...) custom-call(f32[2,8,4096]{2,1,0:T(8,128)S(1)} %copy-done, ...), custom_call_target="tpu_custom_call" | custom-call | tf_op jit(solution)/shard_map/pallas_call | solution.py:238
  33.0 1.7 %collective-permute-start.11 = (f32[2,8,2,8,128]{4,3,2,1,0:T(8,128)S(1)}, f32[2,8,2,8,128]{4,3,2,1,0:T(8,128)S(1)}, u32[]{:S(2)}, u32[]{:S(2)}) collective-permute-start(f32[2,8,2,8,128]{4,3,2,1,0:T(8,128)S(1)} %get-tuple-element.22), channel_id=1, source_target_pairs={{0,1},{1,0},{2,3},{3,2},{4,5},{5,4},{6,7},{7,6},{8,9},{9,8},{10,11... | collective-permute-start | bytes 393224 | tf_op jit(solution)/shard_map/ppermute | solution.py:223
  34.6 2.9 %collective-permute-start.12 = (f32[2,8,2,8,128]{4,3,2,1,0:T(8,128)S(1)}, f32[2,8,2,8,128]{4,3,2,1,0:T(8,128)S(1)}, u32[]{:S(2)}, u32[]{:S(2)}) collective-permute-start(f32[2,8,2,8,128]{4,3,2,1,0:T(8,128)S(1)} %get-tuple-element.23), channel_id=1, source_target_pairs={{0,2},{1,3},{2,0},{3,1},{4,6},{5,7},{6,4},{7,5},{8,10},{9,11},{10,... | collective-permute-start | bytes 393224 | tf_op jit(solution)/shard_map/ppermute | solution.py:223
  37.5 0.2 fusion.3.refs_10_
  37.7 0.1 reduce-precision_convert_fusion.2
  37.8 0.3 collective-permute-start.13
  38.1 1.2 %collective-permute-start.14 = (f32[2,8,2,8,128]{4,3,2,1,0:T(8,128)S(1)}, f32[2,8,2,8,128]{4,3,2,1,0:T(8,128)S(1)}, u32[]{:S(2)}, u32[]{:S(2)}) collective-permute-start(f32[2,8,2,8,128]{4,3,2,1,0:T(8,128)S(1)} %get-tuple-element.25), channel_id=1, source_target_pairs={{0,4},{1,5},{2,6},{3,7},{4,0},{5,1},{6,2},{7,3},{8,12},{9,13},{10,... | collective-permute-start | bytes 393224 | tf_op jit(solution)/shard_map/ppermute | solution.py:223
  39.3 0.6 collective-permute-start.15
  39.9 0.0 collective-permute-done.11
  39.9 4.7 %collective-permute-start.16 = (f32[2,8,2,8,128]{4,3,2,1,0:T(8,128)S(1)}, f32[2,8,2,8,128]{4,3,2,1,0:T(8,128)S(1)}, u32[]{:S(2)}, u32[]{:S(2)}) collective-permute-start(f32[2,8,2,8,128]{4,3,2,1,0:T(8,128)S(1)} %get-tuple-element.27), channel_id=1, source_target_pairs={{0,6},{1,7},{2,4},{3,5},{4,2},{5,3},{6,0},{7,1},{8,14},{9,15},{10,... | collective-permute-start | bytes 393224 | tf_op jit(solution)/shard_map/ppermute | solution.py:223
  44.7 0.0 collective-permute-done.12
  44.7 0.5 collective-permute-start.17
  45.2 0.1 fusion.43
  45.4 1.8 %collective-permute-done.13 = f32[2,8,2,8,128]{4,3,2,1,0:T(8,128)S(1)} collective-permute-done((f32[2,8,2,8,128]{4,3,2,1,0:T(8,128)S(1)}, f32[2,8,2,8,128]{4,3,2,1,0:T(8,128)S(1)}, u32[]{:S(2)}, u32[]{:S(2)}) %collective-permute-start.13) | collective-permute-done | bytes 131104 | tf_op jit(solution)/shard_map/ppermute | solution.py:223
  47.2 0.0 collective-permute-done.14
  47.2 0.0 collective-permute-done.15
  47.2 4.5 %collective-permute-done.16 = f32[2,8,2,8,128]{4,3,2,1,0:T(8,128)S(1)} collective-permute-done((f32[2,8,2,8,128]{4,3,2,1,0:T(8,128)S(1)}, f32[2,8,2,8,128]{4,3,2,1,0:T(8,128)S(1)}, u32[]{:S(2)}, u32[]{:S(2)}) %collective-permute-start.16) | collective-permute-done | bytes 131104 | tf_op jit(solution)/shard_map/ppermute | solution.py:223
  51.7 2.0 %collective-permute-done.17 = f32[2,8,2,8,128]{4,3,2,1,0:T(8,128)S(1)} collective-permute-done((f32[2,8,2,8,128]{4,3,2,1,0:T(8,128)S(1)}, f32[2,8,2,8,128]{4,3,2,1,0:T(8,128)S(1)}, u32[]{:S(2)}, u32[]{:S(2)}) %collective-permute-start.17) | collective-permute-done | bytes 131104 | tf_op jit(solution)/shard_map/ppermute | solution.py:223
  53.7 1.1 %shard_map.18 = (f32[256,128]{1,0:T(8,128)S(1)}, f32[256,128]{1,0:T(8,128)S(1)}, f32[256,128]{1,0:T(8,128)S(1)}, f32[256,128]{1,0:T(8,128)S(1)}, f32[256,128]{1,...) custom-call(f32[256,128]{1,0:T(8,128)S(1)} %bitcast.20, ...), custom_call_target="tpu_custom_call" | custom-call | tf_op jit(solution)/shard_map/pallas_call | solution.py:244
  54.8 0.2 collective-permute-start.18
  55.0 1.7 %collective-permute-start.19 = (f32[2,8,2,8,128]{4,3,2,1,0:T(8,128)S(1)}, f32[2,8,2,8,128]{4,3,2,1,0:T(8,128)S(1)}, u32[]{:S(2)}, u32[]{:S(2)}) collective-permute-start(f32[2,8,2,8,128]{4,3,2,1,0:T(8,128)S(1)} %bitcast.34), channel_id=1, source_target_pairs={{0,2},{1,3},{2,0},{3,1},{4,6},{5,7},{6,4},{7,5},{8,10},{9,11},{10,... | collective-permute-start | bytes 393224 | tf_op jit(solution)/shard_map/ppermute | solution.py:223
  56.7 0.2 fusion.10
  56.9 0.1 reduce-precision_convert_fusion
  57.0 2.9 %collective-permute-start.20 = (f32[2,8,2,8,128]{4,3,2,1,0:T(8,128)S(1)}, f32[2,8,2,8,128]{4,3,2,1,0:T(8,128)S(1)}, u32[]{:S(2)}, u32[]{:S(2)}) collective-permute-start(f32[2,8,2,8,128]{4,3,2,1,0:T(8,128)S(1)} %bitcast.33), channel_id=1, source_target_pairs={{0,3},{1,2},{2,1},{3,0},{4,7},{5,6},{6,5},{7,4},{8,11},{9,10},{10,... | collective-permute-start | bytes 393224 | tf_op jit(solution)/shard_map/ppermute | solution.py:223
  60.0 1.2 %collective-permute-start.21 = (f32[2,8,2,8,128]{4,3,2,1,0:T(8,128)S(1)}, f32[2,8,2,8,128]{4,3,2,1,0:T(8,128)S(1)}, u32[]{:S(2)}, u32[]{:S(2)}) collective-permute-start(f32[2,8,2,8,128]{4,3,2,1,0:T(8,128)S(1)} %bitcast.32), channel_id=1, source_target_pairs={{0,4},{1,5},{2,6},{3,7},{4,0},{5,1},{6,2},{7,3},{8,12},{9,13},{10,... | collective-permute-start | bytes 393224 | tf_op jit(solution)/shard_map/ppermute | solution.py:223
  61.2 2.7 %collective-permute-start.23 = (f32[2,8,2,8,128]{4,3,2,1,0:T(8,128)S(1)}, f32[2,8,2,8,128]{4,3,2,1,0:T(8,128)S(1)}, u32[]{:S(2)}, u32[]{:S(2)}) collective-permute-start(f32[2,8,2,8,128]{4,3,2,1,0:T(8,128)S(1)} %bitcast.30), channel_id=1, source_target_pairs={{0,6},{1,7},{2,4},{3,5},{4,2},{5,3},{6,0},{7,1},{8,14},{9,15},{10,... | collective-permute-start | bytes 393224 | tf_op jit(solution)/shard_map/ppermute | solution.py:223
  63.9 3.1 %collective-permute-start.24 = (f32[2,8,2,8,128]{4,3,2,1,0:T(8,128)S(1)}, f32[2,8,2,8,128]{4,3,2,1,0:T(8,128)S(1)}, u32[]{:S(2)}, u32[]{:S(2)}) collective-permute-start(f32[2,8,2,8,128]{4,3,2,1,0:T(8,128)S(1)} %bitcast.29), channel_id=1, source_target_pairs={{0,7},{1,6},{2,5},{3,4},{4,3},{5,2},{6,1},{7,0},{8,15},{9,14},{10,... | collective-permute-start | bytes 393224 | tf_op jit(solution)/shard_map/ppermute | solution.py:223
  67.1 0.0 collective-permute-done.20.refs_3_
  67.1 1.3 %collective-permute-done.22.refs_5_ = f32[2,8,2,8,128]{4,3,2,1,0:T(8,128)S(1)} collective-permute-done((f32[2,8,2,8,128]{4,3,2,1,0:T(8,128)S(1)}, f32[2,8,2,8,128]{4,3,2,1,0:T(8,128)S(1)}, u32[]{:S(2)}, u32[]{:S(2)}) %collective-permute-start.22) | collective-permute-done | bytes 131104 | tf_op jit(solution)/shard_map/ppermute | solution.py:223
  68.4 2.5 %collective-permute-done.23.refs_6_ = f32[2,8,2,8,128]{4,3,2,1,0:T(8,128)S(1)} collective-permute-done((f32[2,8,2,8,128]{4,3,2,1,0:T(8,128)S(1)}, f32[2,8,2,8,128]{4,3,2,1,0:T(8,128)S(1)}, u32[]{:S(2)}, u32[]{:S(2)}) %collective-permute-start.23) | collective-permute-done | bytes 131104 | tf_op jit(solution)/shard_map/ppermute | solution.py:223
  70.9 1.1 %collective-permute-done.24.refs_7_ = f32[2,8,2,8,128]{4,3,2,1,0:T(8,128)S(1)} collective-permute-done((f32[2,8,2,8,128]{4,3,2,1,0:T(8,128)S(1)}, f32[2,8,2,8,128]{4,3,2,1,0:T(8,128)S(1)}, u32[]{:S(2)}, u32[]{:S(2)}) %collective-permute-start.24) | collective-permute-done | bytes 131104 | tf_op jit(solution)/shard_map/ppermute | solution.py:223
  72.0 1.8 %shard_map.19 = f32[2,8,4096]{2,1,0:T(8,128)} custom-call(f32[2,8,2,8,128]{4,3,2,1,0:T(8,128)S(1)} %bitcast.22, f32[2,8,2,8,128]{4,3,2,1,0:T(8,128)S(1)} %collective-permute-done.18.refs_1_, f32[2,8,2,8,128]{4,3,2,1,0:T(8,128)S(1)} %collective-permute-done.19.refs_2_, f32[2,8,2,8,128]{4,3,2,1,0:T(8,128)S(1)} %collective-permute-done.20.refs_3_, ...), custom_call_target="tpu_custom_call" | custom-call | tf_op jit(solution)/shard_map/pallas_call | solution.py:248
  (17 shorter events, 0.2 us)
Async XLA Ops:
  0.9 8.6 %collective-permute-start = (f32[8,4096]{1,0:T(8,128)S(1)}, f32[8,4096]{1,0:T(8,128)S(1)}, u32[]{:S(2)}, u32[]{:S(2)}) collective-permute-start(f32[8,4096]{1,0:T(8,128)S(1)} %slice_bitcast_fusion), channel_id=1, source_target_pairs={{0,128},{8,136},{1,129},{9,137},{2,130},{10,138},{3,131},{11,139},... | collective-permute-start | bytes 393224 | tf_op jit(solution)/shard_map/ppermute | solution.py:206
  2.2 7.3 %copy-start = (f32[2,8,4096]{2,1,0:T(8,128)S(1)}, f32[2,8,4096]{2,1,0:T(8,128)}, u32[]{:S(2)}) copy-start(f32[2,8,4096]{2,1,0:T(8,128)} %orb_ref.1) | copy-start | bytes 786436
  9.6 6.7 %collective-permute-start.1 = (f32[8,4096]{1,0:T(8,128)S(1)}, f32[8,4096]{1,0:T(8,128)S(1)}, u32[]{:S(2)}, u32[]{:S(2)}) collective-permute-start(f32[8,4096]{1,0:T(8,128)S(1)} %bitcast_select_fusion), channel_id=1, source_target_pairs={{0,112},{8,120},{128,240},{136,248},{1,113},{9,121},{129,241},{137... | collective-permute-start | bytes 393224 | tf_op jit(solution)/shard_map/ppermute | solution.py:213
  10.9 6.7 %collective-permute-start.2 = (f32[8,4096]{1,0:T(8,128)S(1)}, f32[8,4096]{1,0:T(8,128)S(1)}, u32[]{:S(2)}, u32[]{:S(2)}) collective-permute-start(f32[8,4096]{1,0:T(8,128)S(1)} %bitcast_select_fusion), channel_id=1, source_target_pairs={{0,16},{8,24},{128,144},{136,152},{1,17},{9,25},{129,145},{137,153... | collective-permute-start | bytes 393224 | tf_op jit(solution)/shard_map/ppermute | solution.py:213
  12.4 6.9 %collective-permute-start.3 = (f32[8,4096]{1,0:T(8,128)S(1)}, f32[8,4096]{1,0:T(8,128)S(1)}, u32[]{:S(2)}, u32[]{:S(2)}) collective-permute-start(f32[8,4096]{1,0:T(8,128)S(1)} %bitcast_select_fusion), channel_id=1, source_target_pairs={{0,96},{8,104},{128,224},{136,232},{1,97},{9,105},{129,225},{137,2... | collective-permute-start | bytes 393224 | tf_op jit(solution)/shard_map/ppermute | solution.py:213
  13.7 5.6 %collective-permute-start.4 = (f32[8,4096]{1,0:T(8,128)S(1)}, f32[8,4096]{1,0:T(8,128)S(1)}, u32[]{:S(2)}, u32[]{:S(2)}) collective-permute-start(f32[8,4096]{1,0:T(8,128)S(1)} %bitcast_select_fusion), channel_id=1, source_target_pairs={{0,32},{8,40},{128,160},{136,168},{1,33},{9,41},{129,161},{137,169... | collective-permute-start | bytes 393224 | tf_op jit(solution)/shard_map/ppermute | solution.py:213
  15.0 4.3 %collective-permute-start.5 = (f32[8,4096]{1,0:T(8,128)S(1)}, f32[8,4096]{1,0:T(8,128)S(1)}, u32[]{:S(2)}, u32[]{:S(2)}) collective-permute-start(f32[8,4096]{1,0:T(8,128)S(1)} %bitcast_select_fusion), channel_id=1, source_target_pairs={{0,80},{8,88},{128,208},{136,216},{1,81},{9,89},{129,209},{137,217... | collective-permute-start | bytes 393224 | tf_op jit(solution)/shard_map/ppermute | solution.py:213
  16.3 5.2 %collective-permute-start.6 = (f32[8,4096]{1,0:T(8,128)S(1)}, f32[8,4096]{1,0:T(8,128)S(1)}, u32[]{:S(2)}, u32[]{:S(2)}) collective-permute-start(f32[8,4096]{1,0:T(8,128)S(1)} %bitcast_select_fusion), channel_id=1, source_target_pairs={{0,48},{8,56},{128,176},{136,184},{1,49},{9,57},{129,177},{137,185... | collective-permute-start | bytes 393224 | tf_op jit(solution)/shard_map/ppermute | solution.py:213
  17.6 5.5 %collective-permute-start.7 = (f32[8,4096]{1,0:T(8,128)S(1)}, f32[8,4096]{1,0:T(8,128)S(1)}, u32[]{:S(2)}, u32[]{:S(2)}) collective-permute-start(f32[8,4096]{1,0:T(8,128)S(1)} %bitcast_select_fusion), channel_id=1, source_target_pairs={{0,64},{8,72},{128,192},{136,200},{1,65},{9,73},{129,193},{137,201... | collective-permute-start | bytes 393224 | tf_op jit(solution)/shard_map/ppermute | solution.py:213
  23.1 6.6 %collective-permute-start.8 = (f32[8,4096]{1,0:T(8,128)S(1)}, f32[8,4096]{1,0:T(8,128)S(1)}, u32[]{:S(2)}, u32[]{:S(2)}) collective-permute-start(f32[8,4096]{1,0:T(8,128)S(1)} %select_select_fusion.refs_0_.refs_8_), channel_id=1, source_target_pairs={{0,128},{8,136},{16,144},{24,152},{32,160},{40,168},{48,176},{56,1... | collective-permute-start | bytes 393224 | tf_op jit(solution)/shard_map/ppermute | solution.py:214
  23.6 6.2 %collective-permute-start.9 = (f32[8,4096]{1,0:T(8,128)S(1)}, f32[8,4096]{1,0:T(8,128)S(1)}, u32[]{:S(2)}, u32[]{:S(2)}) collective-permute-start(f32[8,4096]{1,0:T(8,128)S(1)} %select_select_fusion.refs_0_.refs_8_), channel_id=1, source_target_pairs={{0,8},{8,0},{16,24},{24,16},{32,40},{40,32},{48,56},{56,48},{64,72... | collective-permute-start | bytes 393224 | tf_op jit(solution)/shard_map/ppermute | solution.py:216
  29.7 1.3 %collective-permute-start.10 = (f32[8,4096]{1,0:T(8,128)S(1)}, f32[8,4096]{1,0:T(8,128)S(1)}, u32[]{:S(2)}, u32[]{:S(2)}) collective-permute-start(f32[8,4096]{1,0:T(8,128)S(1)} %collective-permute-done.8.refs_1_.refs_9_), channel_id=1, source_target_pairs={{0,8},{8,0},{16,24},{24,16},{32,40},{40,32},{48,56},{56,48},{64,72... | collective-permute-start | bytes 393224 | tf_op jit(solution)/shard_map/ppermute | solution.py:216
  33.0 7.0 %collective-permute-start.11 = (f32[2,8,2,8,128]{4,3,2,1,0:T(8,128)S(1)}, f32[2,8,2,8,128]{4,3,2,1,0:T(8,128)S(1)}, u32[]{:S(2)}, u32[]{:S(2)}) collective-permute-start(f32[2,8,2,8,128]{4,3,2,1,0:T(8,128)S(1)} %get-tuple-element.22), channel_id=1, source_target_pairs={{0,1},{1,0},{2,3},{3,2},{4,5},{5,4},{6,7},{7,6},{8,9},{9,8},{10,11... | collective-permute-start | bytes 393224 | tf_op jit(solution)/shard_map/ppermute | solution.py:223
  34.6 10.1 %collective-permute-start.12 = (f32[2,8,2,8,128]{4,3,2,1,0:T(8,128)S(1)}, f32[2,8,2,8,128]{4,3,2,1,0:T(8,128)S(1)}, u32[]{:S(2)}, u32[]{:S(2)}) collective-permute-start(f32[2,8,2,8,128]{4,3,2,1,0:T(8,128)S(1)} %get-tuple-element.23), channel_id=1, source_target_pairs={{0,2},{1,3},{2,0},{3,1},{4,6},{5,7},{6,4},{7,5},{8,10},{9,11},{10,... | collective-permute-start | bytes 393224 | tf_op jit(solution)/shard_map/ppermute | solution.py:223
  37.8 9.3 %collective-permute-start.13 = (f32[2,8,2,8,128]{4,3,2,1,0:T(8,128)S(1)}, f32[2,8,2,8,128]{4,3,2,1,0:T(8,128)S(1)}, u32[]{:S(2)}, u32[]{:S(2)}) collective-permute-start(f32[2,8,2,8,128]{4,3,2,1,0:T(8,128)S(1)} %get-tuple-element.24), channel_id=1, source_target_pairs={{0,3},{1,2},{2,1},{3,0},{4,7},{5,6},{6,5},{7,4},{8,11},{9,10},{10,... | collective-permute-start | bytes 393224 | tf_op jit(solution)/shard_map/ppermute | solution.py:223
  38.1 9.0 %collective-permute-start.14 = (f32[2,8,2,8,128]{4,3,2,1,0:T(8,128)S(1)}, f32[2,8,2,8,128]{4,3,2,1,0:T(8,128)S(1)}, u32[]{:S(2)}, u32[]{:S(2)}) collective-permute-start(f32[2,8,2,8,128]{4,3,2,1,0:T(8,128)S(1)} %get-tuple-element.25), channel_id=1, source_target_pairs={{0,4},{1,5},{2,6},{3,7},{4,0},{5,1},{6,2},{7,3},{8,12},{9,13},{10,... | collective-permute-start | bytes 393224 | tf_op jit(solution)/shard_map/ppermute | solution.py:223
  39.3 7.8 %collective-permute-start.15 = (f32[2,8,2,8,128]{4,3,2,1,0:T(8,128)S(1)}, f32[2,8,2,8,128]{4,3,2,1,0:T(8,128)S(1)}, u32[]{:S(2)}, u32[]{:S(2)}) collective-permute-start(f32[2,8,2,8,128]{4,3,2,1,0:T(8,128)S(1)} %get-tuple-element.26), channel_id=1, source_target_pairs={{0,5},{1,4},{2,7},{3,6},{4,1},{5,0},{6,3},{7,2},{8,13},{9,12},{10,... | collective-permute-start | bytes 393224 | tf_op jit(solution)/shard_map/ppermute | solution.py:223
  39.9 11.7 %collective-permute-start.16 = (f32[2,8,2,8,128]{4,3,2,1,0:T(8,128)S(1)}, f32[2,8,2,8,128]{4,3,2,1,0:T(8,128)S(1)}, u32[]{:S(2)}, u32[]{:S(2)}) collective-permute-start(f32[2,8,2,8,128]{4,3,2,1,0:T(8,128)S(1)} %get-tuple-element.27), channel_id=1, source_target_pairs={{0,6},{1,7},{2,4},{3,5},{4,2},{5,3},{6,0},{7,1},{8,14},{9,15},{10,... | collective-permute-start | bytes 393224 | tf_op jit(solution)/shard_map/ppermute | solution.py:223
  44.7 9.0 %collective-permute-start.17 = (f32[2,8,2,8,128]{4,3,2,1,0:T(8,128)S(1)}, f32[2,8,2,8,128]{4,3,2,1,0:T(8,128)S(1)}, u32[]{:S(2)}, u32[]{:S(2)}) collective-permute-start(f32[2,8,2,8,128]{4,3,2,1,0:T(8,128)S(1)} %get-tuple-element.28), channel_id=1, source_target_pairs={{0,7},{1,6},{2,5},{3,4},{4,3},{5,2},{6,1},{7,0},{8,15},{9,14},{10,... | collective-permute-start | bytes 393224 | tf_op jit(solution)/shard_map/ppermute | solution.py:223
  54.8 6.4 %collective-permute-start.18 = (f32[2,8,2,8,128]{4,3,2,1,0:T(8,128)S(1)}, f32[2,8,2,8,128]{4,3,2,1,0:T(8,128)S(1)}, u32[]{:S(2)}, u32[]{:S(2)}) collective-permute-start(f32[2,8,2,8,128]{4,3,2,1,0:T(8,128)S(1)} %bitcast.35), channel_id=1, source_target_pairs={{0,1},{1,0},{2,3},{3,2},{4,5},{5,4},{6,7},{7,6},{8,9},{9,8},{10,11... | collective-permute-start | bytes 393224 | tf_op jit(solution)/shard_map/ppermute | solution.py:223
  55.0 8.9 %collective-permute-start.19 = (f32[2,8,2,8,128]{4,3,2,1,0:T(8,128)S(1)}, f32[2,8,2,8,128]{4,3,2,1,0:T(8,128)S(1)}, u32[]{:S(2)}, u32[]{:S(2)}) collective-permute-start(f32[2,8,2,8,128]{4,3,2,1,0:T(8,128)S(1)} %bitcast.34), channel_id=1, source_target_pairs={{0,2},{1,3},{2,0},{3,1},{4,6},{5,7},{6,4},{7,5},{8,10},{9,11},{10,... | collective-permute-start | bytes 393224 | tf_op jit(solution)/shard_map/ppermute | solution.py:223
  57.0 10.1 %collective-permute-start.20 = (f32[2,8,2,8,128]{4,3,2,1,0:T(8,128)S(1)}, f32[2,8,2,8,128]{4,3,2,1,0:T(8,128)S(1)}, u32[]{:S(2)}, u32[]{:S(2)}) collective-permute-start(f32[2,8,2,8,128]{4,3,2,1,0:T(8,128)S(1)} %bitcast.33), channel_id=1, source_target_pairs={{0,3},{1,2},{2,1},{3,0},{4,7},{5,6},{6,5},{7,4},{8,11},{9,10},{10,... | collective-permute-start | bytes 393224 | tf_op jit(solution)/shard_map/ppermute | solution.py:223
  60.0 7.1 %collective-permute-start.21 = (f32[2,8,2,8,128]{4,3,2,1,0:T(8,128)S(1)}, f32[2,8,2,8,128]{4,3,2,1,0:T(8,128)S(1)}, u32[]{:S(2)}, u32[]{:S(2)}) collective-permute-start(f32[2,8,2,8,128]{4,3,2,1,0:T(8,128)S(1)} %bitcast.32), channel_id=1, source_target_pairs={{0,4},{1,5},{2,6},{3,7},{4,0},{5,1},{6,2},{7,3},{8,12},{9,13},{10,... | collective-permute-start | bytes 393224 | tf_op jit(solution)/shard_map/ppermute | solution.py:223
  61.2 7.3 %collective-permute-start.22 = (f32[2,8,2,8,128]{4,3,2,1,0:T(8,128)S(1)}, f32[2,8,2,8,128]{4,3,2,1,0:T(8,128)S(1)}, u32[]{:S(2)}, u32[]{:S(2)}) collective-permute-start(f32[2,8,2,8,128]{4,3,2,1,0:T(8,128)S(1)} %bitcast.31), channel_id=1, source_target_pairs={{0,5},{1,4},{2,7},{3,6},{4,1},{5,0},{6,3},{7,2},{8,13},{9,12},{10,... | collective-permute-start | bytes 393224 | tf_op jit(solution)/shard_map/ppermute | solution.py:223
  61.2 9.7 %collective-permute-start.23 = (f32[2,8,2,8,128]{4,3,2,1,0:T(8,128)S(1)}, f32[2,8,2,8,128]{4,3,2,1,0:T(8,128)S(1)}, u32[]{:S(2)}, u32[]{:S(2)}) collective-permute-start(f32[2,8,2,8,128]{4,3,2,1,0:T(8,128)S(1)} %bitcast.30), channel_id=1, source_target_pairs={{0,6},{1,7},{2,4},{3,5},{4,2},{5,3},{6,0},{7,1},{8,14},{9,15},{10,... | collective-permute-start | bytes 393224 | tf_op jit(solution)/shard_map/ppermute | solution.py:223
  63.9 8.1 %collective-permute-start.24 = (f32[2,8,2,8,128]{4,3,2,1,0:T(8,128)S(1)}, f32[2,8,2,8,128]{4,3,2,1,0:T(8,128)S(1)}, u32[]{:S(2)}, u32[]{:S(2)}) collective-permute-start(f32[2,8,2,8,128]{4,3,2,1,0:T(8,128)S(1)} %bitcast.29), channel_id=1, source_target_pairs={{0,7},{1,6},{2,5},{3,4},{4,3},{5,2},{6,1},{7,0},{8,15},{9,14},{10,... | collective-permute-start | bytes 393224 | tf_op jit(solution)/shard_map/ppermute | solution.py:223
where the time goes:
time: 74 us; the launch traced here: 73.8 us
  starting transfers between devices  34.7 us (47%)
  waiting for transfers between devices  31 us (42%)
  Pallas kernels  4.75 us (6%)
  other arithmetic  2.04 us (3%)
  local copies, waits for them, and re-layouts  0.92 us (1%)
    ppermute x14, starting transfers between devices, exchange(): results[d] = lax.ppermute(blocks[d], 'fft', [(p, p ^ d) for p in range(8)])  23.9 us
    ppermute x14, waiting for transfers between devices, exchange(): results[d] = lax.ppermute(blocks[d], 'fft', [(p, p ^ d) for p in range(8)])  13.3 us
    ppermute x7, starting transfers between devices, fetch_sources(): first = jnp.where(z == step, lax.ppermute(root, 'band', pairs), first)  9.08 us
    ppermute x1, waiting for transfers between devices, fetch_sources(): lax.ppermute(orbitals[1], 'band', [(band_of(0, 0, c), band_of(1, 0, c)) f...  6.8 us
    ppermute x1, waiting for transfers between devices, fetch_sources(): second = lax.ppermute(first, 'band', [(b, b ^ 16) for b in range(32)])  5.97 us
    ppermute x7, waiting for transfers between devices, fetch_sources(): first = jnp.where(z == step, lax.ppermute(root, 'band', pairs), first)  3.77 us
    pallas_call x1, Pallas kernels, apply_exchange(): local_call(forward_kernel, [block] * 8, [pltpu.VMEM((2, rows, 2 * LANES),...  1.91 us
    pallas_call x1, Pallas kernels, apply_exchange(): local_call(inverse_kernel, [(2, PLANES, GRID * GRID)], [work])  1.76 us
  transfers between devices with their start and end apart: 25, of which 11 were waited for; matrix products, arithmetic and copies ran while one was open for 3% of the time, Pallas kernels for 0%

commit v1 on v0

--- a/solution.py
+++ b/solution.py
@@ -15,7 +15,7 @@
 LANES = 128
 
 
-ORDER = (6, 7, 5, 4, 2, 3, 1)
+ORDER = (2, 6, 4, 7, 5, 3, 1)
 REACH = (4, 3, 5, 2, 6, 1, 7)
 
 
@@ -36,8 +36,7 @@
     return split_table(jnp.concatenate([top, bottom], 0), 1)
 
 
-def right_table(direction):
-    index = jnp.arange(GRID, dtype=jnp.int32)
+def right_table(index, direction):
     cosine, sine = wave(index, index, direction)
     zero = jnp.zeros_like(cosine)
     table = jnp.concatenate(
@@ -52,11 +51,10 @@
     return split_table(table, 0)
 
 
-def filter_table(y_offset):
-    indices = jnp.arange(GRID, dtype=jnp.int32)
-    signed = jnp.where(indices < GRID // 2, indices, indices - GRID).astype(jnp.float32)
+def filter_table(index, here):
+    signed = jnp.where(index < GRID // 2, index, index - GRID).astype(jnp.float32)
     wavenum = signed * (2.0 * math.pi / GRID)
-    y_indices = y_offset + jnp.arange(PLANES, dtype=jnp.int32)
+    y_indices = here * PLANES + index[:PLANES]
     y_signed = jnp.where(y_indices < GRID // 2, y_indices, y_indices - GRID).astype(jnp.float32)
     y_wavenum = y_signed * (2.0 * math.pi / GRID)
     wide = jnp.concatenate([wavenum, wavenum])
@@ -199,7 +197,7 @@
     return x_half * 16 + z * 2 + core
 
 
-def fetch_sources(orbitals):
+def fetch_sources(orbitals, here):
     cores = (0, 1)
     band = lax.axis_index("band")
     x_half, z = band // 16, band // 2 % 8
@@ -211,10 +209,11 @@
     for step in REACH:
         pairs = [(band_of(h, 0, c), band_of(h, step, c)) for h in cores for c in cores]
         first = jnp.where(z == step, lax.ppermute(root, "band", pairs), first)
+    index, mixed, first = indices_after(first, here)
     second = lax.ppermute(first, "band", [(b, b ^ 16) for b in range(32)])
     own = (first, second)
     other = tuple(lax.ppermute(a, "band", [(b, b ^ 1) for b in range(32)]) for a in own)
-    return own, other
+    return own, other, index, mixed
 
 
 def exchange(blocks):
@@ -224,13 +223,15 @@
     return results
 
 
+def indices_after(value, here):
+    index, value = lax.optimization_barrier((jnp.arange(GRID, dtype=jnp.int32), value))
+    mixed = (index // PLANES ^ here) * PLANES + index % PLANES
+    return index, mixed, value
+
+
 def apply_exchange(orbitals):
-    own, other = fetch_sources(orbitals)
     here = lax.axis_index("fft")
-    filters = filter_table(here * PLANES)
-    index = jnp.arange(GRID, dtype=jnp.int32)
-    mixed = (index // PLANES ^ here) * PLANES + index % PLANES
-    right_forth, right_back = right_table(-1.0), right_table(1.0)
+    own, other, index, mixed = fetch_sources(orbitals, here)
     rows = PLANES * GRID
     work = pltpu.VMEM((2, rows, LANES), jnp.float32)
     block = (2, PLANES, 2, PLANES, LANES)
@@ -239,14 +240,20 @@
         forward_kernel,
         [block] * 8,
         [pltpu.VMEM((2, rows, 2 * LANES), jnp.float32), work],
-    )(orbitals, *own, *other, right_forth, left_table(mixed, index, -1.0))
-    spectrum = [a.reshape(flat) for a in exchange(spectrum)]
+    )(orbitals, *own, *other, right_table(index, -1.0), left_table(mixed, index, -1.0))
+    spectrum = exchange(spectrum)
+    index, mixed, spectrum[ORDER[0]] = indices_after(spectrum[ORDER[0]], here)
+    spectrum = [a.reshape(flat) for a in spectrum]
     filtered = local_call(middle_kernel, [flat] * 8, [])(
-        *spectrum, left_table(index, mixed, -1.0), left_table(mixed, index, 1.0), filters
+        *spectrum,
+        left_table(index, mixed, -1.0),
+        left_table(mixed, index, 1.0),
+        filter_table(index, here),
     )
     returned = exchange([a.reshape(block) for a in filtered])
+    index, mixed, returned[ORDER[0]] = indices_after(returned[ORDER[0]], here)
     return local_call(inverse_kernel, [(2, PLANES, GRID * GRID)], [work])(
-        *returned, *own, *other, right_back, left_table(index, mixed, 1.0)
+        *returned, *own, *other, right_table(index, 1.0), left_table(index, mixed, 1.0)
     )[0]
 
 

time: 74 us -> 73.9 us (level)
  the two profiles are of different devices: /device:TPU:4 before, /device:TPU:6 now
where the time goes in v1:
time: 73.9 us; the launch traced here: 73.7 us
  waiting for transfers between devices  33.8 us (46%)
  starting transfers between devices  31.3 us (42%)
  Pallas kernels  4.76 us (6%)
  other arithmetic  2.47 us (3%)
  local copies, waits for them, and re-layouts  1 us (1%)
    ppermute x14, starting transfers between devices, exchange(): results[d] = lax.ppermute(blocks[d], 'fft', [(p, p ^ d) for p in range(8)])  20.6 us
    ppermute x14, waiting for transfers between devices, exchange(): results[d] = lax.ppermute(blocks[d], 'fft', [(p, p ^ d) for p in range(8)])  15.4 us
    ppermute x7, starting transfers between devices, fetch_sources(): first = jnp.where(z == step, lax.ppermute(root, 'band', pairs), first)  9.08 us
    ppermute x1, waiting for transfers between devices, fetch_sources(): lax.ppermute(orbitals[1], 'band', [(band_of(0, 0, c), band_of(1, 0, c)) f...  7.32 us
    ppermute x1, waiting for transfers between devices, fetch_sources(): second = lax.ppermute(first, 'band', [(b, b ^ 16) for b in range(32)])  5.45 us
    ppermute x7, waiting for transfers between devices, fetch_sources(): first = jnp.where(z == step, lax.ppermute(root, 'band', pairs), first)  4.29 us
    pallas_call x1, Pallas kernels, apply_exchange(): local_call(forward_kernel, [block] * 8, [pltpu.VMEM((2, rows, 2 * LANES),...  1.92 us
    pallas_call x1, Pallas kernels, apply_exchange(): local_call(inverse_kernel, [(2, PLANES, GRID * GRID)], [work])  1.77 us
  transfers between devices with their start and end apart: 25, of which 13 were waited for; matrix products, arithmetic and copies ran while one was open for 3% of the time, Pallas kernels for 0%

profile of v1, /device:TPU:6, one launch (start us, length us, event | category | flops | bytes accessed | tf_op | source)
XLA Modules:
  0.0 73.7 jit_solution(6411775670150026473)
XLA Ops:
  0.0 1.0 %slice_bitcast_fusion = f32[8,4096]{1,0:T(8,128)S(1)} fusion(f32[2,8,4096]{2,1,0:T(8,128)} %orb_ref.1), kind=kLoop, calls=%fused_computation.49 | loop fusion | bytes 262144 | tf_op jit(solution)/shard_map/squeeze | solution.py:205
  1.0 1.3 %collective-permute-start = (f32[8,4096]{1,0:T(8,128)S(1)}, f32[8,4096]{1,0:T(8,128)S(1)}, u32[]{:S(2)}, u32[]{:S(2)}) collective-permute-start(f32[8,4096]{1,0:T(8,128)S(1)} %slice_bitcast_fusion), channel_id=1, source_target_pairs={{0,128},{8,136},{1,129},{9,137},{2,130},{10,138},{3,131},{11,139},... | collective-permute-start | bytes 393224 | tf_op jit(solution)/shard_map/ppermute | solution.py:204
  2.3 7.3 %collective-permute-done = f32[8,4096]{1,0:T(8,128)S(1)} collective-permute-done((f32[8,4096]{1,0:T(8,128)S(1)}, f32[8,4096]{1,0:T(8,128)S(1)}, u32[]{:S(2)}, u32[]{:S(2)}) %collective-permute-start) | collective-permute-done | bytes 131104 | tf_op jit(solution)/shard_map/ppermute | solution.py:204
  9.6 1.3 %collective-permute-start.1 = (f32[8,4096]{1,0:T(8,128)S(1)}, f32[8,4096]{1,0:T(8,128)S(1)}, u32[]{:S(2)}, u32[]{:S(2)}) collective-permute-start(f32[8,4096]{1,0:T(8,128)S(1)} %bitcast_select_fusion), channel_id=1, source_target_pairs={{0,112},{8,120},{128,240},{136,248},{1,113},{9,121},{129,241},{137... | collective-permute-start | bytes 393224 | tf_op jit(solution)/shard_map/ppermute | solution.py:211
  11.0 1.3 %collective-permute-start.2 = (f32[8,4096]{1,0:T(8,128)S(1)}, f32[8,4096]{1,0:T(8,128)S(1)}, u32[]{:S(2)}, u32[]{:S(2)}) collective-permute-start(f32[8,4096]{1,0:T(8,128)S(1)} %bitcast_select_fusion), channel_id=1, source_target_pairs={{0,16},{8,24},{128,144},{136,152},{1,17},{9,25},{129,145},{137,153... | collective-permute-start | bytes 393224 | tf_op jit(solution)/shard_map/ppermute | solution.py:211
  12.3 1.3 %collective-permute-start.3 = (f32[8,4096]{1,0:T(8,128)S(1)}, f32[8,4096]{1,0:T(8,128)S(1)}, u32[]{:S(2)}, u32[]{:S(2)}) collective-permute-start(f32[8,4096]{1,0:T(8,128)S(1)} %bitcast_select_fusion), channel_id=1, source_target_pairs={{0,96},{8,104},{128,224},{136,232},{1,97},{9,105},{129,225},{137,2... | collective-permute-start | bytes 393224 | tf_op jit(solution)/shard_map/ppermute | solution.py:211
  13.6 1.3 %collective-permute-start.4 = (f32[8,4096]{1,0:T(8,128)S(1)}, f32[8,4096]{1,0:T(8,128)S(1)}, u32[]{:S(2)}, u32[]{:S(2)}) collective-permute-start(f32[8,4096]{1,0:T(8,128)S(1)} %bitcast_select_fusion), channel_id=1, source_target_pairs={{0,32},{8,40},{128,160},{136,168},{1,33},{9,41},{129,161},{137,169... | collective-permute-start | bytes 393224 | tf_op jit(solution)/shard_map/ppermute | solution.py:211
  14.9 1.3 %collective-permute-start.5 = (f32[8,4096]{1,0:T(8,128)S(1)}, f32[8,4096]{1,0:T(8,128)S(1)}, u32[]{:S(2)}, u32[]{:S(2)}) collective-permute-start(f32[8,4096]{1,0:T(8,128)S(1)} %bitcast_select_fusion), channel_id=1, source_target_pairs={{0,80},{8,88},{128,208},{136,216},{1,81},{9,89},{129,209},{137,217... | collective-permute-start | bytes 393224 | tf_op jit(solution)/shard_map/ppermute | solution.py:211
  16.2 0.0 collective-permute-done.1
  16.2 1.3 %collective-permute-start.6 = (f32[8,4096]{1,0:T(8,128)S(1)}, f32[8,4096]{1,0:T(8,128)S(1)}, u32[]{:S(2)}, u32[]{:S(2)}) collective-permute-start(f32[8,4096]{1,0:T(8,128)S(1)} %bitcast_select_fusion), channel_id=1, source_target_pairs={{0,48},{8,56},{128,176},{136,184},{1,49},{9,57},{129,177},{137,185... | collective-permute-start | bytes 393224 | tf_op jit(solution)/shard_map/ppermute | solution.py:211
  17.5 0.0 collective-permute-done.2
  17.5 1.3 %collective-permute-start.7 = (f32[8,4096]{1,0:T(8,128)S(1)}, f32[8,4096]{1,0:T(8,128)S(1)}, u32[]{:S(2)}, u32[]{:S(2)}) collective-permute-start(f32[8,4096]{1,0:T(8,128)S(1)} %bitcast_select_fusion), channel_id=1, source_target_pairs={{0,64},{8,72},{128,192},{136,200},{1,65},{9,73},{129,193},{137,201... | collective-permute-start | bytes 393224 | tf_op jit(solution)/shard_map/ppermute | solution.py:211
  18.8 0.0 collective-permute-done.3
  18.9 0.0 collective-permute-done.4
  18.9 0.2 collective-permute-done.5
  19.0 2.3 %collective-permute-done.6 = f32[8,4096]{1,0:T(8,128)S(1)} collective-permute-done((f32[8,4096]{1,0:T(8,128)S(1)}, f32[8,4096]{1,0:T(8,128)S(1)}, u32[]{:S(2)}, u32[]{:S(2)}) %collective-permute-start.6) | collective-permute-done | bytes 131104 | tf_op jit(solution)/shard_map/ppermute | solution.py:211
  21.4 1.8 %collective-permute-done.7 = f32[8,4096]{1,0:T(8,128)S(1)} collective-permute-done((f32[8,4096]{1,0:T(8,128)S(1)}, f32[8,4096]{1,0:T(8,128)S(1)}, u32[]{:S(2)}, u32[]{:S(2)}) %collective-permute-start.7) | collective-permute-done | bytes 131104 | tf_op jit(solution)/shard_map/ppermute | solution.py:211
  23.2 0.3 collective-permute-start.8
  23.5 0.0 collective-permute-start.9
  23.5 0.3 fusion.58
  23.9 0.1 reduce-precision_convert_fusion.1
  24.0 0.1 reduce-precision_convert_fusion.5
  24.1 0.2 fusion.7
  24.3 5.5 %collective-permute-done.8.refs_1_.refs_9_ = f32[8,4096]{1,0:T(8,128)S(1)} collective-permute-done((f32[8,4096]{1,0:T(8,128)S(1)}, f32[8,4096]{1,0:T(8,128)S(1)}, u32[]{:S(2)}, u32[]{:S(2)}) %collective-permute-start.8) | collective-permute-done | bytes 131104 | tf_op jit(solution)/shard_map/ppermute | solution.py:213
  29.8 0.0 collective-permute-start.10
  29.8 0.0 collective-permute-done.9.refs_2_.refs_10_
  29.8 1.3 %collective-permute-done.10.refs_3_.refs_11_ = f32[8,4096]{1,0:T(8,128)S(1)} collective-permute-done((f32[8,4096]{1,0:T(8,128)S(1)}, f32[8,4096]{1,0:T(8,128)S(1)}, u32[]{:S(2)}, u32[]{:S(2)}) %collective-permute-start.10) | collective-permute-done | bytes 131104 | tf_op jit(solution)/shard_map/ppermute | solution.py:215
  31.1 1.9 %shard_map.17 = (f32[2,8,2,8,128]{4,3,2,1,0:T(8,128)S(1)}, f32[2,8,2,8,128]{4,3,2,1,0:T(8,128)S(1)}, f32[2,8,2,8,128]{4,3,2,1,0:T(8,128)S(1)}, f32[2,8,2,8,128]{...) custom-call(f32[2,8,4096]{2,1,0:T(8,128)S(1)} %copy-done, ...), custom_call_target="tpu_custom_call" | custom-call | tf_op jit(solution)/shard_map/pallas_call | solution.py:239
  33.0 3.3 %collective-permute-start.12 = (f32[2,8,2,8,128]{4,3,2,1,0:T(8,128)S(1)}, f32[2,8,2,8,128]{4,3,2,1,0:T(8,128)S(1)}, u32[]{:S(2)}, u32[]{:S(2)}) collective-permute-start(f32[2,8,2,8,128]{4,3,2,1,0:T(8,128)S(1)} %get-tuple-element.31), channel_id=1, source_target_pairs={{0,2},{1,3},{2,0},{3,1},{4,6},{5,7},{6,4},{7,5},{8,10},{9,11},{10,... | collective-permute-start | bytes 393224 | tf_op jit(solution)/shard_map/ppermute | solution.py:222
  36.3 0.7 collective-permute-start.11
  37.0 0.4 collective-permute-start.13
  37.4 0.8 %collective-permute-start.14 = (f32[2,8,2,8,128]{4,3,2,1,0:T(8,128)S(1)}, f32[2,8,2,8,128]{4,3,2,1,0:T(8,128)S(1)}, u32[]{:S(2)}, u32[]{:S(2)}) collective-permute-start(f32[2,8,2,8,128]{4,3,2,1,0:T(8,128)S(1)} %get-tuple-element.34), channel_id=1, source_target_pairs={{0,4},{1,5},{2,6},{3,7},{4,0},{5,1},{6,2},{7,3},{8,12},{9,13},{10,... | collective-permute-start | bytes 393224 | tf_op jit(solution)/shard_map/ppermute | solution.py:222
  38.2 2.1 %collective-permute-start.15 = (f32[2,8,2,8,128]{4,3,2,1,0:T(8,128)S(1)}, f32[2,8,2,8,128]{4,3,2,1,0:T(8,128)S(1)}, u32[]{:S(2)}, u32[]{:S(2)}) collective-permute-start(f32[2,8,2,8,128]{4,3,2,1,0:T(8,128)S(1)} %get-tuple-element.35), channel_id=1, source_target_pairs={{0,5},{1,4},{2,7},{3,6},{4,1},{5,0},{6,3},{7,2},{8,13},{9,12},{10,... | collective-permute-start | bytes 393224 | tf_op jit(solution)/shard_map/ppermute | solution.py:222
  40.3 0.7 collective-permute-done.12
  41.0 3.6 %collective-permute-start.16 = (f32[2,8,2,8,128]{4,3,2,1,0:T(8,128)S(1)}, f32[2,8,2,8,128]{4,3,2,1,0:T(8,128)S(1)}, u32[]{:S(2)}, u32[]{:S(2)}) collective-permute-start(f32[2,8,2,8,128]{4,3,2,1,0:T(8,128)S(1)} %get-tuple-element.36), channel_id=1, source_target_pairs={{0,6},{1,7},{2,4},{3,5},{4,2},{5,3},{6,0},{7,1},{8,14},{9,15},{10,... | collective-permute-start | bytes 393224 | tf_op jit(solution)/shard_map/ppermute | solution.py:222
  44.7 0.1 maximum_multiply_fusion
  44.8 0.1 broadcast_add_fusion
  44.8 0.2 fusion.3.refs_10_
  45.0 0.3 fusion.56
  45.4 0.1 reduce-precision_convert_fusion.3
  45.5 2.3 %collective-permute-done.11 = f32[2,8,2,8,128]{4,3,2,1,0:T(8,128)S(1)} collective-permute-done((f32[2,8,2,8,128]{4,3,2,1,0:T(8,128)S(1)}, f32[2,8,2,8,128]{4,3,2,1,0:T(8,128)S(1)}, u32[]{:S(2)}, u32[]{:S(2)}) %collective-permute-start.11) | collective-permute-done | bytes 131104 | tf_op jit(solution)/shard_map/ppermute | solution.py:222
  47.8 0.0 collective-permute-start.17
  47.8 0.0 collective-permute-done.13
  47.8 0.0 collective-permute-done.14
  47.8 3.6 %collective-permute-done.16 = f32[2,8,2,8,128]{4,3,2,1,0:T(8,128)S(1)} collective-permute-done((f32[2,8,2,8,128]{4,3,2,1,0:T(8,128)S(1)}, f32[2,8,2,8,128]{4,3,2,1,0:T(8,128)S(1)}, u32[]{:S(2)}, u32[]{:S(2)}) %collective-permute-start.16) | collective-permute-done | bytes 131104 | tf_op jit(solution)/shard_map/ppermute | solution.py:222
  51.5 3.4 %collective-permute-done.17 = f32[2,8,2,8,128]{4,3,2,1,0:T(8,128)S(1)} collective-permute-done((f32[2,8,2,8,128]{4,3,2,1,0:T(8,128)S(1)}, f32[2,8,2,8,128]{4,3,2,1,0:T(8,128)S(1)}, u32[]{:S(2)}, u32[]{:S(2)}) %collective-permute-start.17) | collective-permute-done | bytes 131104 | tf_op jit(solution)/shard_map/ppermute | solution.py:222
  54.9 1.1 %shard_map.18 = (f32[256,128]{1,0:T(8,128)S(1)}, f32[256,128]{1,0:T(8,128)S(1)}, f32[256,128]{1,0:T(8,128)S(1)}, f32[256,128]{1,0:T(8,128)S(1)}, f32[256,128]{1,...) custom-call(f32[256,128]{1,0:T(8,128)S(1)} %bitcast.20, ...), custom_call_target="tpu_custom_call" | custom-call | tf_op jit(solution)/shard_map/pallas_call | solution.py:247
  55.9 0.1 collective-permute-start.19
  56.0 0.2 collective-permute-start.18
  56.2 3.9 %collective-permute-start.20 = (f32[2,8,2,8,128]{4,3,2,1,0:T(8,128)S(1)}, f32[2,8,2,8,128]{4,3,2,1,0:T(8,128)S(1)}, u32[]{:S(2)}, u32[]{:S(2)}) collective-permute-start(f32[2,8,2,8,128]{4,3,2,1,0:T(8,128)S(1)} %bitcast.33), channel_id=1, source_target_pairs={{0,3},{1,2},{2,1},{3,0},{4,7},{5,6},{6,5},{7,4},{8,11},{9,10},{10,... | collective-permute-start | bytes 393224 | tf_op jit(solution)/shard_map/ppermute | solution.py:222
  60.1 0.8 %collective-permute-start.21 = (f32[2,8,2,8,128]{4,3,2,1,0:T(8,128)S(1)}, f32[2,8,2,8,128]{4,3,2,1,0:T(8,128)S(1)}, u32[]{:S(2)}, u32[]{:S(2)}) collective-permute-start(f32[2,8,2,8,128]{4,3,2,1,0:T(8,128)S(1)} %bitcast.32), channel_id=1, source_target_pairs={{0,4},{1,5},{2,6},{3,7},{4,0},{5,1},{6,2},{7,3},{8,12},{9,13},{10,... | collective-permute-start | bytes 393224 | tf_op jit(solution)/shard_map/ppermute | solution.py:222
  60.9 0.5 collective-permute-start.22
  61.5 1.6 %collective-permute-done.19.refs_2_ = f32[2,8,2,8,128]{4,3,2,1,0:T(8,128)S(1)} collective-permute-done((f32[2,8,2,8,128]{4,3,2,1,0:T(8,128)S(1)}, f32[2,8,2,8,128]{4,3,2,1,0:T(8,128)S(1)}, u32[]{:S(2)}, u32[]{:S(2)}) %collective-permute-start.19) | collective-permute-done | bytes 131104 | tf_op jit(solution)/shard_map/ppermute | solution.py:222
  63.1 0.2 collective-permute-start.23
  63.3 0.3 fusion.57
  63.7 0.1 reduce-precision_convert_fusion
  63.8 0.1 reduce-precision_convert_fusion.2
  63.9 0.2 fusion.8
  64.1 4.0 %collective-permute-start.24 = (f32[2,8,2,8,128]{4,3,2,1,0:T(8,128)S(1)}, f32[2,8,2,8,128]{4,3,2,1,0:T(8,128)S(1)}, u32[]{:S(2)}, u32[]{:S(2)}) collective-permute-start(f32[2,8,2,8,128]{4,3,2,1,0:T(8,128)S(1)} %bitcast.29), channel_id=1, source_target_pairs={{0,7},{1,6},{2,5},{3,4},{4,3},{5,2},{6,1},{7,0},{8,15},{9,14},{10,... | collective-permute-start | bytes 393224 | tf_op jit(solution)/shard_map/ppermute | solution.py:222
  68.1 0.0 collective-permute-done.20.refs_3_
  68.1 0.0 collective-permute-done.22.refs_5_
  68.1 2.7 %collective-permute-done.23.refs_6_ = f32[2,8,2,8,128]{4,3,2,1,0:T(8,128)S(1)} collective-permute-done((f32[2,8,2,8,128]{4,3,2,1,0:T(8,128)S(1)}, f32[2,8,2,8,128]{4,3,2,1,0:T(8,128)S(1)}, u32[]{:S(2)}, u32[]{:S(2)}) %collective-permute-start.23) | collective-permute-done | bytes 131104 | tf_op jit(solution)/shard_map/ppermute | solution.py:222
  70.8 1.0 %collective-permute-done.24.refs_7_ = f32[2,8,2,8,128]{4,3,2,1,0:T(8,128)S(1)} collective-permute-done((f32[2,8,2,8,128]{4,3,2,1,0:T(8,128)S(1)}, f32[2,8,2,8,128]{4,3,2,1,0:T(8,128)S(1)}, u32[]{:S(2)}, u32[]{:S(2)}) %collective-permute-start.24) | collective-permute-done | bytes 131104 | tf_op jit(solution)/shard_map/ppermute | solution.py:222
  71.9 1.8 %shard_map.19 = f32[2,8,4096]{2,1,0:T(8,128)} custom-call(f32[2,8,2,8,128]{4,3,2,1,0:T(8,128)S(1)} %bitcast.22, f32[2,8,2,8,128]{4,3,2,1,0:T(8,128)S(1)} %collective-permute-done.18.refs_1_, f32[2,8,2,8,128]{4,3,2,1,0:T(8,128)S(1)} %collective-permute-done.19.refs_2_, f32[2,8,2,8,128]{4,3,2,1,0:T(8,128)S(1)} %collective-permute-done.20.refs_3_, ...), custom_call_target="tpu_custom_call" | custom-call | tf_op jit(solution)/shard_map/pallas_call | solution.py:255
  (22 shorter events, 0.3 us)
Async XLA Ops:
  0.0 9.6 %copy-start = (f32[2,8,4096]{2,1,0:T(8,128)S(1)}, f32[2,8,4096]{2,1,0:T(8,128)}, u32[]{:S(2)}) copy-start(f32[2,8,4096]{2,1,0:T(8,128)} %orb_ref.1) | copy-start | bytes 786436
  1.0 8.6 %collective-permute-start = (f32[8,4096]{1,0:T(8,128)S(1)}, f32[8,4096]{1,0:T(8,128)S(1)}, u32[]{:S(2)}, u32[]{:S(2)}) collective-permute-start(f32[8,4096]{1,0:T(8,128)S(1)} %slice_bitcast_fusion), channel_id=1, source_target_pairs={{0,128},{8,136},{1,129},{9,137},{2,130},{10,138},{3,131},{11,139},... | collective-permute-start | bytes 393224 | tf_op jit(solution)/shard_map/ppermute | solution.py:204
  9.6 6.5 %collective-permute-start.1 = (f32[8,4096]{1,0:T(8,128)S(1)}, f32[8,4096]{1,0:T(8,128)S(1)}, u32[]{:S(2)}, u32[]{:S(2)}) collective-permute-start(f32[8,4096]{1,0:T(8,128)S(1)} %bitcast_select_fusion), channel_id=1, source_target_pairs={{0,112},{8,120},{128,240},{136,248},{1,113},{9,121},{129,241},{137... | collective-permute-start | bytes 393224 | tf_op jit(solution)/shard_map/ppermute | solution.py:211
  11.0 6.5 %collective-permute-start.2 = (f32[8,4096]{1,0:T(8,128)S(1)}, f32[8,4096]{1,0:T(8,128)S(1)}, u32[]{:S(2)}, u32[]{:S(2)}) collective-permute-start(f32[8,4096]{1,0:T(8,128)S(1)} %bitcast_select_fusion), channel_id=1, source_target_pairs={{0,16},{8,24},{128,144},{136,152},{1,17},{9,25},{129,145},{137,153... | collective-permute-start | bytes 393224 | tf_op jit(solution)/shard_map/ppermute | solution.py:211
  12.3 6.6 %collective-permute-start.3 = (f32[8,4096]{1,0:T(8,128)S(1)}, f32[8,4096]{1,0:T(8,128)S(1)}, u32[]{:S(2)}, u32[]{:S(2)}) collective-permute-start(f32[8,4096]{1,0:T(8,128)S(1)} %bitcast_select_fusion), channel_id=1, source_target_pairs={{0,96},{8,104},{128,224},{136,232},{1,97},{9,105},{129,225},{137,2... | collective-permute-start | bytes 393224 | tf_op jit(solution)/shard_map/ppermute | solution.py:211
  13.6 5.3 %collective-permute-start.4 = (f32[8,4096]{1,0:T(8,128)S(1)}, f32[8,4096]{1,0:T(8,128)S(1)}, u32[]{:S(2)}, u32[]{:S(2)}) collective-permute-start(f32[8,4096]{1,0:T(8,128)S(1)} %bitcast_select_fusion), channel_id=1, source_target_pairs={{0,32},{8,40},{128,160},{136,168},{1,33},{9,41},{129,161},{137,169... | collective-permute-start | bytes 393224 | tf_op jit(solution)/shard_map/ppermute | solution.py:211
  14.9 4.2 %collective-permute-start.5 = (f32[8,4096]{1,0:T(8,128)S(1)}, f32[8,4096]{1,0:T(8,128)S(1)}, u32[]{:S(2)}, u32[]{:S(2)}) collective-permute-start(f32[8,4096]{1,0:T(8,128)S(1)} %bitcast_select_fusion), channel_id=1, source_target_pairs={{0,80},{8,88},{128,208},{136,216},{1,81},{9,89},{129,209},{137,217... | collective-permute-start | bytes 393224 | tf_op jit(solution)/shard_map/ppermute | solution.py:211
  16.2 5.2 %collective-permute-start.6 = (f32[8,4096]{1,0:T(8,128)S(1)}, f32[8,4096]{1,0:T(8,128)S(1)}, u32[]{:S(2)}, u32[]{:S(2)}) collective-permute-start(f32[8,4096]{1,0:T(8,128)S(1)} %bitcast_select_fusion), channel_id=1, source_target_pairs={{0,48},{8,56},{128,176},{136,184},{1,49},{9,57},{129,177},{137,185... | collective-permute-start | bytes 393224 | tf_op jit(solution)/shard_map/ppermute | solution.py:211
  17.5 5.6 %collective-permute-start.7 = (f32[8,4096]{1,0:T(8,128)S(1)}, f32[8,4096]{1,0:T(8,128)S(1)}, u32[]{:S(2)}, u32[]{:S(2)}) collective-permute-start(f32[8,4096]{1,0:T(8,128)S(1)} %bitcast_select_fusion), channel_id=1, source_target_pairs={{0,64},{8,72},{128,192},{136,200},{1,65},{9,73},{129,193},{137,201... | collective-permute-start | bytes 393224 | tf_op jit(solution)/shard_map/ppermute | solution.py:211
  23.2 6.6 %collective-permute-start.8 = (f32[8,4096]{1,0:T(8,128)S(1)}, f32[8,4096]{1,0:T(8,128)S(1)}, u32[]{:S(2)}, u32[]{:S(2)}) collective-permute-start(f32[8,4096]{1,0:T(8,128)S(1)} %select_select_fusion.refs_0_.refs_8_), channel_id=1, source_target_pairs={{0,128},{8,136},{16,144},{24,152},{32,160},{40,168},{48,176},{56,1... | collective-permute-start | bytes 393224 | tf_op jit(solution)/shard_map/ppermute | solution.py:213
  23.5 6.3 %collective-permute-start.9 = (f32[8,4096]{1,0:T(8,128)S(1)}, f32[8,4096]{1,0:T(8,128)S(1)}, u32[]{:S(2)}, u32[]{:S(2)}) collective-permute-start(f32[8,4096]{1,0:T(8,128)S(1)} %select_select_fusion.refs_0_.refs_8_), channel_id=1, source_target_pairs={{0,8},{8,0},{16,24},{24,16},{32,40},{40,32},{48,56},{56,48},{64,72... | collective-permute-start | bytes 393224 | tf_op jit(solution)/shard_map/ppermute | solution.py:215
  29.8 1.3 %collective-permute-start.10 = (f32[8,4096]{1,0:T(8,128)S(1)}, f32[8,4096]{1,0:T(8,128)S(1)}, u32[]{:S(2)}, u32[]{:S(2)}) collective-permute-start(f32[8,4096]{1,0:T(8,128)S(1)} %collective-permute-done.8.refs_1_.refs_9_), channel_id=1, source_target_pairs={{0,8},{8,0},{16,24},{24,16},{32,40},{40,32},{48,56},{56,48},{64,72... | collective-permute-start | bytes 393224 | tf_op jit(solution)/shard_map/ppermute | solution.py:215
  33.0 8.0 %collective-permute-start.12 = (f32[2,8,2,8,128]{4,3,2,1,0:T(8,128)S(1)}, f32[2,8,2,8,128]{4,3,2,1,0:T(8,128)S(1)}, u32[]{:S(2)}, u32[]{:S(2)}) collective-permute-start(f32[2,8,2,8,128]{4,3,2,1,0:T(8,128)S(1)} %get-tuple-element.31), channel_id=1, source_target_pairs={{0,2},{1,3},{2,0},{3,1},{4,6},{5,7},{6,4},{7,5},{8,10},{9,11},{10,... | collective-permute-start | bytes 393224 | tf_op jit(solution)/shard_map/ppermute | solution.py:222
  36.3 11.5 %collective-permute-start.11 = (f32[2,8,2,8,128]{4,3,2,1,0:T(8,128)S(1)}, f32[2,8,2,8,128]{4,3,2,1,0:T(8,128)S(1)}, u32[]{:S(2)}, u32[]{:S(2)}) collective-permute-start(f32[2,8,2,8,128]{4,3,2,1,0:T(8,128)S(1)} %get-tuple-element.30), channel_id=1, source_target_pairs={{0,1},{1,0},{2,3},{3,2},{4,5},{5,4},{6,7},{7,6},{8,9},{9,8},{10,11... | collective-permute-start | bytes 393224 | tf_op jit(solution)/shard_map/ppermute | solution.py:222
  37.0 10.8 %collective-permute-start.13 = (f32[2,8,2,8,128]{4,3,2,1,0:T(8,128)S(1)}, f32[2,8,2,8,128]{4,3,2,1,0:T(8,128)S(1)}, u32[]{:S(2)}, u32[]{:S(2)}) collective-permute-start(f32[2,8,2,8,128]{4,3,2,1,0:T(8,128)S(1)} %get-tuple-element.33), channel_id=1, source_target_pairs={{0,3},{1,2},{2,1},{3,0},{4,7},{5,6},{6,5},{7,4},{8,11},{9,10},{10,... | collective-permute-start | bytes 393224 | tf_op jit(solution)/shard_map/ppermute | solution.py:222
  37.4 10.4 %collective-permute-start.14 = (f32[2,8,2,8,128]{4,3,2,1,0:T(8,128)S(1)}, f32[2,8,2,8,128]{4,3,2,1,0:T(8,128)S(1)}, u32[]{:S(2)}, u32[]{:S(2)}) collective-permute-start(f32[2,8,2,8,128]{4,3,2,1,0:T(8,128)S(1)} %get-tuple-element.34), channel_id=1, source_target_pairs={{0,4},{1,5},{2,6},{3,7},{4,0},{5,1},{6,2},{7,3},{8,12},{9,13},{10,... | collective-permute-start | bytes 393224 | tf_op jit(solution)/shard_map/ppermute | solution.py:222
  38.2 9.6 %collective-permute-start.15 = (f32[2,8,2,8,128]{4,3,2,1,0:T(8,128)S(1)}, f32[2,8,2,8,128]{4,3,2,1,0:T(8,128)S(1)}, u32[]{:S(2)}, u32[]{:S(2)}) collective-permute-start(f32[2,8,2,8,128]{4,3,2,1,0:T(8,128)S(1)} %get-tuple-element.35), channel_id=1, source_target_pairs={{0,5},{1,4},{2,7},{3,6},{4,1},{5,0},{6,3},{7,2},{8,13},{9,12},{10,... | collective-permute-start | bytes 393224 | tf_op jit(solution)/shard_map/ppermute | solution.py:222
  41.0 10.5 %collective-permute-start.16 = (f32[2,8,2,8,128]{4,3,2,1,0:T(8,128)S(1)}, f32[2,8,2,8,128]{4,3,2,1,0:T(8,128)S(1)}, u32[]{:S(2)}, u32[]{:S(2)}) collective-permute-start(f32[2,8,2,8,128]{4,3,2,1,0:T(8,128)S(1)} %get-tuple-element.36), channel_id=1, source_target_pairs={{0,6},{1,7},{2,4},{3,5},{4,2},{5,3},{6,0},{7,1},{8,14},{9,15},{10,... | collective-permute-start | bytes 393224 | tf_op jit(solution)/shard_map/ppermute | solution.py:222
  47.8 7.1 %collective-permute-start.17 = (f32[2,8,2,8,128]{4,3,2,1,0:T(8,128)S(1)}, f32[2,8,2,8,128]{4,3,2,1,0:T(8,128)S(1)}, u32[]{:S(2)}, u32[]{:S(2)}) collective-permute-start(f32[2,8,2,8,128]{4,3,2,1,0:T(8,128)S(1)} %get-tuple-element.37), channel_id=1, source_target_pairs={{0,7},{1,6},{2,5},{3,4},{4,3},{5,2},{6,1},{7,0},{8,15},{9,14},{10,... | collective-permute-start | bytes 393224 | tf_op jit(solution)/shard_map/ppermute | solution.py:222
  55.9 7.2 %collective-permute-start.19 = (f32[2,8,2,8,128]{4,3,2,1,0:T(8,128)S(1)}, f32[2,8,2,8,128]{4,3,2,1,0:T(8,128)S(1)}, u32[]{:S(2)}, u32[]{:S(2)}) collective-permute-start(f32[2,8,2,8,128]{4,3,2,1,0:T(8,128)S(1)} %bitcast.35), channel_id=1, source_target_pairs={{0,2},{1,3},{2,0},{3,1},{4,6},{5,7},{6,4},{7,5},{8,10},{9,11},{10,... | collective-permute-start | bytes 393224 | tf_op jit(solution)/shard_map/ppermute | solution.py:222
  56.0 8.1 %collective-permute-start.18 = (f32[2,8,2,8,128]{4,3,2,1,0:T(8,128)S(1)}, f32[2,8,2,8,128]{4,3,2,1,0:T(8,128)S(1)}, u32[]{:S(2)}, u32[]{:S(2)}) collective-permute-start(f32[2,8,2,8,128]{4,3,2,1,0:T(8,128)S(1)} %bitcast.34), channel_id=1, source_target_pairs={{0,1},{1,0},{2,3},{3,2},{4,5},{5,4},{6,7},{7,6},{8,9},{9,8},{10,11... | collective-permute-start | bytes 393224 | tf_op jit(solution)/shard_map/ppermute | solution.py:222
  56.2 11.9 %collective-permute-start.20 = (f32[2,8,2,8,128]{4,3,2,1,0:T(8,128)S(1)}, f32[2,8,2,8,128]{4,3,2,1,0:T(8,128)S(1)}, u32[]{:S(2)}, u32[]{:S(2)}) collective-permute-start(f32[2,8,2,8,128]{4,3,2,1,0:T(8,128)S(1)} %bitcast.33), channel_id=1, source_target_pairs={{0,3},{1,2},{2,1},{3,0},{4,7},{5,6},{6,5},{7,4},{8,11},{9,10},{10,... | collective-permute-start | bytes 393224 | tf_op jit(solution)/shard_map/ppermute | solution.py:222
  60.1 8.0 %collective-permute-start.21 = (f32[2,8,2,8,128]{4,3,2,1,0:T(8,128)S(1)}, f32[2,8,2,8,128]{4,3,2,1,0:T(8,128)S(1)}, u32[]{:S(2)}, u32[]{:S(2)}) collective-permute-start(f32[2,8,2,8,128]{4,3,2,1,0:T(8,128)S(1)} %bitcast.32), channel_id=1, source_target_pairs={{0,4},{1,5},{2,6},{3,7},{4,0},{5,1},{6,2},{7,3},{8,12},{9,13},{10,... | collective-permute-start | bytes 393224 | tf_op jit(solution)/shard_map/ppermute | solution.py:222
  60.9 7.2 %collective-permute-start.22 = (f32[2,8,2,8,128]{4,3,2,1,0:T(8,128)S(1)}, f32[2,8,2,8,128]{4,3,2,1,0:T(8,128)S(1)}, u32[]{:S(2)}, u32[]{:S(2)}) collective-permute-start(f32[2,8,2,8,128]{4,3,2,1,0:T(8,128)S(1)} %bitcast.31), channel_id=1, source_target_pairs={{0,5},{1,4},{2,7},{3,6},{4,1},{5,0},{6,3},{7,2},{8,13},{9,12},{10,... | collective-permute-start | bytes 393224 | tf_op jit(solution)/shard_map/ppermute | solution.py:222
  63.1 7.7 %collective-permute-start.23 = (f32[2,8,2,8,128]{4,3,2,1,0:T(8,128)S(1)}, f32[2,8,2,8,128]{4,3,2,1,0:T(8,128)S(1)}, u32[]{:S(2)}, u32[]{:S(2)}) collective-permute-start(f32[2,8,2,8,128]{4,3,2,1,0:T(8,128)S(1)} %bitcast.30), channel_id=1, source_target_pairs={{0,6},{1,7},{2,4},{3,5},{4,2},{5,3},{6,0},{7,1},{8,14},{9,15},{10,... | collective-permute-start | bytes 393224 | tf_op jit(solution)/shard_map/ppermute | solution.py:222
  64.1 7.8 %collective-permute-start.24 = (f32[2,8,2,8,128]{4,3,2,1,0:T(8,128)S(1)}, f32[2,8,2,8,128]{4,3,2,1,0:T(8,128)S(1)}, u32[]{:S(2)}, u32[]{:S(2)}) collective-permute-start(f32[2,8,2,8,128]{4,3,2,1,0:T(8,128)S(1)} %bitcast.29), channel_id=1, source_target_pairs={{0,7},{1,6},{2,5},{3,4},{4,3},{5,2},{6,1},{7,0},{8,15},{9,14},{10,... | collective-permute-start | bytes 393224 | tf_op jit(solution)/shard_map/ppermute | solution.py:222

commit v2 on v1

--- a/solution.py
+++ b/solution.py
@@ -16,7 +16,7 @@
 
 
 ORDER = (2, 6, 4, 7, 5, 3, 1)
-REACH = (4, 3, 5, 2, 6, 1, 7)
+REACH = (5, 3, 6, 2, 7, 1)
 
 
 def split_table(table, axis):
@@ -205,15 +205,24 @@
         orbitals[1], "band", [(band_of(0, 0, c), band_of(1, 0, c)) for c in cores]
     )
     root = jnp.where(x_half == 1, handed, orbitals[0])
+    arrived = {
+        step: lax.ppermute(
+            root, "band", [(band_of(h, 0, c), band_of(h, step, c)) for h in cores for c in cores]
+        )
+        for step in REACH
+    }
+    arrived[4] = lax.ppermute(
+        arrived[5], "band", [(band_of(h, 5, c), band_of(h, 4, c)) for h in cores for c in cores]
+    )
     first = root
-    for step in REACH:
-        pairs = [(band_of(h, 0, c), band_of(h, step, c)) for h in cores for c in cores]
-        first = jnp.where(z == step, lax.ppermute(root, "band", pairs), first)
+    for step, value in arrived.items():
+        first = jnp.where(z == step, value, first)
     index, mixed, first = indices_after(first, here)
+    tables = right_table(index, -1.0), left_table(mixed, index, -1.0)
     second = lax.ppermute(first, "band", [(b, b ^ 16) for b in range(32)])
     own = (first, second)
     other = tuple(lax.ppermute(a, "band", [(b, b ^ 1) for b in range(32)]) for a in own)
-    return own, other, index, mixed
+    return own, other, tables
 
 
 def exchange(blocks):
@@ -231,7 +240,7 @@
 
 def apply_exchange(orbitals):
     here = lax.axis_index("fft")
-    own, other, index, mixed = fetch_sources(orbitals, here)
+    own, other, (right, left) = fetch_sources(orbitals, here)
     rows = PLANES * GRID
     work = pltpu.VMEM((2, rows, LANES), jnp.float32)
     block = (2, PLANES, 2, PLANES, LANES)
@@ -240,7 +249,7 @@
         forward_kernel,
         [block] * 8,
         [pltpu.VMEM((2, rows, 2 * LANES), jnp.float32), work],
-    )(orbitals, *own, *other, right_table(index, -1.0), left_table(mixed, index, -1.0))
+    )(orbitals, *own, *other, right, left)
     spectrum = exchange(spectrum)
     index, mixed, spectrum[ORDER[0]] = indices_after(spectrum[ORDER[0]], here)
     spectrum = [a.reshape(flat) for a in spectrum]

time: 73.9 us -> 71.4 us (0.966)
  the two profiles are of different devices: /device:TPU:6 before, /device:TPU:2 now
where the time goes in v2:
time: 71.4 us; the launch traced here: 71.1 us
  starting transfers between devices  35.8 us (50%)
  waiting for transfers between devices  26.7 us (37%)
  Pallas kernels  4.76 us (7%)
  other arithmetic  2.47 us (3%)
  local copies, waits for them, and re-layouts  1 us (1%)
    ppermute x14, starting transfers between devices, exchange(): results[d] = lax.ppermute(blocks[d], 'fft', [(p, p ^ d) for p in range(8)])  19.5 us
    ppermute x14, waiting for transfers between devices, exchange(): results[d] = lax.ppermute(blocks[d], 'fft', [(p, p ^ d) for p in range(8)])  17 us
    ppermute x6, starting transfers between devices, fetch_sources(): lax.ppermute(root, 'band', [(band_of(h, 0, c), band_of(h, step, c)) for h...  9.09 us
    ppermute x1, starting transfers between devices, fetch_sources(): lax.ppermute(orbitals[1], 'band', [(band_of(0, 0, c), band_of(1, 0, c)) f...  4.04 us
    ppermute x1, waiting for transfers between devices, fetch_sources(): second = lax.ppermute(first, 'band', [(b, b ^ 16) for b in range(32)])  3.27 us
    ppermute x1, waiting for transfers between devices, fetch_sources(): lax.ppermute(orbitals[1], 'band', [(band_of(0, 0, c), band_of(1, 0, c)) f...  2.71 us
    ppermute x1, starting transfers between devices, fetch_sources(): second = lax.ppermute(first, 'band', [(b, b ^ 16) for b in range(32)])  2.5 us
    ppermute x6, waiting for transfers between devices, fetch_sources(): lax.ppermute(root, 'band', [(band_of(h, 0, c), band_of(h, step, c)) for h...  2.38 us
  transfers between devices with their start and end apart: 25, of which 12 were waited for; matrix products, arithmetic and copies ran while one was open for 3% of the time, Pallas kernels for 0%

profile of v2, /device:TPU:2, one launch (start us, length us, event | category | flops | bytes accessed | tf_op | source)
XLA Modules:
  0.0 71.1 jit_solution(17461277477298456749)
XLA Ops:
  0.0 1.0 %slice_bitcast_fusion = f32[8,4096]{1,0:T(8,128)S(1)} fusion(f32[2,8,4096]{2,1,0:T(8,128)} %orb_ref.1), kind=kLoop, calls=%fused_computation.49 | loop fusion | bytes 262144 | tf_op jit(solution)/shard_map/squeeze | solution.py:205
  1.0 4.0 %collective-permute-start = (f32[8,4096]{1,0:T(8,128)S(1)}, f32[8,4096]{1,0:T(8,128)S(1)}, u32[]{:S(2)}, u32[]{:S(2)}) collective-permute-start(f32[8,4096]{1,0:T(8,128)S(1)} %slice_bitcast_fusion), channel_id=1, source_target_pairs={{0,128},{8,136},{1,129},{9,137},{2,130},{10,138},{3,131},{11,139},... | collective-permute-start | bytes 393224 | tf_op jit(solution)/shard_map/ppermute | solution.py:204
  5.1 2.7 %collective-permute-done = f32[8,4096]{1,0:T(8,128)S(1)} collective-permute-done((f32[8,4096]{1,0:T(8,128)S(1)}, f32[8,4096]{1,0:T(8,128)S(1)}, u32[]{:S(2)}, u32[]{:S(2)}) %collective-permute-start) | collective-permute-done | bytes 131104 | tf_op jit(solution)/shard_map/ppermute | solution.py:204
  7.8 2.6 %collective-permute-start.1 = (f32[8,4096]{1,0:T(8,128)S(1)}, f32[8,4096]{1,0:T(8,128)S(1)}, u32[]{:S(2)}, u32[]{:S(2)}) collective-permute-start(f32[8,4096]{1,0:T(8,128)S(1)} %bitcast_select_fusion), channel_id=1, source_target_pairs={{0,80},{8,88},{128,208},{136,216},{1,81},{9,89},{129,209},{137,217... | collective-permute-start | bytes 393224 | tf_op jit(solution)/shard_map/ppermute | solution.py:209
  10.4 1.3 %collective-permute-start.3 = (f32[8,4096]{1,0:T(8,128)S(1)}, f32[8,4096]{1,0:T(8,128)S(1)}, u32[]{:S(2)}, u32[]{:S(2)}) collective-permute-start(f32[8,4096]{1,0:T(8,128)S(1)} %bitcast_select_fusion), channel_id=1, source_target_pairs={{0,16},{8,24},{128,144},{136,152},{1,17},{9,25},{129,145},{137,153... | collective-permute-start | bytes 393224 | tf_op jit(solution)/shard_map/ppermute | solution.py:209
  11.7 1.3 %collective-permute-start.4 = (f32[8,4096]{1,0:T(8,128)S(1)}, f32[8,4096]{1,0:T(8,128)S(1)}, u32[]{:S(2)}, u32[]{:S(2)}) collective-permute-start(f32[8,4096]{1,0:T(8,128)S(1)} %bitcast_select_fusion), channel_id=1, source_target_pairs={{0,112},{8,120},{128,240},{136,248},{1,113},{9,121},{129,241},{137... | collective-permute-start | bytes 393224 | tf_op jit(solution)/shard_map/ppermute | solution.py:209
  13.0 1.3 %collective-permute-start.5 = (f32[8,4096]{1,0:T(8,128)S(1)}, f32[8,4096]{1,0:T(8,128)S(1)}, u32[]{:S(2)}, u32[]{:S(2)}) collective-permute-start(f32[8,4096]{1,0:T(8,128)S(1)} %bitcast_select_fusion), channel_id=1, source_target_pairs={{0,32},{8,40},{128,160},{136,168},{1,33},{9,41},{129,161},{137,169... | collective-permute-start | bytes 393224 | tf_op jit(solution)/shard_map/ppermute | solution.py:209
  14.3 1.3 %collective-permute-start.6 = (f32[8,4096]{1,0:T(8,128)S(1)}, f32[8,4096]{1,0:T(8,128)S(1)}, u32[]{:S(2)}, u32[]{:S(2)}) collective-permute-start(f32[8,4096]{1,0:T(8,128)S(1)} %bitcast_select_fusion), channel_id=1, source_target_pairs={{0,96},{8,104},{128,224},{136,232},{1,97},{9,105},{129,225},{137,2... | collective-permute-start | bytes 393224 | tf_op jit(solution)/shard_map/ppermute | solution.py:209
  15.6 0.0 collective-permute-done.1
  15.6 1.3 %collective-permute-start.7 = (f32[8,4096]{1,0:T(8,128)S(1)}, f32[8,4096]{1,0:T(8,128)S(1)}, u32[]{:S(2)}, u32[]{:S(2)}) collective-permute-start(f32[8,4096]{1,0:T(8,128)S(1)} %bitcast_select_fusion), channel_id=1, source_target_pairs={{0,48},{8,56},{128,176},{136,184},{1,49},{9,57},{129,177},{137,185... | collective-permute-start | bytes 393224 | tf_op jit(solution)/shard_map/ppermute | solution.py:209
  16.9 0.0 collective-permute-done.3
  16.9 0.7 collective-permute-start.2
  17.7 0.0 collective-permute-done.4
  17.7 0.0 collective-permute-done.5
  17.7 1.1 %collective-permute-done.6 = f32[8,4096]{1,0:T(8,128)S(1)} collective-permute-done((f32[8,4096]{1,0:T(8,128)S(1)}, f32[8,4096]{1,0:T(8,128)S(1)}, u32[]{:S(2)}, u32[]{:S(2)}) %collective-permute-start.6) | collective-permute-done | bytes 131104 | tf_op jit(solution)/shard_map/ppermute | solution.py:209
  18.7 1.3 %collective-permute-done.7 = f32[8,4096]{1,0:T(8,128)S(1)} collective-permute-done((f32[8,4096]{1,0:T(8,128)S(1)}, f32[8,4096]{1,0:T(8,128)S(1)}, u32[]{:S(2)}, u32[]{:S(2)}) %collective-permute-start.7) | collective-permute-done | bytes 131104 | tf_op jit(solution)/shard_map/ppermute | solution.py:209
  20.0 0.0 collective-permute-done.2
  20.1 2.5 %collective-permute-start.8 = (f32[8,4096]{1,0:T(8,128)S(1)}, f32[8,4096]{1,0:T(8,128)S(1)}, u32[]{:S(2)}, u32[]{:S(2)}) collective-permute-start(f32[8,4096]{1,0:T(8,128)S(1)} %select_select_fusion.refs_0_.refs_8_), channel_id=1, source_target_pairs={{0,128},{8,136},{16,144},{24,152},{32,160},{40,168},{48,176},{56,1... | collective-permute-start | bytes 393224 | tf_op jit(solution)/shard_map/ppermute | solution.py:222
  22.6 0.0 collective-permute-start.9
  22.6 0.3 fusion.58
  23.0 0.1 reduce-precision_convert_fusion.1
  23.1 0.1 reduce-precision_convert_fusion.5
  23.2 0.2 fusion.7
  23.4 3.3 %collective-permute-done.8.refs_1_.refs_9_ = f32[8,4096]{1,0:T(8,128)S(1)} collective-permute-done((f32[8,4096]{1,0:T(8,128)S(1)}, f32[8,4096]{1,0:T(8,128)S(1)}, u32[]{:S(2)}, u32[]{:S(2)}) %collective-permute-start.8) | collective-permute-done | bytes 131104 | tf_op jit(solution)/shard_map/ppermute | solution.py:222
  26.7 0.0 collective-permute-start.10
  26.7 0.0 collective-permute-done.9.refs_2_.refs_10_
  26.7 1.3 %collective-permute-done.10.refs_3_.refs_11_ = f32[8,4096]{1,0:T(8,128)S(1)} collective-permute-done((f32[8,4096]{1,0:T(8,128)S(1)}, f32[8,4096]{1,0:T(8,128)S(1)}, u32[]{:S(2)}, u32[]{:S(2)}) %collective-permute-start.10) | collective-permute-done | bytes 131104 | tf_op jit(solution)/shard_map/ppermute | solution.py:224
  28.0 1.9 %shard_map.17 = (f32[2,8,2,8,128]{4,3,2,1,0:T(8,128)S(1)}, f32[2,8,2,8,128]{4,3,2,1,0:T(8,128)S(1)}, f32[2,8,2,8,128]{4,3,2,1,0:T(8,128)S(1)}, f32[2,8,2,8,128]{...) custom-call(f32[2,8,4096]{2,1,0:T(8,128)S(1)} %copy-done, ...), custom_call_target="tpu_custom_call" | custom-call | tf_op jit(solution)/shard_map/pallas_call | solution.py:248
  29.9 3.3 %collective-permute-start.12 = (f32[2,8,2,8,128]{4,3,2,1,0:T(8,128)S(1)}, f32[2,8,2,8,128]{4,3,2,1,0:T(8,128)S(1)}, u32[]{:S(2)}, u32[]{:S(2)}) collective-permute-start(f32[2,8,2,8,128]{4,3,2,1,0:T(8,128)S(1)} %get-tuple-element.31), channel_id=1, source_target_pairs={{0,2},{1,3},{2,0},{3,1},{4,6},{5,7},{6,4},{7,5},{8,10},{9,11},{10,... | collective-permute-start | bytes 393224 | tf_op jit(solution)/shard_map/ppermute | solution.py:231
  33.2 0.7 collective-permute-start.11
  33.9 0.4 collective-permute-start.13
  34.3 0.5 collective-permute-start.14
  34.8 2.3 %collective-permute-start.15 = (f32[2,8,2,8,128]{4,3,2,1,0:T(8,128)S(1)}, f32[2,8,2,8,128]{4,3,2,1,0:T(8,128)S(1)}, u32[]{:S(2)}, u32[]{:S(2)}) collective-permute-start(f32[2,8,2,8,128]{4,3,2,1,0:T(8,128)S(1)} %get-tuple-element.35), channel_id=1, source_target_pairs={{0,5},{1,4},{2,7},{3,6},{4,1},{5,0},{6,3},{7,2},{8,13},{9,12},{10,... | collective-permute-start | bytes 393224 | tf_op jit(solution)/shard_map/ppermute | solution.py:231
  37.2 0.7 %collective-permute-done.12 = f32[2,8,2,8,128]{4,3,2,1,0:T(8,128)S(1)} collective-permute-done((f32[2,8,2,8,128]{4,3,2,1,0:T(8,128)S(1)}, f32[2,8,2,8,128]{4,3,2,1,0:T(8,128)S(1)}, u32[]{:S(2)}, u32[]{:S(2)}) %collective-permute-start.12) | collective-permute-done | bytes 131104 | tf_op jit(solution)/shard_map/ppermute | solution.py:231
  37.9 3.2 %collective-permute-start.16 = (f32[2,8,2,8,128]{4,3,2,1,0:T(8,128)S(1)}, f32[2,8,2,8,128]{4,3,2,1,0:T(8,128)S(1)}, u32[]{:S(2)}, u32[]{:S(2)}) collective-permute-start(f32[2,8,2,8,128]{4,3,2,1,0:T(8,128)S(1)} %get-tuple-element.36), channel_id=1, source_target_pairs={{0,6},{1,7},{2,4},{3,5},{4,2},{5,3},{6,0},{7,1},{8,14},{9,15},{10,... | collective-permute-start | bytes 393224 | tf_op jit(solution)/shard_map/ppermute | solution.py:231
  41.1 0.1 maximum_multiply_fusion
  41.2 0.1 broadcast_add_fusion
  41.3 0.2 fusion.3.refs_10_
  41.4 0.3 fusion.56
  41.8 0.1 reduce-precision_convert_fusion.3
  41.9 2.8 %collective-permute-done.11 = f32[2,8,2,8,128]{4,3,2,1,0:T(8,128)S(1)} collective-permute-done((f32[2,8,2,8,128]{4,3,2,1,0:T(8,128)S(1)}, f32[2,8,2,8,128]{4,3,2,1,0:T(8,128)S(1)}, u32[]{:S(2)}, u32[]{:S(2)}) %collective-permute-start.11) | collective-permute-done | bytes 131104 | tf_op jit(solution)/shard_map/ppermute | solution.py:231
  44.7 0.0 collective-permute-start.17
  44.7 0.0 collective-permute-done.13
  44.7 0.0 collective-permute-done.15
  44.8 3.6 %collective-permute-done.16 = f32[2,8,2,8,128]{4,3,2,1,0:T(8,128)S(1)} collective-permute-done((f32[2,8,2,8,128]{4,3,2,1,0:T(8,128)S(1)}, f32[2,8,2,8,128]{4,3,2,1,0:T(8,128)S(1)}, u32[]{:S(2)}, u32[]{:S(2)}) %collective-permute-start.16) | collective-permute-done | bytes 131104 | tf_op jit(solution)/shard_map/ppermute | solution.py:231
  48.4 3.4 %collective-permute-done.17 = f32[2,8,2,8,128]{4,3,2,1,0:T(8,128)S(1)} collective-permute-done((f32[2,8,2,8,128]{4,3,2,1,0:T(8,128)S(1)}, f32[2,8,2,8,128]{4,3,2,1,0:T(8,128)S(1)}, u32[]{:S(2)}, u32[]{:S(2)}) %collective-permute-start.17) | collective-permute-done | bytes 131104 | tf_op jit(solution)/shard_map/ppermute | solution.py:231
  51.8 1.1 %shard_map.18 = (f32[256,128]{1,0:T(8,128)S(1)}, f32[256,128]{1,0:T(8,128)S(1)}, f32[256,128]{1,0:T(8,128)S(1)}, f32[256,128]{1,0:T(8,128)S(1)}, f32[256,128]{1,...) custom-call(f32[256,128]{1,0:T(8,128)S(1)} %bitcast.20, ...), custom_call_target="tpu_custom_call" | custom-call | tf_op jit(solution)/shard_map/pallas_call | solution.py:256
  52.8 0.1 collective-permute-start.19
  52.9 0.1 collective-permute-start.18
  53.0 4.0 %collective-permute-start.20 = (f32[2,8,2,8,128]{4,3,2,1,0:T(8,128)S(1)}, f32[2,8,2,8,128]{4,3,2,1,0:T(8,128)S(1)}, u32[]{:S(2)}, u32[]{:S(2)}) collective-permute-start(f32[2,8,2,8,128]{4,3,2,1,0:T(8,128)S(1)} %bitcast.33), channel_id=1, source_target_pairs={{0,3},{1,2},{2,1},{3,0},{4,7},{5,6},{6,5},{7,4},{8,11},{9,10},{10,... | collective-permute-start | bytes 393224 | tf_op jit(solution)/shard_map/ppermute | solution.py:231
  57.0 0.5 collective-permute-start.21
  57.6 0.8 %collective-permute-start.22 = (f32[2,8,2,8,128]{4,3,2,1,0:T(8,128)S(1)}, f32[2,8,2,8,128]{4,3,2,1,0:T(8,128)S(1)}, u32[]{:S(2)}, u32[]{:S(2)}) collective-permute-start(f32[2,8,2,8,128]{4,3,2,1,0:T(8,128)S(1)} %bitcast.31), channel_id=1, source_target_pairs={{0,5},{1,4},{2,7},{3,6},{4,1},{5,0},{6,3},{7,2},{8,13},{9,12},{10,... | collective-permute-start | bytes 393224 | tf_op jit(solution)/shard_map/ppermute | solution.py:231
  58.4 2.2 %collective-permute-done.19.refs_2_ = f32[2,8,2,8,128]{4,3,2,1,0:T(8,128)S(1)} collective-permute-done((f32[2,8,2,8,128]{4,3,2,1,0:T(8,128)S(1)}, f32[2,8,2,8,128]{4,3,2,1,0:T(8,128)S(1)}, u32[]{:S(2)}, u32[]{:S(2)}) %collective-permute-start.19) | collective-permute-done | bytes 131104 | tf_op jit(solution)/shard_map/ppermute | solution.py:231
  60.6 0.0 collective-permute-start.23
  60.6 0.3 fusion.57
  61.0 0.1 reduce-precision_convert_fusion
  61.1 0.1 reduce-precision_convert_fusion.2
  61.2 0.2 fusion.8
  61.4 3.6 %collective-permute-start.24 = (f32[2,8,2,8,128]{4,3,2,1,0:T(8,128)S(1)}, f32[2,8,2,8,128]{4,3,2,1,0:T(8,128)S(1)}, u32[]{:S(2)}, u32[]{:S(2)}) collective-permute-start(f32[2,8,2,8,128]{4,3,2,1,0:T(8,128)S(1)} %bitcast.29), channel_id=1, source_target_pairs={{0,7},{1,6},{2,5},{3,4},{4,3},{5,2},{6,1},{7,0},{8,15},{9,14},{10,... | collective-permute-start | bytes 393224 | tf_op jit(solution)/shard_map/ppermute | solution.py:231
  65.0 0.0 collective-permute-done.20.refs_3_
  65.0 0.0 collective-permute-done.21.refs_4_
  65.1 3.7 %collective-permute-done.23.refs_6_ = f32[2,8,2,8,128]{4,3,2,1,0:T(8,128)S(1)} collective-permute-done((f32[2,8,2,8,128]{4,3,2,1,0:T(8,128)S(1)}, f32[2,8,2,8,128]{4,3,2,1,0:T(8,128)S(1)}, u32[]{:S(2)}, u32[]{:S(2)}) %collective-permute-start.23) | collective-permute-done | bytes 131104 | tf_op jit(solution)/shard_map/ppermute | solution.py:231
  68.8 0.6 collective-permute-done.24.refs_7_
  69.4 1.8 %shard_map.19 = f32[2,8,4096]{2,1,0:T(8,128)} custom-call(f32[2,8,2,8,128]{4,3,2,1,0:T(8,128)S(1)} %bitcast.22, f32[2,8,2,8,128]{4,3,2,1,0:T(8,128)S(1)} %collective-permute-done.18.refs_1_, f32[2,8,2,8,128]{4,3,2,1,0:T(8,128)S(1)} %collective-permute-done.19.refs_2_, f32[2,8,2,8,128]{4,3,2,1,0:T(8,128)S(1)} %collective-permute-done.20.refs_3_, ...), custom_call_target="tpu_custom_call" | custom-call | tf_op jit(solution)/shard_map/pallas_call | solution.py:264
  (22 shorter events, 0.3 us)
Async XLA Ops:
  0.0 7.8 %copy-start = (f32[2,8,4096]{2,1,0:T(8,128)S(1)}, f32[2,8,4096]{2,1,0:T(8,128)}, u32[]{:S(2)}) copy-start(f32[2,8,4096]{2,1,0:T(8,128)} %orb_ref.1) | copy-start | bytes 786436
  1.0 6.8 %collective-permute-start = (f32[8,4096]{1,0:T(8,128)S(1)}, f32[8,4096]{1,0:T(8,128)S(1)}, u32[]{:S(2)}, u32[]{:S(2)}) collective-permute-start(f32[8,4096]{1,0:T(8,128)S(1)} %slice_bitcast_fusion), channel_id=1, source_target_pairs={{0,128},{8,136},{1,129},{9,137},{2,130},{10,138},{3,131},{11,139},... | collective-permute-start | bytes 393224 | tf_op jit(solution)/shard_map/ppermute | solution.py:204
  7.8 7.8 %collective-permute-start.1 = (f32[8,4096]{1,0:T(8,128)S(1)}, f32[8,4096]{1,0:T(8,128)S(1)}, u32[]{:S(2)}, u32[]{:S(2)}) collective-permute-start(f32[8,4096]{1,0:T(8,128)S(1)} %bitcast_select_fusion), channel_id=1, source_target_pairs={{0,80},{8,88},{128,208},{136,216},{1,81},{9,89},{129,209},{137,217... | collective-permute-start | bytes 393224 | tf_op jit(solution)/shard_map/ppermute | solution.py:209
  10.4 6.5 %collective-permute-start.3 = (f32[8,4096]{1,0:T(8,128)S(1)}, f32[8,4096]{1,0:T(8,128)S(1)}, u32[]{:S(2)}, u32[]{:S(2)}) collective-permute-start(f32[8,4096]{1,0:T(8,128)S(1)} %bitcast_select_fusion), channel_id=1, source_target_pairs={{0,16},{8,24},{128,144},{136,152},{1,17},{9,25},{129,145},{137,153... | collective-permute-start | bytes 393224 | tf_op jit(solution)/shard_map/ppermute | solution.py:209
  11.7 6.0 %collective-permute-start.4 = (f32[8,4096]{1,0:T(8,128)S(1)}, f32[8,4096]{1,0:T(8,128)S(1)}, u32[]{:S(2)}, u32[]{:S(2)}) collective-permute-start(f32[8,4096]{1,0:T(8,128)S(1)} %bitcast_select_fusion), channel_id=1, source_target_pairs={{0,112},{8,120},{128,240},{136,248},{1,113},{9,121},{129,241},{137... | collective-permute-start | bytes 393224 | tf_op jit(solution)/shard_map/ppermute | solution.py:209
  13.0 4.7 %collective-permute-start.5 = (f32[8,4096]{1,0:T(8,128)S(1)}, f32[8,4096]{1,0:T(8,128)S(1)}, u32[]{:S(2)}, u32[]{:S(2)}) collective-permute-start(f32[8,4096]{1,0:T(8,128)S(1)} %bitcast_select_fusion), channel_id=1, source_target_pairs={{0,32},{8,40},{128,160},{136,168},{1,33},{9,41},{129,161},{137,169... | collective-permute-start | bytes 393224 | tf_op jit(solution)/shard_map/ppermute | solution.py:209
  14.3 4.4 %collective-permute-start.6 = (f32[8,4096]{1,0:T(8,128)S(1)}, f32[8,4096]{1,0:T(8,128)S(1)}, u32[]{:S(2)}, u32[]{:S(2)}) collective-permute-start(f32[8,4096]{1,0:T(8,128)S(1)} %bitcast_select_fusion), channel_id=1, source_target_pairs={{0,96},{8,104},{128,224},{136,232},{1,97},{9,105},{129,225},{137,2... | collective-permute-start | bytes 393224 | tf_op jit(solution)/shard_map/ppermute | solution.py:209
  15.6 4.4 %collective-permute-start.7 = (f32[8,4096]{1,0:T(8,128)S(1)}, f32[8,4096]{1,0:T(8,128)S(1)}, u32[]{:S(2)}, u32[]{:S(2)}) collective-permute-start(f32[8,4096]{1,0:T(8,128)S(1)} %bitcast_select_fusion), channel_id=1, source_target_pairs={{0,48},{8,56},{128,176},{136,184},{1,49},{9,57},{129,177},{137,185... | collective-permute-start | bytes 393224 | tf_op jit(solution)/shard_map/ppermute | solution.py:209
  16.9 3.1 %collective-permute-start.2 = (f32[8,4096]{1,0:T(8,128)S(1)}, f32[8,4096]{1,0:T(8,128)S(1)}, u32[]{:S(2)}, u32[]{:S(2)}) collective-permute-start(f32[8,4096]{1,0:T(8,128)S(1)} %collective-permute-done.1), channel_id=1, source_target_pairs={{80,64},{88,72},{208,192},{216,200},{81,65},{89,73},{209,193},{217... | collective-permute-start | bytes 393224 | tf_op jit(solution)/shard_map/ppermute | solution.py:214
  20.1 6.6 %collective-permute-start.8 = (f32[8,4096]{1,0:T(8,128)S(1)}, f32[8,4096]{1,0:T(8,128)S(1)}, u32[]{:S(2)}, u32[]{:S(2)}) collective-permute-start(f32[8,4096]{1,0:T(8,128)S(1)} %select_select_fusion.refs_0_.refs_8_), channel_id=1, source_target_pairs={{0,128},{8,136},{16,144},{24,152},{32,160},{40,168},{48,176},{56,1... | collective-permute-start | bytes 393224 | tf_op jit(solution)/shard_map/ppermute | solution.py:222
  22.6 4.1 %collective-permute-start.9 = (f32[8,4096]{1,0:T(8,128)S(1)}, f32[8,4096]{1,0:T(8,128)S(1)}, u32[]{:S(2)}, u32[]{:S(2)}) collective-permute-start(f32[8,4096]{1,0:T(8,128)S(1)} %select_select_fusion.refs_0_.refs_8_), channel_id=1, source_target_pairs={{0,8},{8,0},{16,24},{24,16},{32,40},{40,32},{48,56},{56,48},{64,72... | collective-permute-start | bytes 393224 | tf_op jit(solution)/shard_map/ppermute | solution.py:224
  26.7 1.3 %collective-permute-start.10 = (f32[8,4096]{1,0:T(8,128)S(1)}, f32[8,4096]{1,0:T(8,128)S(1)}, u32[]{:S(2)}, u32[]{:S(2)}) collective-permute-start(f32[8,4096]{1,0:T(8,128)S(1)} %collective-permute-done.8.refs_1_.refs_9_), channel_id=1, source_target_pairs={{0,8},{8,0},{16,24},{24,16},{32,40},{40,32},{48,56},{56,48},{64,72... | collective-permute-start | bytes 393224 | tf_op jit(solution)/shard_map/ppermute | solution.py:224
  29.9 8.0 %collective-permute-start.12 = (f32[2,8,2,8,128]{4,3,2,1,0:T(8,128)S(1)}, f32[2,8,2,8,128]{4,3,2,1,0:T(8,128)S(1)}, u32[]{:S(2)}, u32[]{:S(2)}) collective-permute-start(f32[2,8,2,8,128]{4,3,2,1,0:T(8,128)S(1)} %get-tuple-element.31), channel_id=1, source_target_pairs={{0,2},{1,3},{2,0},{3,1},{4,6},{5,7},{6,4},{7,5},{8,10},{9,11},{10,... | collective-permute-start | bytes 393224 | tf_op jit(solution)/shard_map/ppermute | solution.py:231
  33.2 11.5 %collective-permute-start.11 = (f32[2,8,2,8,128]{4,3,2,1,0:T(8,128)S(1)}, f32[2,8,2,8,128]{4,3,2,1,0:T(8,128)S(1)}, u32[]{:S(2)}, u32[]{:S(2)}) collective-permute-start(f32[2,8,2,8,128]{4,3,2,1,0:T(8,128)S(1)} %get-tuple-element.30), channel_id=1, source_target_pairs={{0,1},{1,0},{2,3},{3,2},{4,5},{5,4},{6,7},{7,6},{8,9},{9,8},{10,11... | collective-permute-start | bytes 393224 | tf_op jit(solution)/shard_map/ppermute | solution.py:231
  33.9 10.8 %collective-permute-start.13 = (f32[2,8,2,8,128]{4,3,2,1,0:T(8,128)S(1)}, f32[2,8,2,8,128]{4,3,2,1,0:T(8,128)S(1)}, u32[]{:S(2)}, u32[]{:S(2)}) collective-permute-start(f32[2,8,2,8,128]{4,3,2,1,0:T(8,128)S(1)} %get-tuple-element.33), channel_id=1, source_target_pairs={{0,3},{1,2},{2,1},{3,0},{4,7},{5,6},{6,5},{7,4},{8,11},{9,10},{10,... | collective-permute-start | bytes 393224 | tf_op jit(solution)/shard_map/ppermute | solution.py:231
  34.3 10.4 %collective-permute-start.14 = (f32[2,8,2,8,128]{4,3,2,1,0:T(8,128)S(1)}, f32[2,8,2,8,128]{4,3,2,1,0:T(8,128)S(1)}, u32[]{:S(2)}, u32[]{:S(2)}) collective-permute-start(f32[2,8,2,8,128]{4,3,2,1,0:T(8,128)S(1)} %get-tuple-element.34), channel_id=1, source_target_pairs={{0,4},{1,5},{2,6},{3,7},{4,0},{5,1},{6,2},{7,3},{8,12},{9,13},{10,... | collective-permute-start | bytes 393224 | tf_op jit(solution)/shard_map/ppermute | solution.py:231
  34.8 9.9 %collective-permute-start.15 = (f32[2,8,2,8,128]{4,3,2,1,0:T(8,128)S(1)}, f32[2,8,2,8,128]{4,3,2,1,0:T(8,128)S(1)}, u32[]{:S(2)}, u32[]{:S(2)}) collective-permute-start(f32[2,8,2,8,128]{4,3,2,1,0:T(8,128)S(1)} %get-tuple-element.35), channel_id=1, source_target_pairs={{0,5},{1,4},{2,7},{3,6},{4,1},{5,0},{6,3},{7,2},{8,13},{9,12},{10,... | collective-permute-start | bytes 393224 | tf_op jit(solution)/shard_map/ppermute | solution.py:231
  37.9 10.5 %collective-permute-start.16 = (f32[2,8,2,8,128]{4,3,2,1,0:T(8,128)S(1)}, f32[2,8,2,8,128]{4,3,2,1,0:T(8,128)S(1)}, u32[]{:S(2)}, u32[]{:S(2)}) collective-permute-start(f32[2,8,2,8,128]{4,3,2,1,0:T(8,128)S(1)} %get-tuple-element.36), channel_id=1, source_target_pairs={{0,6},{1,7},{2,4},{3,5},{4,2},{5,3},{6,0},{7,1},{8,14},{9,15},{10,... | collective-permute-start | bytes 393224 | tf_op jit(solution)/shard_map/ppermute | solution.py:231
  44.7 7.1 %collective-permute-start.17 = (f32[2,8,2,8,128]{4,3,2,1,0:T(8,128)S(1)}, f32[2,8,2,8,128]{4,3,2,1,0:T(8,128)S(1)}, u32[]{:S(2)}, u32[]{:S(2)}) collective-permute-start(f32[2,8,2,8,128]{4,3,2,1,0:T(8,128)S(1)} %get-tuple-element.37), channel_id=1, source_target_pairs={{0,7},{1,6},{2,5},{3,4},{4,3},{5,2},{6,1},{7,0},{8,15},{9,14},{10,... | collective-permute-start | bytes 393224 | tf_op jit(solution)/shard_map/ppermute | solution.py:231
  52.8 7.7 %collective-permute-start.19 = (f32[2,8,2,8,128]{4,3,2,1,0:T(8,128)S(1)}, f32[2,8,2,8,128]{4,3,2,1,0:T(8,128)S(1)}, u32[]{:S(2)}, u32[]{:S(2)}) collective-permute-start(f32[2,8,2,8,128]{4,3,2,1,0:T(8,128)S(1)} %bitcast.35), channel_id=1, source_target_pairs={{0,2},{1,3},{2,0},{3,1},{4,6},{5,7},{6,4},{7,5},{8,10},{9,11},{10,... | collective-permute-start | bytes 393224 | tf_op jit(solution)/shard_map/ppermute | solution.py:231
  52.9 8.4 %collective-permute-start.18 = (f32[2,8,2,8,128]{4,3,2,1,0:T(8,128)S(1)}, f32[2,8,2,8,128]{4,3,2,1,0:T(8,128)S(1)}, u32[]{:S(2)}, u32[]{:S(2)}) collective-permute-start(f32[2,8,2,8,128]{4,3,2,1,0:T(8,128)S(1)} %bitcast.34), channel_id=1, source_target_pairs={{0,1},{1,0},{2,3},{3,2},{4,5},{5,4},{6,7},{7,6},{8,9},{9,8},{10,11... | collective-permute-start | bytes 393224 | tf_op jit(solution)/shard_map/ppermute | solution.py:231
  53.0 12.0 %collective-permute-start.20 = (f32[2,8,2,8,128]{4,3,2,1,0:T(8,128)S(1)}, f32[2,8,2,8,128]{4,3,2,1,0:T(8,128)S(1)}, u32[]{:S(2)}, u32[]{:S(2)}) collective-permute-start(f32[2,8,2,8,128]{4,3,2,1,0:T(8,128)S(1)} %bitcast.33), channel_id=1, source_target_pairs={{0,3},{1,2},{2,1},{3,0},{4,7},{5,6},{6,5},{7,4},{8,11},{9,10},{10,... | collective-permute-start | bytes 393224 | tf_op jit(solution)/shard_map/ppermute | solution.py:231
  57.0 8.0 %collective-permute-start.21 = (f32[2,8,2,8,128]{4,3,2,1,0:T(8,128)S(1)}, f32[2,8,2,8,128]{4,3,2,1,0:T(8,128)S(1)}, u32[]{:S(2)}, u32[]{:S(2)}) collective-permute-start(f32[2,8,2,8,128]{4,3,2,1,0:T(8,128)S(1)} %bitcast.32), channel_id=1, source_target_pairs={{0,4},{1,5},{2,6},{3,7},{4,0},{5,1},{6,2},{7,3},{8,12},{9,13},{10,... | collective-permute-start | bytes 393224 | tf_op jit(solution)/shard_map/ppermute | solution.py:231
  57.6 7.5 %collective-permute-start.22 = (f32[2,8,2,8,128]{4,3,2,1,0:T(8,128)S(1)}, f32[2,8,2,8,128]{4,3,2,1,0:T(8,128)S(1)}, u32[]{:S(2)}, u32[]{:S(2)}) collective-permute-start(f32[2,8,2,8,128]{4,3,2,1,0:T(8,128)S(1)} %bitcast.31), channel_id=1, source_target_pairs={{0,5},{1,4},{2,7},{3,6},{4,1},{5,0},{6,3},{7,2},{8,13},{9,12},{10,... | collective-permute-start | bytes 393224 | tf_op jit(solution)/shard_map/ppermute | solution.py:231
  60.6 8.2 %collective-permute-start.23 = (f32[2,8,2,8,128]{4,3,2,1,0:T(8,128)S(1)}, f32[2,8,2,8,128]{4,3,2,1,0:T(8,128)S(1)}, u32[]{:S(2)}, u32[]{:S(2)}) collective-permute-start(f32[2,8,2,8,128]{4,3,2,1,0:T(8,128)S(1)} %bitcast.30), channel_id=1, source_target_pairs={{0,6},{1,7},{2,4},{3,5},{4,2},{5,3},{6,0},{7,1},{8,14},{9,15},{10,... | collective-permute-start | bytes 393224 | tf_op jit(solution)/shard_map/ppermute | solution.py:231
  61.4 8.0 %collective-permute-start.24 = (f32[2,8,2,8,128]{4,3,2,1,0:T(8,128)S(1)}, f32[2,8,2,8,128]{4,3,2,1,0:T(8,128)S(1)}, u32[]{:S(2)}, u32[]{:S(2)}) collective-permute-start(f32[2,8,2,8,128]{4,3,2,1,0:T(8,128)S(1)} %bitcast.29), channel_id=1, source_target_pairs={{0,7},{1,6},{2,5},{3,4},{4,3},{5,2},{6,1},{7,0},{8,15},{9,14},{10,... | collective-permute-start | bytes 393224 | tf_op jit(solution)/shard_map/ppermute | solution.py:231

commit v3 on v2

--- a/solution.py
+++ b/solution.py
@@ -84,49 +84,52 @@
     return jnp.dot(stacked, table, preferred_element_type=jnp.float32)
 
 
-def pair_sources(own_refs, other_refs, part, y_half, low_lanes):
-    columns = slice(y_half * LANES, (y_half + 1) * LANES)
-    own, other = own_refs[part][:, columns], other_refs[part][:, columns]
-    even = jnp.where(low_lanes, own, pltpu.roll(other, GRID, 1))
-    odd = jnp.where(low_lanes, pltpu.roll(own, GRID, 1), other)
-    return even, odd
+def both_rows(tile, low_lanes):
+    turned = pltpu.roll(tile, GRID, 1)
+    return jnp.where(low_lanes, tile, turned), jnp.where(low_lanes, turned, tile)
+
+
+def join_rows(first, second, low_lanes):
+    return (
+        jnp.where(low_lanes, first, pltpu.roll(second, GRID, 1)),
+        jnp.where(low_lanes, pltpu.roll(first, GRID, 1), second),
+    )
+
+
+def low_half():
+    return lax.broadcasted_iota(jnp.int32, (PLANES, LANES), 1) < GRID
 
 
 def forward_kernel(orb_ref, *refs):
-    own_refs, other_refs, (right_ref, left_ref) = refs[:2], refs[2:4], refs[4:6]
-    out_refs, (pair_ref, work_ref) = refs[6:14], refs[14:]
-    low_lanes = lax.broadcasted_iota(jnp.int32, (PLANES, LANES), 1) < GRID
+    source_refs, (right_ref, left_ref) = refs[:2], refs[2:4]
+    out_refs, (pair_ref, work_ref) = refs[-10:-2], refs[-2:]
+    low_lanes = low_half()
     for y_half in range(GRID // 2):
+        columns = slice(y_half * LANES, (y_half + 1) * LANES)
+        tiles = join_rows(orb_ref[0, :, columns], orb_ref[1, :, columns], low_lanes)
         for part in range(2):
-            even, odd = pair_sources(own_refs, other_refs, part, y_half, low_lanes)
-            for i in range(2):
-                tile = orb_ref[i, :, y_half * LANES : (y_half + 1) * LANES]
-                turned = pltpu.roll(tile, GRID, 1)
-                base = y_half * 2 * PLANES
-                lanes = slice(part * LANES, (part + 1) * LANES)
-                pair_ref[i, base : base + PLANES, lanes] = (
-                    jnp.where(low_lanes, tile, turned) * even
+            sources = both_rows(source_refs[part][:, columns], low_lanes)
+            for odd in range(2):
+                base = (y_half * 2 + odd) * PLANES
+                pair_ref[base : base + PLANES, part * LANES : (part + 1) * LANES] = (
+                    tiles[odd] * sources[odd]
                 )
-                pair_ref[i, base + PLANES : base + 2 * PLANES, lanes] = (
-                    jnp.where(low_lanes, turned, tile) * odd
-                )
-    for i in range(2):
-        result = times_right(pair_ref[i], right_ref[...])
-        work_ref[0] = result[:, :LANES]
-        work_ref[1] = result[:, LANES:]
-        for x in range(0, PLANES, 2):
-            columns = []
-            for plane in (x, x + 1):
-                rows = [work_ref[part, pl.ds(plane, GRID, stride=PLANES), :] for part in range(2)]
-                columns.append(jnp.concatenate(rows, 0))
-            result = times_left(left_ref[...], jnp.concatenate(columns, 1))
-            for k in range(2):
-                for part in range(2):
-                    for block in range(8):
-                        top = part * GRID + block * PLANES
-                        out_refs[block][i, x + k, part] = result[
-                            top : top + PLANES, k * LANES : (k + 1) * LANES
-                        ]
+    result = times_right(pair_ref[...], right_ref[...])
+    work_ref[0] = result[:, :LANES]
+    work_ref[1] = result[:, LANES:]
+    for x in range(0, PLANES, 2):
+        columns = []
+        for plane in (x, x + 1):
+            rows = [work_ref[part, pl.ds(plane, GRID, stride=PLANES), :] for part in range(2)]
+            columns.append(jnp.concatenate(rows, 0))
+        result = times_left(left_ref[...], jnp.concatenate(columns, 1))
+        for k in range(2):
+            for part in range(2):
+                for block in range(8):
+                    top = part * GRID + block * PLANES
+                    out_refs[block][0, x + k, part] = result[
+                        top : top + PLANES, k * LANES : (k + 1) * LANES
+                    ]
 
 
 def middle_kernel(*refs):
@@ -156,14 +159,14 @@
 
 
 def inverse_kernel(*refs):
-    in_refs, own_refs, other_refs = refs[:8], refs[8:10], refs[10:12]
-    right_ref, left_ref, out_ref, work_ref = refs[12:]
-    low_lanes = lax.broadcasted_iota(jnp.int32, (PLANES, LANES), 1) < GRID
-    for i in range(2):
+    in_refs, source_refs = refs[:8], (refs[8:10], refs[10:12])
+    right_ref, left_ref, out_ref, work_ref, sum_ref = refs[12:]
+    low_lanes = low_half()
+    for pair in range(2):
         for x in range(0, PLANES, 2):
             columns = []
             for plane in (x, x + 1):
-                rows = [ref[i, plane, part] for part in range(2) for ref in in_refs]
+                rows = [ref[pair, plane, part] for part in range(2) for ref in in_refs]
                 columns.append(jnp.concatenate(rows, 0))
             result = times_left(left_ref[...], jnp.concatenate(columns, 1))
             for k in range(2):
@@ -173,15 +176,20 @@
                     ]
         potential = times_right(jnp.concatenate([work_ref[0], work_ref[1]], 1), right_ref[...])
         for y_half in range(GRID // 2):
-            sums = [0.0, 0.0]
-            for part in range(2):
-                pair = pair_sources(own_refs, other_refs, part, y_half, low_lanes)
-                for odd in range(2):
-                    base = (y_half * 2 + odd) * PLANES
-                    values = potential[base : base + PLANES, part * LANES : (part + 1) * LANES]
-                    sums[odd] = sums[odd] + values * pair[odd]
-            even, odd = (s + pltpu.roll(s, GRID, 1) for s in sums)
-            out_ref[i, :, y_half * LANES : (y_half + 1) * LANES] = jnp.where(low_lanes, even, odd)
+            columns = slice(y_half * LANES, (y_half + 1) * LANES)
+            sources = [both_rows(ref[:, columns], low_lanes) for ref in source_refs[pair]]
+            sums = []
+            for odd in range(2):
+                base = (y_half * 2 + odd) * PLANES
+                rows = slice(base, base + PLANES)
+                values = potential[rows, :LANES] * sources[0][odd]
+                values = values + potential[rows, LANES:] * sources[1][odd]
+                if pair == 0:
+                    sum_ref[rows] = values
+                else:
+                    sums.append(sum_ref[rows] + values)
+            if sums:
+                out_ref[0, :, columns], out_ref[1, :, columns] = join_rows(*sums, low_lanes)
 
 
 def local_call(kernel, shapes, scratch):
@@ -191,6 +199,25 @@
         scratch_shapes=scratch,
         compiler_params=pltpu.CompilerParams(vmem_limit_bytes=24 << 20),
     )
+
+
+def forward_call(pair, blocks, *operands):
+    shape = jax.ShapeDtypeStruct((2, PLANES, 2, PLANES, LANES), jnp.float32)
+    rows = PLANES * GRID
+    whole = pl.BlockSpec(memory_space=pltpu.VMEM)
+    return pl.pallas_call(
+        forward_kernel,
+        grid=(1,),
+        in_specs=[whole] * len(operands) + [pl.BlockSpec(memory_space=pl.ANY)] * len(blocks),
+        out_specs=[pl.BlockSpec((1, PLANES, 2, PLANES, LANES), lambda _: (pair, 0, 0, 0, 0))] * 8,
+        out_shape=[shape] * 8,
+        scratch_shapes=[
+            pltpu.VMEM((rows, 2 * LANES), jnp.float32),
+            pltpu.VMEM((2, rows, LANES), jnp.float32),
+        ],
+        input_output_aliases={len(operands) + k: k for k in range(len(blocks))},
+        compiler_params=pltpu.CompilerParams(vmem_limit_bytes=24 << 20),
+    )(*operands, *blocks)
 
 
 def band_of(x_half, z, core):
@@ -245,11 +272,8 @@
     work = pltpu.VMEM((2, rows, LANES), jnp.float32)
     block = (2, PLANES, 2, PLANES, LANES)
     flat = (2 * PLANES * 2 * PLANES, LANES)
-    spectrum = local_call(
-        forward_kernel,
-        [block] * 8,
-        [pltpu.VMEM((2, rows, 2 * LANES), jnp.float32), work],
-    )(orbitals, *own, *other, right, left)
+    spectrum = forward_call(0, [], orbitals, *own, right, left)
+    spectrum = forward_call(1, spectrum, orbitals, *other, right, left)
     spectrum = exchange(spectrum)
     index, mixed, spectrum[ORDER[0]] = indices_after(spectrum[ORDER[0]], here)
     spectrum = [a.reshape(flat) for a in spectrum]
@@ -261,7 +285,8 @@
     )
     returned = exchange([a.reshape(block) for a in filtered])
     index, mixed, returned[ORDER[0]] = indices_after(returned[ORDER[0]], here)
-    return local_call(inverse_kernel, [(2, PLANES, GRID * GRID)], [work])(
+    total = pltpu.VMEM((rows, LANES), jnp.float32)
+    return local_call(inverse_kernel, [(2, PLANES, GRID * GRID)], [work, total])(
         *returned, *own, *other, right_table(index, 1.0), left_table(index, mixed, 1.0)
     )[0]
 

time: 71.4 us -> 70.7 us (level)
  the two profiles are of different devices: /device:TPU:2 before, /device:TPU:6 now
where the time goes in v3:
time: 70.7 us; the launch traced here: 70.4 us
  starting transfers between devices  31.1 us (44%)
  waiting for transfers between devices  30.7 us (43%)
  Pallas kernels  4.75 us (7%)
  other arithmetic  2.47 us (3%)
  local copies, waits for them, and re-layouts  1 us (1%)
    ppermute x14, starting transfers between devices, exchange(): results[d] = lax.ppermute(blocks[d], 'fft', [(p, p ^ d) for p in range(8)])  20.2 us
    ppermute x14, waiting for transfers between devices, exchange(): results[d] = lax.ppermute(blocks[d], 'fft', [(p, p ^ d) for p in range(8)])  16.4 us
    ppermute x6, starting transfers between devices, fetch_sources(): lax.ppermute(root, 'band', [(band_of(h, 0, c), band_of(h, step, c)) for h...  7.78 us
    ppermute x1, waiting for transfers between devices, fetch_sources(): lax.ppermute(orbitals[1], 'band', [(band_of(0, 0, c), band_of(1, 0, c)) f...  7.32 us
    ppermute x1, waiting for transfers between devices, fetch_sources(): second = lax.ppermute(first, 'band', [(b, b ^ 16) for b in range(32)])  4.56 us
    ppermute x6, waiting for transfers between devices, fetch_sources(): lax.ppermute(root, 'band', [(band_of(h, 0, c), band_of(h, step, c)) for h...  2.11 us
    pallas_call x2, Pallas kernels, forward_call(): pl.pallas_call(forward_kernel, grid=(1,), in_specs=[whole] * len(operands...  1.91 us
    pallas_call x1, Pallas kernels, apply_exchange(): local_call(inverse_kernel, [(2, PLANES, GRID * GRID)], [work, total])  1.77 us
  transfers between devices with their start and end apart: 25, of which 12 were waited for; matrix products, arithmetic and copies ran while one was open for 3% of the time, Pallas kernels for 1%

profile of v3, /device:TPU:6, one launch (start us, length us, event | category | flops | bytes accessed | tf_op | source)
XLA Modules:
  0.0 70.4 jit_solution(13273801665948936880)
XLA Ops:
  0.0 1.0 %slice_bitcast_fusion = f32[8,4096]{1,0:T(8,128)S(1)} fusion(f32[2,8,4096]{2,1,0:T(8,128)} %orb_ref.3), kind=kLoop, calls=%fused_computation.49 | loop fusion | bytes 262144 | tf_op jit(solution)/shard_map/squeeze | solution.py:232
  1.0 1.3 %collective-permute-start = (f32[8,4096]{1,0:T(8,128)S(1)}, f32[8,4096]{1,0:T(8,128)S(1)}, u32[]{:S(2)}, u32[]{:S(2)}) collective-permute-start(f32[8,4096]{1,0:T(8,128)S(1)} %slice_bitcast_fusion), channel_id=1, source_target_pairs={{0,128},{8,136},{1,129},{9,137},{2,130},{10,138},{3,131},{11,139},... | collective-permute-start | bytes 393224 | tf_op jit(solution)/shard_map/ppermute | solution.py:231
  2.3 7.3 %collective-permute-done = f32[8,4096]{1,0:T(8,128)S(1)} collective-permute-done((f32[8,4096]{1,0:T(8,128)S(1)}, f32[8,4096]{1,0:T(8,128)S(1)}, u32[]{:S(2)}, u32[]{:S(2)}) %collective-permute-start) | collective-permute-done | bytes 131104 | tf_op jit(solution)/shard_map/ppermute | solution.py:231
  9.6 1.3 %collective-permute-start.1 = (f32[8,4096]{1,0:T(8,128)S(1)}, f32[8,4096]{1,0:T(8,128)S(1)}, u32[]{:S(2)}, u32[]{:S(2)}) collective-permute-start(f32[8,4096]{1,0:T(8,128)S(1)} %bitcast_select_fusion), channel_id=1, source_target_pairs={{0,80},{8,88},{128,208},{136,216},{1,81},{9,89},{129,209},{137,217... | collective-permute-start | bytes 393224 | tf_op jit(solution)/shard_map/ppermute | solution.py:236
  11.0 1.3 %collective-permute-start.3 = (f32[8,4096]{1,0:T(8,128)S(1)}, f32[8,4096]{1,0:T(8,128)S(1)}, u32[]{:S(2)}, u32[]{:S(2)}) collective-permute-start(f32[8,4096]{1,0:T(8,128)S(1)} %bitcast_select_fusion), channel_id=1, source_target_pairs={{0,16},{8,24},{128,144},{136,152},{1,17},{9,25},{129,145},{137,153... | collective-permute-start | bytes 393224 | tf_op jit(solution)/shard_map/ppermute | solution.py:236
  12.3 1.3 %collective-permute-start.4 = (f32[8,4096]{1,0:T(8,128)S(1)}, f32[8,4096]{1,0:T(8,128)S(1)}, u32[]{:S(2)}, u32[]{:S(2)}) collective-permute-start(f32[8,4096]{1,0:T(8,128)S(1)} %bitcast_select_fusion), channel_id=1, source_target_pairs={{0,112},{8,120},{128,240},{136,248},{1,113},{9,121},{129,241},{137... | collective-permute-start | bytes 393224 | tf_op jit(solution)/shard_map/ppermute | solution.py:236
  13.6 1.3 %collective-permute-start.5 = (f32[8,4096]{1,0:T(8,128)S(1)}, f32[8,4096]{1,0:T(8,128)S(1)}, u32[]{:S(2)}, u32[]{:S(2)}) collective-permute-start(f32[8,4096]{1,0:T(8,128)S(1)} %bitcast_select_fusion), channel_id=1, source_target_pairs={{0,32},{8,40},{128,160},{136,168},{1,33},{9,41},{129,161},{137,169... | collective-permute-start | bytes 393224 | tf_op jit(solution)/shard_map/ppermute | solution.py:236
  14.9 1.3 %collective-permute-start.6 = (f32[8,4096]{1,0:T(8,128)S(1)}, f32[8,4096]{1,0:T(8,128)S(1)}, u32[]{:S(2)}, u32[]{:S(2)}) collective-permute-start(f32[8,4096]{1,0:T(8,128)S(1)} %bitcast_select_fusion), channel_id=1, source_target_pairs={{0,96},{8,104},{128,224},{136,232},{1,97},{9,105},{129,225},{137,2... | collective-permute-start | bytes 393224 | tf_op jit(solution)/shard_map/ppermute | solution.py:236
  16.2 0.0 collective-permute-done.1
  16.2 1.3 %collective-permute-start.7 = (f32[8,4096]{1,0:T(8,128)S(1)}, f32[8,4096]{1,0:T(8,128)S(1)}, u32[]{:S(2)}, u32[]{:S(2)}) collective-permute-start(f32[8,4096]{1,0:T(8,128)S(1)} %bitcast_select_fusion), channel_id=1, source_target_pairs={{0,48},{8,56},{128,176},{136,184},{1,49},{9,57},{129,177},{137,185... | collective-permute-start | bytes 393224 | tf_op jit(solution)/shard_map/ppermute | solution.py:236
  17.5 0.0 collective-permute-done.3
  17.5 0.7 collective-permute-start.2
  18.2 0.0 collective-permute-done.4
  18.2 0.0 collective-permute-done.5
  18.2 0.8 %collective-permute-done.6 = f32[8,4096]{1,0:T(8,128)S(1)} collective-permute-done((f32[8,4096]{1,0:T(8,128)S(1)}, f32[8,4096]{1,0:T(8,128)S(1)}, u32[]{:S(2)}, u32[]{:S(2)}) %collective-permute-start.6) | collective-permute-done | bytes 131104 | tf_op jit(solution)/shard_map/ppermute | solution.py:236
  19.0 1.3 %collective-permute-done.7 = f32[8,4096]{1,0:T(8,128)S(1)} collective-permute-done((f32[8,4096]{1,0:T(8,128)S(1)}, f32[8,4096]{1,0:T(8,128)S(1)}, u32[]{:S(2)}, u32[]{:S(2)}) %collective-permute-start.7) | collective-permute-done | bytes 131104 | tf_op jit(solution)/shard_map/ppermute | solution.py:236
  20.3 0.0 collective-permute-done.2
  20.4 1.2 %collective-permute-start.9 = (f32[8,4096]{1,0:T(8,128)S(1)}, f32[8,4096]{1,0:T(8,128)S(1)}, u32[]{:S(2)}, u32[]{:S(2)}) collective-permute-start(f32[8,4096]{1,0:T(8,128)S(1)} %select_select_fusion.refs_0_.refs_8_), channel_id=1, source_target_pairs={{0,128},{8,136},{16,144},{24,152},{32,160},{40,168},{48,176},{56,1... | collective-permute-start | bytes 393224 | tf_op jit(solution)/shard_map/ppermute | solution.py:249
  21.6 0.0 collective-permute-start.8
  21.6 0.3 fusion.58
  22.0 0.1 reduce-precision_convert_fusion.1
  22.1 0.1 reduce-precision_convert_fusion.5
  22.2 0.2 fusion.7
  22.4 4.6 %collective-permute-done.9.refs_1_.refs_9_ = f32[8,4096]{1,0:T(8,128)S(1)} collective-permute-done((f32[8,4096]{1,0:T(8,128)S(1)}, f32[8,4096]{1,0:T(8,128)S(1)}, u32[]{:S(2)}, u32[]{:S(2)}) %collective-permute-start.9) | collective-permute-done | bytes 131104 | tf_op jit(solution)/shard_map/ppermute | solution.py:249
  27.0 0.0 collective-permute-start.10
  27.0 1.0 %shard_map.17 = (f32[2,8,2,8,128]{4,3,2,1,0:T(8,128)S(1)}, f32[2,8,2,8,128]{4,3,2,1,0:T(8,128)S(1)}, f32[2,8,2,8,128]{4,3,2,1,0:T(8,128)S(1)}, f32[2,8,2,8,128]{...) custom-call(f32[2,8,4096]{2,1,0:T(8,128)S(1)} %copy-done, ...), custom_call_target="tpu_custom_call" | custom-call | tf_op jit(solution)/shard_map/pallas_call | solution.py:208
  28.0 0.0 collective-permute-done.8.refs_0_.refs_10_
  28.0 0.3 collective-permute-done.10.refs_1_.refs_11_
  28.3 1.0 %shard_map.18 = (f32[2,8,2,8,128]{4,3,2,1,0:T(8,128)S(1)}, f32[2,8,2,8,128]{4,3,2,1,0:T(8,128)S(1)}, f32[2,8,2,8,128]{4,3,2,1,0:T(8,128)S(1)}, f32[2,8,2,8,128]{...) custom-call(f32[2,8,4096]{2,1,0:T(8,128)S(1)} %copy-done, ...), custom_call_target="tpu_custom_call", output_to_operand_aliasing={{0}: (5, {}), {1}: (6, {}), {2}: (7, {}), {3}: (8, {}), {4}... | custom-call | tf_op jit(solution)/shard_map/pallas_call | solution.py:208
  29.3 3.3 %collective-permute-start.12 = (f32[2,8,2,8,128]{4,3,2,1,0:T(8,128)S(1)}, f32[2,8,2,8,128]{4,3,2,1,0:T(8,128)S(1)}, u32[]{:S(2)}, u32[]{:S(2)}) collective-permute-start(f32[2,8,2,8,128]{4,3,2,1,0:T(8,128)S(1)} %get-tuple-element.47), channel_id=1, source_target_pairs={{0,2},{1,3},{2,0},{3,1},{4,6},{5,7},{6,4},{7,5},{8,10},{9,11},{10,... | collective-permute-start | bytes 393224 | tf_op jit(solution)/shard_map/ppermute | solution.py:258
  32.6 0.7 collective-permute-start.11
  33.2 0.4 collective-permute-start.13
  33.6 0.8 %collective-permute-start.14 = (f32[2,8,2,8,128]{4,3,2,1,0:T(8,128)S(1)}, f32[2,8,2,8,128]{4,3,2,1,0:T(8,128)S(1)}, u32[]{:S(2)}, u32[]{:S(2)}) collective-permute-start(f32[2,8,2,8,128]{4,3,2,1,0:T(8,128)S(1)} %get-tuple-element.50), channel_id=1, source_target_pairs={{0,4},{1,5},{2,6},{3,7},{4,0},{5,1},{6,2},{7,3},{8,12},{9,13},{10,... | collective-permute-start | bytes 393224 | tf_op jit(solution)/shard_map/ppermute | solution.py:258
  34.4 2.1 %collective-permute-start.15 = (f32[2,8,2,8,128]{4,3,2,1,0:T(8,128)S(1)}, f32[2,8,2,8,128]{4,3,2,1,0:T(8,128)S(1)}, u32[]{:S(2)}, u32[]{:S(2)}) collective-permute-start(f32[2,8,2,8,128]{4,3,2,1,0:T(8,128)S(1)} %get-tuple-element.51), channel_id=1, source_target_pairs={{0,5},{1,4},{2,7},{3,6},{4,1},{5,0},{6,3},{7,2},{8,13},{9,12},{10,... | collective-permute-start | bytes 393224 | tf_op jit(solution)/shard_map/ppermute | solution.py:258
  36.5 0.7 %collective-permute-done.12 = f32[2,8,2,8,128]{4,3,2,1,0:T(8,128)S(1)} collective-permute-done((f32[2,8,2,8,128]{4,3,2,1,0:T(8,128)S(1)}, f32[2,8,2,8,128]{4,3,2,1,0:T(8,128)S(1)}, u32[]{:S(2)}, u32[]{:S(2)}) %collective-permute-start.12) | collective-permute-done | bytes 131104 | tf_op jit(solution)/shard_map/ppermute | solution.py:258
  37.2 3.6 %collective-permute-start.16 = (f32[2,8,2,8,128]{4,3,2,1,0:T(8,128)S(1)}, f32[2,8,2,8,128]{4,3,2,1,0:T(8,128)S(1)}, u32[]{:S(2)}, u32[]{:S(2)}) collective-permute-start(f32[2,8,2,8,128]{4,3,2,1,0:T(8,128)S(1)} %get-tuple-element.52), channel_id=1, source_target_pairs={{0,6},{1,7},{2,4},{3,5},{4,2},{5,3},{6,0},{7,1},{8,14},{9,15},{10,... | collective-permute-start | bytes 393224 | tf_op jit(solution)/shard_map/ppermute | solution.py:258
  40.9 0.1 maximum_multiply_fusion
  41.0 0.1 broadcast_add_fusion
  41.0 0.2 fusion.3.refs_10_
  41.2 0.3 fusion.56
  41.6 0.1 reduce-precision_convert_fusion.3
  41.7 2.5 %collective-permute-done.11 = f32[2,8,2,8,128]{4,3,2,1,0:T(8,128)S(1)} collective-permute-done((f32[2,8,2,8,128]{4,3,2,1,0:T(8,128)S(1)}, f32[2,8,2,8,128]{4,3,2,1,0:T(8,128)S(1)}, u32[]{:S(2)}, u32[]{:S(2)}) %collective-permute-start.11) | collective-permute-done | bytes 131104 | tf_op jit(solution)/shard_map/ppermute | solution.py:258
  44.2 0.0 collective-permute-done.13
  44.2 0.0 collective-permute-done.14
  44.2 3.6 %collective-permute-done.16 = f32[2,8,2,8,128]{4,3,2,1,0:T(8,128)S(1)} collective-permute-done((f32[2,8,2,8,128]{4,3,2,1,0:T(8,128)S(1)}, f32[2,8,2,8,128]{4,3,2,1,0:T(8,128)S(1)}, u32[]{:S(2)}, u32[]{:S(2)}) %collective-permute-start.16) | collective-permute-done | bytes 131104 | tf_op jit(solution)/shard_map/ppermute | solution.py:258
  47.8 3.4 %collective-permute-done.17 = f32[2,8,2,8,128]{4,3,2,1,0:T(8,128)S(1)} collective-permute-done((f32[2,8,2,8,128]{4,3,2,1,0:T(8,128)S(1)}, f32[2,8,2,8,128]{4,3,2,1,0:T(8,128)S(1)}, u32[]{:S(2)}, u32[]{:S(2)}) %collective-permute-start.17) | collective-permute-done | bytes 131104 | tf_op jit(solution)/shard_map/ppermute | solution.py:258
  51.2 1.1 %shard_map.19 = (f32[256,128]{1,0:T(8,128)S(1)}, f32[256,128]{1,0:T(8,128)S(1)}, f32[256,128]{1,0:T(8,128)S(1)}, f32[256,128]{1,0:T(8,128)S(1)}, f32[256,128]{1,...) custom-call(f32[256,128]{1,0:T(8,128)S(1)} %bitcast.20, ...), custom_call_target="tpu_custom_call" | custom-call | tf_op jit(solution)/shard_map/pallas_call | solution.py:280
  52.3 0.1 collective-permute-start.19
  52.4 0.2 collective-permute-start.18
  52.6 3.9 %collective-permute-start.20 = (f32[2,8,2,8,128]{4,3,2,1,0:T(8,128)S(1)}, f32[2,8,2,8,128]{4,3,2,1,0:T(8,128)S(1)}, u32[]{:S(2)}, u32[]{:S(2)}) collective-permute-start(f32[2,8,2,8,128]{4,3,2,1,0:T(8,128)S(1)} %bitcast.33), channel_id=1, source_target_pairs={{0,3},{1,2},{2,1},{3,0},{4,7},{5,6},{6,5},{7,4},{8,11},{9,10},{10,... | collective-permute-start | bytes 393224 | tf_op jit(solution)/shard_map/ppermute | solution.py:258
  56.5 0.8 %collective-permute-start.21 = (f32[2,8,2,8,128]{4,3,2,1,0:T(8,128)S(1)}, f32[2,8,2,8,128]{4,3,2,1,0:T(8,128)S(1)}, u32[]{:S(2)}, u32[]{:S(2)}) collective-permute-start(f32[2,8,2,8,128]{4,3,2,1,0:T(8,128)S(1)} %bitcast.32), channel_id=1, source_target_pairs={{0,4},{1,5},{2,6},{3,7},{4,0},{5,1},{6,2},{7,3},{8,12},{9,13},{10,... | collective-permute-start | bytes 393224 | tf_op jit(solution)/shard_map/ppermute | solution.py:258
  57.3 0.6 collective-permute-start.22
  57.9 2.0 %collective-permute-done.19.refs_2_ = f32[2,8,2,8,128]{4,3,2,1,0:T(8,128)S(1)} collective-permute-done((f32[2,8,2,8,128]{4,3,2,1,0:T(8,128)S(1)}, f32[2,8,2,8,128]{4,3,2,1,0:T(8,128)S(1)}, u32[]{:S(2)}, u32[]{:S(2)}) %collective-permute-start.19) | collective-permute-done | bytes 131104 | tf_op jit(solution)/shard_map/ppermute | solution.py:258
  59.9 0.0 collective-permute-start.23
  59.9 0.3 fusion.57
  60.3 0.1 reduce-precision_convert_fusion
  60.4 0.1 reduce-precision_convert_fusion.2
  60.5 0.2 fusion.8
  60.7 3.7 %collective-permute-start.24 = (f32[2,8,2,8,128]{4,3,2,1,0:T(8,128)S(1)}, f32[2,8,2,8,128]{4,3,2,1,0:T(8,128)S(1)}, u32[]{:S(2)}, u32[]{:S(2)}) collective-permute-start(f32[2,8,2,8,128]{4,3,2,1,0:T(8,128)S(1)} %bitcast.29), channel_id=1, source_target_pairs={{0,7},{1,6},{2,5},{3,4},{4,3},{5,2},{6,1},{7,0},{8,15},{9,14},{10,... | collective-permute-start | bytes 393224 | tf_op jit(solution)/shard_map/ppermute | solution.py:258
  64.5 0.0 collective-permute-done.20.refs_3_
  64.5 0.0 collective-permute-done.22.refs_5_
  64.5 3.6 %collective-permute-done.23.refs_6_ = f32[2,8,2,8,128]{4,3,2,1,0:T(8,128)S(1)} collective-permute-done((f32[2,8,2,8,128]{4,3,2,1,0:T(8,128)S(1)}, f32[2,8,2,8,128]{4,3,2,1,0:T(8,128)S(1)}, u32[]{:S(2)}, u32[]{:S(2)}) %collective-permute-start.23) | collective-permute-done | bytes 131104 | tf_op jit(solution)/shard_map/ppermute | solution.py:258
  68.1 0.6 collective-permute-done.24.refs_7_
  68.7 1.8 %shard_map.20 = f32[2,8,4096]{2,1,0:T(8,128)} custom-call(f32[2,8,2,8,128]{4,3,2,1,0:T(8,128)S(1)} %bitcast.22, f32[2,8,2,8,128]{4,3,2,1,0:T(8,128)S(1)} %collective-permute-done.18.refs_1_, f32[2,8,2,8,128]{4,3,2,1,0:T(8,128)S(1)} %collective-permute-done.19.refs_2_, f32[2,8,2,8,128]{4,3,2,1,0:T(8,128)S(1)} %collective-permute-done.20.refs_3_, ...), custom_call_target="tpu_custom_call" | custom-call | tf_op jit(solution)/shard_map/pallas_call | solution.py:289
  (23 shorter events, 0.3 us)
Async XLA Ops:
  0.0 9.6 %copy-start = (f32[2,8,4096]{2,1,0:T(8,128)S(1)}, f32[2,8,4096]{2,1,0:T(8,128)}, u32[]{:S(2)}) copy-start(f32[2,8,4096]{2,1,0:T(8,128)} %orb_ref.3) | copy-start | bytes 786436
  1.0 8.6 %collective-permute-start = (f32[8,4096]{1,0:T(8,128)S(1)}, f32[8,4096]{1,0:T(8,128)S(1)}, u32[]{:S(2)}, u32[]{:S(2)}) collective-permute-start(f32[8,4096]{1,0:T(8,128)S(1)} %slice_bitcast_fusion), channel_id=1, source_target_pairs={{0,128},{8,136},{1,129},{9,137},{2,130},{10,138},{3,131},{11,139},... | collective-permute-start | bytes 393224 | tf_op jit(solution)/shard_map/ppermute | solution.py:231
  9.6 6.5 %collective-permute-start.1 = (f32[8,4096]{1,0:T(8,128)S(1)}, f32[8,4096]{1,0:T(8,128)S(1)}, u32[]{:S(2)}, u32[]{:S(2)}) collective-permute-start(f32[8,4096]{1,0:T(8,128)S(1)} %bitcast_select_fusion), channel_id=1, source_target_pairs={{0,80},{8,88},{128,208},{136,216},{1,81},{9,89},{129,209},{137,217... | collective-permute-start | bytes 393224 | tf_op jit(solution)/shard_map/ppermute | solution.py:236
  11.0 6.5 %collective-permute-start.3 = (f32[8,4096]{1,0:T(8,128)S(1)}, f32[8,4096]{1,0:T(8,128)S(1)}, u32[]{:S(2)}, u32[]{:S(2)}) collective-permute-start(f32[8,4096]{1,0:T(8,128)S(1)} %bitcast_select_fusion), channel_id=1, source_target_pairs={{0,16},{8,24},{128,144},{136,152},{1,17},{9,25},{129,145},{137,153... | collective-permute-start | bytes 393224 | tf_op jit(solution)/shard_map/ppermute | solution.py:236
  12.3 6.0 %collective-permute-start.4 = (f32[8,4096]{1,0:T(8,128)S(1)}, f32[8,4096]{1,0:T(8,128)S(1)}, u32[]{:S(2)}, u32[]{:S(2)}) collective-permute-start(f32[8,4096]{1,0:T(8,128)S(1)} %bitcast_select_fusion), channel_id=1, source_target_pairs={{0,112},{8,120},{128,240},{136,248},{1,113},{9,121},{129,241},{137... | collective-permute-start | bytes 393224 | tf_op jit(solution)/shard_map/ppermute | solution.py:236
  13.6 4.7 %collective-permute-start.5 = (f32[8,4096]{1,0:T(8,128)S(1)}, f32[8,4096]{1,0:T(8,128)S(1)}, u32[]{:S(2)}, u32[]{:S(2)}) collective-permute-start(f32[8,4096]{1,0:T(8,128)S(1)} %bitcast_select_fusion), channel_id=1, source_target_pairs={{0,32},{8,40},{128,160},{136,168},{1,33},{9,41},{129,161},{137,169... | collective-permute-start | bytes 393224 | tf_op jit(solution)/shard_map/ppermute | solution.py:236
  14.9 4.2 %collective-permute-start.6 = (f32[8,4096]{1,0:T(8,128)S(1)}, f32[8,4096]{1,0:T(8,128)S(1)}, u32[]{:S(2)}, u32[]{:S(2)}) collective-permute-start(f32[8,4096]{1,0:T(8,128)S(1)} %bitcast_select_fusion), channel_id=1, source_target_pairs={{0,96},{8,104},{128,224},{136,232},{1,97},{9,105},{129,225},{137,2... | collective-permute-start | bytes 393224 | tf_op jit(solution)/shard_map/ppermute | solution.py:236
  16.2 4.2 %collective-permute-start.7 = (f32[8,4096]{1,0:T(8,128)S(1)}, f32[8,4096]{1,0:T(8,128)S(1)}, u32[]{:S(2)}, u32[]{:S(2)}) collective-permute-start(f32[8,4096]{1,0:T(8,128)S(1)} %bitcast_select_fusion), channel_id=1, source_target_pairs={{0,48},{8,56},{128,176},{136,184},{1,49},{9,57},{129,177},{137,185... | collective-permute-start | bytes 393224 | tf_op jit(solution)/shard_map/ppermute | solution.py:236
  17.5 2.8 %collective-permute-start.2 = (f32[8,4096]{1,0:T(8,128)S(1)}, f32[8,4096]{1,0:T(8,128)S(1)}, u32[]{:S(2)}, u32[]{:S(2)}) collective-permute-start(f32[8,4096]{1,0:T(8,128)S(1)} %collective-permute-done.1), channel_id=1, source_target_pairs={{80,64},{88,72},{208,192},{216,200},{81,65},{89,73},{209,193},{217... | collective-permute-start | bytes 393224 | tf_op jit(solution)/shard_map/ppermute | solution.py:241
  20.4 6.6 %collective-permute-start.9 = (f32[8,4096]{1,0:T(8,128)S(1)}, f32[8,4096]{1,0:T(8,128)S(1)}, u32[]{:S(2)}, u32[]{:S(2)}) collective-permute-start(f32[8,4096]{1,0:T(8,128)S(1)} %select_select_fusion.refs_0_.refs_8_), channel_id=1, source_target_pairs={{0,128},{8,136},{16,144},{24,152},{32,160},{40,168},{48,176},{56,1... | collective-permute-start | bytes 393224 | tf_op jit(solution)/shard_map/ppermute | solution.py:249
  21.6 6.4 %collective-permute-start.8 = (f32[8,4096]{1,0:T(8,128)S(1)}, f32[8,4096]{1,0:T(8,128)S(1)}, u32[]{:S(2)}, u32[]{:S(2)}) collective-permute-start(f32[8,4096]{1,0:T(8,128)S(1)} %select_select_fusion.refs_0_.refs_8_), channel_id=1, source_target_pairs={{0,8},{8,0},{16,24},{24,16},{32,40},{40,32},{48,56},{56,48},{64,72... | collective-permute-start | bytes 393224 | tf_op jit(solution)/shard_map/ppermute | solution.py:251
  27.0 1.3 %collective-permute-start.10 = (f32[8,4096]{1,0:T(8,128)S(1)}, f32[8,4096]{1,0:T(8,128)S(1)}, u32[]{:S(2)}, u32[]{:S(2)}) collective-permute-start(f32[8,4096]{1,0:T(8,128)S(1)} %collective-permute-done.9.refs_1_.refs_9_), channel_id=1, source_target_pairs={{0,8},{8,0},{16,24},{24,16},{32,40},{40,32},{48,56},{56,48},{64,72... | collective-permute-start | bytes 393224 | tf_op jit(solution)/shard_map/ppermute | solution.py:251
  29.3 8.0 %collective-permute-start.12 = (f32[2,8,2,8,128]{4,3,2,1,0:T(8,128)S(1)}, f32[2,8,2,8,128]{4,3,2,1,0:T(8,128)S(1)}, u32[]{:S(2)}, u32[]{:S(2)}) collective-permute-start(f32[2,8,2,8,128]{4,3,2,1,0:T(8,128)S(1)} %get-tuple-element.47), channel_id=1, source_target_pairs={{0,2},{1,3},{2,0},{3,1},{4,6},{5,7},{6,4},{7,5},{8,10},{9,11},{10,... | collective-permute-start | bytes 393224 | tf_op jit(solution)/shard_map/ppermute | solution.py:258
  32.6 11.6 %collective-permute-start.11 = (f32[2,8,2,8,128]{4,3,2,1,0:T(8,128)S(1)}, f32[2,8,2,8,128]{4,3,2,1,0:T(8,128)S(1)}, u32[]{:S(2)}, u32[]{:S(2)}) collective-permute-start(f32[2,8,2,8,128]{4,3,2,1,0:T(8,128)S(1)} %get-tuple-element.46), channel_id=1, source_target_pairs={{0,1},{1,0},{2,3},{3,2},{4,5},{5,4},{6,7},{7,6},{8,9},{9,8},{10,11... | collective-permute-start | bytes 393224 | tf_op jit(solution)/shard_map/ppermute | solution.py:258
  33.2 10.9 %collective-permute-start.13 = (f32[2,8,2,8,128]{4,3,2,1,0:T(8,128)S(1)}, f32[2,8,2,8,128]{4,3,2,1,0:T(8,128)S(1)}, u32[]{:S(2)}, u32[]{:S(2)}) collective-permute-start(f32[2,8,2,8,128]{4,3,2,1,0:T(8,128)S(1)} %get-tuple-element.49), channel_id=1, source_target_pairs={{0,3},{1,2},{2,1},{3,0},{4,7},{5,6},{6,5},{7,4},{8,11},{9,10},{10,... | collective-permute-start | bytes 393224 | tf_op jit(solution)/shard_map/ppermute | solution.py:258
  33.6 10.6 %collective-permute-start.14 = (f32[2,8,2,8,128]{4,3,2,1,0:T(8,128)S(1)}, f32[2,8,2,8,128]{4,3,2,1,0:T(8,128)S(1)}, u32[]{:S(2)}, u32[]{:S(2)}) collective-permute-start(f32[2,8,2,8,128]{4,3,2,1,0:T(8,128)S(1)} %get-tuple-element.50), channel_id=1, source_target_pairs={{0,4},{1,5},{2,6},{3,7},{4,0},{5,1},{6,2},{7,3},{8,12},{9,13},{10,... | collective-permute-start | bytes 393224 | tf_op jit(solution)/shard_map/ppermute | solution.py:258
  34.4 9.7 %collective-permute-start.15 = (f32[2,8,2,8,128]{4,3,2,1,0:T(8,128)S(1)}, f32[2,8,2,8,128]{4,3,2,1,0:T(8,128)S(1)}, u32[]{:S(2)}, u32[]{:S(2)}) collective-permute-start(f32[2,8,2,8,128]{4,3,2,1,0:T(8,128)S(1)} %get-tuple-element.51), channel_id=1, source_target_pairs={{0,5},{1,4},{2,7},{3,6},{4,1},{5,0},{6,3},{7,2},{8,13},{9,12},{10,... | collective-permute-start | bytes 393224 | tf_op jit(solution)/shard_map/ppermute | solution.py:258
  37.2 10.5 %collective-permute-start.16 = (f32[2,8,2,8,128]{4,3,2,1,0:T(8,128)S(1)}, f32[2,8,2,8,128]{4,3,2,1,0:T(8,128)S(1)}, u32[]{:S(2)}, u32[]{:S(2)}) collective-permute-start(f32[2,8,2,8,128]{4,3,2,1,0:T(8,128)S(1)} %get-tuple-element.52), channel_id=1, source_target_pairs={{0,6},{1,7},{2,4},{3,5},{4,2},{5,3},{6,0},{7,1},{8,14},{9,15},{10,... | collective-permute-start | bytes 393224 | tf_op jit(solution)/shard_map/ppermute | solution.py:258
  44.1 7.1 %collective-permute-start.17 = (f32[2,8,2,8,128]{4,3,2,1,0:T(8,128)S(1)}, f32[2,8,2,8,128]{4,3,2,1,0:T(8,128)S(1)}, u32[]{:S(2)}, u32[]{:S(2)}) collective-permute-start(f32[2,8,2,8,128]{4,3,2,1,0:T(8,128)S(1)} %get-tuple-element.53), channel_id=1, source_target_pairs={{0,7},{1,6},{2,5},{3,4},{4,3},{5,2},{6,1},{7,0},{8,15},{9,14},{10,... | collective-permute-start | bytes 393224 | tf_op jit(solution)/shard_map/ppermute | solution.py:258
  52.3 7.6 %collective-permute-start.19 = (f32[2,8,2,8,128]{4,3,2,1,0:T(8,128)S(1)}, f32[2,8,2,8,128]{4,3,2,1,0:T(8,128)S(1)}, u32[]{:S(2)}, u32[]{:S(2)}) collective-permute-start(f32[2,8,2,8,128]{4,3,2,1,0:T(8,128)S(1)} %bitcast.35), channel_id=1, source_target_pairs={{0,2},{1,3},{2,0},{3,1},{4,6},{5,7},{6,4},{7,5},{8,10},{9,11},{10,... | collective-permute-start | bytes 393224 | tf_op jit(solution)/shard_map/ppermute | solution.py:258
  52.4 8.3 %collective-permute-start.18 = (f32[2,8,2,8,128]{4,3,2,1,0:T(8,128)S(1)}, f32[2,8,2,8,128]{4,3,2,1,0:T(8,128)S(1)}, u32[]{:S(2)}, u32[]{:S(2)}) collective-permute-start(f32[2,8,2,8,128]{4,3,2,1,0:T(8,128)S(1)} %bitcast.34), channel_id=1, source_target_pairs={{0,1},{1,0},{2,3},{3,2},{4,5},{5,4},{6,7},{7,6},{8,9},{9,8},{10,11... | collective-permute-start | bytes 393224 | tf_op jit(solution)/shard_map/ppermute | solution.py:258
  52.6 11.9 %collective-permute-start.20 = (f32[2,8,2,8,128]{4,3,2,1,0:T(8,128)S(1)}, f32[2,8,2,8,128]{4,3,2,1,0:T(8,128)S(1)}, u32[]{:S(2)}, u32[]{:S(2)}) collective-permute-start(f32[2,8,2,8,128]{4,3,2,1,0:T(8,128)S(1)} %bitcast.33), channel_id=1, source_target_pairs={{0,3},{1,2},{2,1},{3,0},{4,7},{5,6},{6,5},{7,4},{8,11},{9,10},{10,... | collective-permute-start | bytes 393224 | tf_op jit(solution)/shard_map/ppermute | solution.py:258
  56.5 8.0 %collective-permute-start.21 = (f32[2,8,2,8,128]{4,3,2,1,0:T(8,128)S(1)}, f32[2,8,2,8,128]{4,3,2,1,0:T(8,128)S(1)}, u32[]{:S(2)}, u32[]{:S(2)}) collective-permute-start(f32[2,8,2,8,128]{4,3,2,1,0:T(8,128)S(1)} %bitcast.32), channel_id=1, source_target_pairs={{0,4},{1,5},{2,6},{3,7},{4,0},{5,1},{6,2},{7,3},{8,12},{9,13},{10,... | collective-permute-start | bytes 393224 | tf_op jit(solution)/shard_map/ppermute | solution.py:258
  57.3 7.2 %collective-permute-start.22 = (f32[2,8,2,8,128]{4,3,2,1,0:T(8,128)S(1)}, f32[2,8,2,8,128]{4,3,2,1,0:T(8,128)S(1)}, u32[]{:S(2)}, u32[]{:S(2)}) collective-permute-start(f32[2,8,2,8,128]{4,3,2,1,0:T(8,128)S(1)} %bitcast.31), channel_id=1, source_target_pairs={{0,5},{1,4},{2,7},{3,6},{4,1},{5,0},{6,3},{7,2},{8,13},{9,12},{10,... | collective-permute-start | bytes 393224 | tf_op jit(solution)/shard_map/ppermute | solution.py:258
  59.9 8.2 %collective-permute-start.23 = (f32[2,8,2,8,128]{4,3,2,1,0:T(8,128)S(1)}, f32[2,8,2,8,128]{4,3,2,1,0:T(8,128)S(1)}, u32[]{:S(2)}, u32[]{:S(2)}) collective-permute-start(f32[2,8,2,8,128]{4,3,2,1,0:T(8,128)S(1)} %bitcast.30), channel_id=1, source_target_pairs={{0,6},{1,7},{2,4},{3,5},{4,2},{5,3},{6,0},{7,1},{8,14},{9,15},{10,... | collective-permute-start | bytes 393224 | tf_op jit(solution)/shard_map/ppermute | solution.py:258
  60.7 8.0 %collective-permute-start.24 = (f32[2,8,2,8,128]{4,3,2,1,0:T(8,128)S(1)}, f32[2,8,2,8,128]{4,3,2,1,0:T(8,128)S(1)}, u32[]{:S(2)}, u32[]{:S(2)}) collective-permute-start(f32[2,8,2,8,128]{4,3,2,1,0:T(8,128)S(1)} %bitcast.29), channel_id=1, source_target_pairs={{0,7},{1,6},{2,5},{3,4},{4,3},{5,2},{6,1},{7,0},{8,15},{9,14},{10,... | collective-permute-start | bytes 393224 | tf_op jit(solution)/shard_map/ppermute | solution.py:258

commit v4 on v3

--- a/solution.py
+++ b/solution.py
@@ -15,7 +15,7 @@
 LANES = 128
 
 
-ORDER = (2, 6, 4, 7, 5, 3, 1)
+ORDER = (6, 2, 3, 5, 1, 7, 4)
 REACH = (5, 3, 6, 2, 7, 1)
 
 
@@ -244,25 +244,32 @@
     first = root
     for step, value in arrived.items():
         first = jnp.where(z == step, value, first)
-    index, mixed, first = indices_after(first, here)
-    tables = right_table(index, -1.0), left_table(mixed, index, -1.0)
+    index, sent, _, first = indices_after(first, here)
+    tables = right_table(index, -1.0), left_table(sent, index, -1.0)
     second = lax.ppermute(first, "band", [(b, b ^ 16) for b in range(32)])
     own = (first, second)
     other = tuple(lax.ppermute(a, "band", [(b, b ^ 1) for b in range(32)]) for a in own)
     return own, other, tables
 
 
+def partner(p, block, sign):
+    return (p // 4 ^ block // 4) * 4 + (p + sign * block) % 4
+
+
 def exchange(blocks):
     results = list(blocks)
     for d in ORDER:
-        results[d] = lax.ppermute(blocks[d], "fft", [(p, p ^ d) for p in range(8)])
+        pairs = [(p, partner(p, d, 1)) for p in range(8)]
+        results[d] = lax.ppermute(blocks[d], "fft", pairs)
     return results
 
 
 def indices_after(value, here):
     index, value = lax.optimization_barrier((jnp.arange(GRID, dtype=jnp.int32), value))
-    mixed = (index // PLANES ^ here) * PLANES + index % PLANES
-    return index, mixed, value
+    sent, received = (
+        partner(here, index // PLANES, sign) * PLANES + index % PLANES for sign in (1, -1)
+    )
+    return index, sent, received, value
 
 
 def apply_exchange(orbitals):
@@ -275,19 +282,19 @@
     spectrum = forward_call(0, [], orbitals, *own, right, left)
     spectrum = forward_call(1, spectrum, orbitals, *other, right, left)
     spectrum = exchange(spectrum)
-    index, mixed, spectrum[ORDER[0]] = indices_after(spectrum[ORDER[0]], here)
+    index, sent, received, spectrum[ORDER[0]] = indices_after(spectrum[ORDER[0]], here)
     spectrum = [a.reshape(flat) for a in spectrum]
     filtered = local_call(middle_kernel, [flat] * 8, [])(
         *spectrum,
-        left_table(index, mixed, -1.0),
-        left_table(mixed, index, 1.0),
+        left_table(index, received, -1.0),
+        left_table(sent, index, 1.0),
         filter_table(index, here),
     )
     returned = exchange([a.reshape(block) for a in filtered])
-    index, mixed, returned[ORDER[0]] = indices_after(returned[ORDER[0]], here)
+    index, _, received, returned[ORDER[0]] = indices_after(returned[ORDER[0]], here)
     total = pltpu.VMEM((rows, LANES), jnp.float32)
     return local_call(inverse_kernel, [(2, PLANES, GRID * GRID)], [work, total])(
-        *returned, *own, *other, right_table(index, 1.0), left_table(index, mixed, 1.0)
+        *returned, *own, *other, right_table(index, 1.0), left_table(index, received, 1.0)
     )[0]
 
 

time: 70.7 us -> 67.9 us (0.960)
  waiting for transfers between devices: 30.7 us -> 24.3 us
  starting transfers between devices: 31.1 us -> 34.7 us
    ppermute x14, waiting for transfers between devices: 16.4 us -> 10 us  [exchange(): results[d] = lax.ppermute(blocks[d], 'fft', pairs)]
    ppermute x14, starting transfers between devices: 20.2 us -> 23.8 us  [exchange(): results[d] = lax.ppermute(blocks[d], 'fft', pairs)]
  transfers between devices with their start and end apart: 25 -> 25, of which waited for: 12 -> 14; matrix products, arithmetic and copies ran while one was open for 3% -> 4% of each run, Pallas kernels for 1% -> 1%
where the time goes in v4:
time: 67.9 us; the launch traced here: 67.7 us
  starting transfers between devices  34.7 us (51%)
  waiting for transfers between devices  24.3 us (36%)
  Pallas kernels  4.75 us (7%)
  other arithmetic  2.5 us (4%)
  local copies, waits for them, and re-layouts  1 us (1%)
    ppermute x14, starting transfers between devices, exchange(): results[d] = lax.ppermute(blocks[d], 'fft', pairs)  23.8 us
    ppermute x14, waiting for transfers between devices, exchange(): results[d] = lax.ppermute(blocks[d], 'fft', pairs)  10 us
    ppermute x6, starting transfers between devices, fetch_sources(): lax.ppermute(root, 'band', [(band_of(h, 0, c), band_of(h, step, c)) for h...  7.78 us
    ppermute x1, waiting for transfers between devices, fetch_sources(): lax.ppermute(orbitals[1], 'band', [(band_of(0, 0, c), band_of(1, 0, c)) f...  7.32 us
    ppermute x1, waiting for transfers between devices, fetch_sources(): second = lax.ppermute(first, 'band', [(b, b ^ 16) for b in range(32)])  4.56 us
    ppermute x6, waiting for transfers between devices, fetch_sources(): lax.ppermute(root, 'band', [(band_of(h, 0, c), band_of(h, step, c)) for h...  2.1 us
    pallas_call x2, Pallas kernels, forward_call(): pl.pallas_call(forward_kernel, grid=(1,), in_specs=[whole] * len(operands...  1.91 us
    pallas_call x1, Pallas kernels, apply_exchange(): local_call(inverse_kernel, [(2, PLANES, GRID * GRID)], [work, total])  1.76 us
  transfers between devices with their start and end apart: 25, of which 14 were waited for; matrix products, arithmetic and copies ran while one was open for 4% of the time, Pallas kernels for 1%

profile of v4, /device:TPU:6, one launch (start us, length us, event | category | flops | bytes accessed | tf_op | source)
XLA Modules:
  0.0 67.7 jit_solution(17461600838639174813)
XLA Ops:
  0.0 1.0 %slice_bitcast_fusion = f32[8,4096]{1,0:T(8,128)S(1)} fusion(f32[2,8,4096]{2,1,0:T(8,128)} %orb_ref.3), kind=kLoop, calls=%fused_computation.49 | loop fusion | bytes 262144 | tf_op jit(solution)/shard_map/squeeze | solution.py:232
  1.0 1.3 %collective-permute-start = (f32[8,4096]{1,0:T(8,128)S(1)}, f32[8,4096]{1,0:T(8,128)S(1)}, u32[]{:S(2)}, u32[]{:S(2)}) collective-permute-start(f32[8,4096]{1,0:T(8,128)S(1)} %slice_bitcast_fusion), channel_id=1, source_target_pairs={{0,128},{8,136},{1,129},{9,137},{2,130},{10,138},{3,131},{11,139},... | collective-permute-start | bytes 393224 | tf_op jit(solution)/shard_map/ppermute | solution.py:231
  2.3 7.3 %collective-permute-done = f32[8,4096]{1,0:T(8,128)S(1)} collective-permute-done((f32[8,4096]{1,0:T(8,128)S(1)}, f32[8,4096]{1,0:T(8,128)S(1)}, u32[]{:S(2)}, u32[]{:S(2)}) %collective-permute-start) | collective-permute-done | bytes 131104 | tf_op jit(solution)/shard_map/ppermute | solution.py:231
  9.6 1.3 %collective-permute-start.1 = (f32[8,4096]{1,0:T(8,128)S(1)}, f32[8,4096]{1,0:T(8,128)S(1)}, u32[]{:S(2)}, u32[]{:S(2)}) collective-permute-start(f32[8,4096]{1,0:T(8,128)S(1)} %bitcast_select_fusion), channel_id=1, source_target_pairs={{0,80},{8,88},{128,208},{136,216},{1,81},{9,89},{129,209},{137,217... | collective-permute-start | bytes 393224 | tf_op jit(solution)/shard_map/ppermute | solution.py:236
  11.0 1.3 %collective-permute-start.3 = (f32[8,4096]{1,0:T(8,128)S(1)}, f32[8,4096]{1,0:T(8,128)S(1)}, u32[]{:S(2)}, u32[]{:S(2)}) collective-permute-start(f32[8,4096]{1,0:T(8,128)S(1)} %bitcast_select_fusion), channel_id=1, source_target_pairs={{0,16},{8,24},{128,144},{136,152},{1,17},{9,25},{129,145},{137,153... | collective-permute-start | bytes 393224 | tf_op jit(solution)/shard_map/ppermute | solution.py:236
  12.3 1.3 %collective-permute-start.4 = (f32[8,4096]{1,0:T(8,128)S(1)}, f32[8,4096]{1,0:T(8,128)S(1)}, u32[]{:S(2)}, u32[]{:S(2)}) collective-permute-start(f32[8,4096]{1,0:T(8,128)S(1)} %bitcast_select_fusion), channel_id=1, source_target_pairs={{0,112},{8,120},{128,240},{136,248},{1,113},{9,121},{129,241},{137... | collective-permute-start | bytes 393224 | tf_op jit(solution)/shard_map/ppermute | solution.py:236
  13.6 1.3 %collective-permute-start.5 = (f32[8,4096]{1,0:T(8,128)S(1)}, f32[8,4096]{1,0:T(8,128)S(1)}, u32[]{:S(2)}, u32[]{:S(2)}) collective-permute-start(f32[8,4096]{1,0:T(8,128)S(1)} %bitcast_select_fusion), channel_id=1, source_target_pairs={{0,32},{8,40},{128,160},{136,168},{1,33},{9,41},{129,161},{137,169... | collective-permute-start | bytes 393224 | tf_op jit(solution)/shard_map/ppermute | solution.py:236
  14.9 1.3 %collective-permute-start.6 = (f32[8,4096]{1,0:T(8,128)S(1)}, f32[8,4096]{1,0:T(8,128)S(1)}, u32[]{:S(2)}, u32[]{:S(2)}) collective-permute-start(f32[8,4096]{1,0:T(8,128)S(1)} %bitcast_select_fusion), channel_id=1, source_target_pairs={{0,96},{8,104},{128,224},{136,232},{1,97},{9,105},{129,225},{137,2... | collective-permute-start | bytes 393224 | tf_op jit(solution)/shard_map/ppermute | solution.py:236
  16.2 0.0 collective-permute-done.1
  16.2 1.3 %collective-permute-start.7 = (f32[8,4096]{1,0:T(8,128)S(1)}, f32[8,4096]{1,0:T(8,128)S(1)}, u32[]{:S(2)}, u32[]{:S(2)}) collective-permute-start(f32[8,4096]{1,0:T(8,128)S(1)} %bitcast_select_fusion), channel_id=1, source_target_pairs={{0,48},{8,56},{128,176},{136,184},{1,49},{9,57},{129,177},{137,185... | collective-permute-start | bytes 393224 | tf_op jit(solution)/shard_map/ppermute | solution.py:236
  17.5 0.0 collective-permute-done.3
  17.5 0.7 collective-permute-start.2
  18.2 0.0 collective-permute-done.4
  18.2 0.0 collective-permute-done.5
  18.3 0.8 %collective-permute-done.6 = f32[8,4096]{1,0:T(8,128)S(1)} collective-permute-done((f32[8,4096]{1,0:T(8,128)S(1)}, f32[8,4096]{1,0:T(8,128)S(1)}, u32[]{:S(2)}, u32[]{:S(2)}) %collective-permute-start.6) | collective-permute-done | bytes 131104 | tf_op jit(solution)/shard_map/ppermute | solution.py:236
  19.0 1.3 %collective-permute-done.7 = f32[8,4096]{1,0:T(8,128)S(1)} collective-permute-done((f32[8,4096]{1,0:T(8,128)S(1)}, f32[8,4096]{1,0:T(8,128)S(1)}, u32[]{:S(2)}, u32[]{:S(2)}) %collective-permute-start.7) | collective-permute-done | bytes 131104 | tf_op jit(solution)/shard_map/ppermute | solution.py:236
  20.3 0.0 collective-permute-done.2
  20.4 1.2 %collective-permute-start.9 = (f32[8,4096]{1,0:T(8,128)S(1)}, f32[8,4096]{1,0:T(8,128)S(1)}, u32[]{:S(2)}, u32[]{:S(2)}) collective-permute-start(f32[8,4096]{1,0:T(8,128)S(1)} %select_select_fusion.refs_0_.refs_8_), channel_id=1, source_target_pairs={{0,128},{8,136},{16,144},{24,152},{32,160},{40,168},{48,176},{56,1... | collective-permute-start | bytes 393224 | tf_op jit(solution)/shard_map/ppermute | solution.py:249
  21.6 0.0 collective-permute-start.8
  21.6 0.3 fusion.58
  22.0 0.1 reduce-precision_convert_fusion.1
  22.1 0.1 reduce-precision_convert_fusion.5
  22.2 0.2 fusion.7
  22.4 4.6 %collective-permute-done.9.refs_1_.refs_9_ = f32[8,4096]{1,0:T(8,128)S(1)} collective-permute-done((f32[8,4096]{1,0:T(8,128)S(1)}, f32[8,4096]{1,0:T(8,128)S(1)}, u32[]{:S(2)}, u32[]{:S(2)}) %collective-permute-start.9) | collective-permute-done | bytes 131104 | tf_op jit(solution)/shard_map/ppermute | solution.py:249
  27.0 0.0 collective-permute-start.10
  27.0 1.0 %shard_map.17 = (f32[2,8,2,8,128]{4,3,2,1,0:T(8,128)S(1)}, f32[2,8,2,8,128]{4,3,2,1,0:T(8,128)S(1)}, f32[2,8,2,8,128]{4,3,2,1,0:T(8,128)S(1)}, f32[2,8,2,8,128]{...) custom-call(f32[2,8,4096]{2,1,0:T(8,128)S(1)} %copy-done, ...), custom_call_target="tpu_custom_call" | custom-call | tf_op jit(solution)/shard_map/pallas_call | solution.py:208
  28.0 0.3 collective-permute-done.10.refs_1_.refs_11_
  28.3 1.0 %shard_map.18 = (f32[2,8,2,8,128]{4,3,2,1,0:T(8,128)S(1)}, f32[2,8,2,8,128]{4,3,2,1,0:T(8,128)S(1)}, f32[2,8,2,8,128]{4,3,2,1,0:T(8,128)S(1)}, f32[2,8,2,8,128]{...) custom-call(f32[2,8,4096]{2,1,0:T(8,128)S(1)} %copy-done, ...), custom_call_target="tpu_custom_call", output_to_operand_aliasing={{0}: (5, {}), {1}: (6, {}), {2}: (7, {}), {3}: (8, {}), {4}... | custom-call | tf_op jit(solution)/shard_map/pallas_call | solution.py:208
  29.3 3.5 %collective-permute-start.16 = (f32[2,8,2,8,128]{4,3,2,1,0:T(8,128)S(1)}, f32[2,8,2,8,128]{4,3,2,1,0:T(8,128)S(1)}, u32[]{:S(2)}, u32[]{:S(2)}) collective-permute-start(f32[2,8,2,8,128]{4,3,2,1,0:T(8,128)S(1)} %get-tuple-element.51), channel_id=1, source_target_pairs={{0,6},{1,7},{2,4},{3,5},{4,2},{5,3},{6,0},{7,1},{8,14},{9,15},{10,... | collective-permute-start | bytes 393224 | tf_op jit(solution)/shard_map/ppermute | solution.py:263
  32.8 0.7 %collective-permute-start.11 = (f32[2,8,2,8,128]{4,3,2,1,0:T(8,128)S(1)}, f32[2,8,2,8,128]{4,3,2,1,0:T(8,128)S(1)}, u32[]{:S(2)}, u32[]{:S(2)}) collective-permute-start(f32[2,8,2,8,128]{4,3,2,1,0:T(8,128)S(1)} %get-tuple-element.46), channel_id=1, source_target_pairs={{0,1},{1,2},{2,3},{3,0},{4,5},{5,6},{6,7},{7,4},{8,9},{9,10},{10,1... | collective-permute-start | bytes 393224 | tf_op jit(solution)/shard_map/ppermute | solution.py:263
  33.5 1.8 %collective-permute-start.12 = (f32[2,8,2,8,128]{4,3,2,1,0:T(8,128)S(1)}, f32[2,8,2,8,128]{4,3,2,1,0:T(8,128)S(1)}, u32[]{:S(2)}, u32[]{:S(2)}) collective-permute-start(f32[2,8,2,8,128]{4,3,2,1,0:T(8,128)S(1)} %get-tuple-element.47), channel_id=1, source_target_pairs={{0,2},{1,3},{2,0},{3,1},{4,6},{5,7},{6,4},{7,5},{8,10},{9,11},{10,... | collective-permute-start | bytes 393224 | tf_op jit(solution)/shard_map/ppermute | solution.py:263
  35.3 0.8 %collective-permute-start.13 = (f32[2,8,2,8,128]{4,3,2,1,0:T(8,128)S(1)}, f32[2,8,2,8,128]{4,3,2,1,0:T(8,128)S(1)}, u32[]{:S(2)}, u32[]{:S(2)}) collective-permute-start(f32[2,8,2,8,128]{4,3,2,1,0:T(8,128)S(1)} %get-tuple-element.48), channel_id=1, source_target_pairs={{0,3},{1,0},{2,1},{3,2},{4,7},{5,4},{6,5},{7,6},{8,11},{9,8},{10,9... | collective-permute-start | bytes 393224 | tf_op jit(solution)/shard_map/ppermute | solution.py:263
  36.2 1.2 %collective-permute-start.14 = (f32[2,8,2,8,128]{4,3,2,1,0:T(8,128)S(1)}, f32[2,8,2,8,128]{4,3,2,1,0:T(8,128)S(1)}, u32[]{:S(2)}, u32[]{:S(2)}) collective-permute-start(f32[2,8,2,8,128]{4,3,2,1,0:T(8,128)S(1)} %get-tuple-element.49), channel_id=1, source_target_pairs={{0,4},{1,5},{2,6},{3,7},{4,0},{5,1},{6,2},{7,3},{8,12},{9,13},{10,... | collective-permute-start | bytes 393224 | tf_op jit(solution)/shard_map/ppermute | solution.py:263
  37.4 0.2 collective-permute-done.16
  37.5 1.8 %collective-permute-start.15 = (f32[2,8,2,8,128]{4,3,2,1,0:T(8,128)S(1)}, f32[2,8,2,8,128]{4,3,2,1,0:T(8,128)S(1)}, u32[]{:S(2)}, u32[]{:S(2)}) collective-permute-start(f32[2,8,2,8,128]{4,3,2,1,0:T(8,128)S(1)} %get-tuple-element.50), channel_id=1, source_target_pairs={{0,5},{1,6},{2,7},{3,4},{4,1},{5,2},{6,3},{7,0},{8,13},{9,14},{10,... | collective-permute-start | bytes 393224 | tf_op jit(solution)/shard_map/ppermute | solution.py:263
  39.4 0.1 maximum_multiply_fusion
  39.4 0.1 broadcast_add_fusion
  39.5 0.2 fusion.3.refs_10_
  39.7 0.3 fusion.56
  40.1 0.1 reduce-precision_convert_fusion.3
  40.2 0.2 collective-permute-done.11
  40.4 2.3 %collective-permute-start.17 = (f32[2,8,2,8,128]{4,3,2,1,0:T(8,128)S(1)}, f32[2,8,2,8,128]{4,3,2,1,0:T(8,128)S(1)}, u32[]{:S(2)}, u32[]{:S(2)}) collective-permute-start(f32[2,8,2,8,128]{4,3,2,1,0:T(8,128)S(1)} %get-tuple-element.53), channel_id=1, source_target_pairs={{0,7},{1,4},{2,5},{3,6},{4,3},{5,0},{6,1},{7,2},{8,15},{9,12},{10,... | collective-permute-start | bytes 393224 | tf_op jit(solution)/shard_map/ppermute | solution.py:263
  42.7 2.1 %collective-permute-done.12 = f32[2,8,2,8,128]{4,3,2,1,0:T(8,128)S(1)} collective-permute-done((f32[2,8,2,8,128]{4,3,2,1,0:T(8,128)S(1)}, f32[2,8,2,8,128]{4,3,2,1,0:T(8,128)S(1)}, u32[]{:S(2)}, u32[]{:S(2)}) %collective-permute-start.12) | collective-permute-done | bytes 131104 | tf_op jit(solution)/shard_map/ppermute | solution.py:263
  44.8 0.0 collective-permute-done.14
  44.8 1.8 %collective-permute-done.15 = f32[2,8,2,8,128]{4,3,2,1,0:T(8,128)S(1)} collective-permute-done((f32[2,8,2,8,128]{4,3,2,1,0:T(8,128)S(1)}, f32[2,8,2,8,128]{4,3,2,1,0:T(8,128)S(1)}, u32[]{:S(2)}, u32[]{:S(2)}) %collective-permute-start.15) | collective-permute-done | bytes 131104 | tf_op jit(solution)/shard_map/ppermute | solution.py:263
  46.6 1.0 %collective-permute-done.17 = f32[2,8,2,8,128]{4,3,2,1,0:T(8,128)S(1)} collective-permute-done((f32[2,8,2,8,128]{4,3,2,1,0:T(8,128)S(1)}, f32[2,8,2,8,128]{4,3,2,1,0:T(8,128)S(1)}, u32[]{:S(2)}, u32[]{:S(2)}) %collective-permute-start.17) | collective-permute-done | bytes 131104 | tf_op jit(solution)/shard_map/ppermute | solution.py:263
  47.6 1.1 %shard_map.19 = (f32[256,128]{1,0:T(8,128)S(1)}, f32[256,128]{1,0:T(8,128)S(1)}, f32[256,128]{1,0:T(8,128)S(1)}, f32[256,128]{1,0:T(8,128)S(1)}, f32[256,128]{1,...) custom-call(f32[256,128]{1,0:T(8,128)S(1)} %bitcast.20, ...), custom_call_target="tpu_custom_call" | custom-call | tf_op jit(solution)/shard_map/pallas_call | solution.py:287
  48.6 2.7 %collective-permute-start.23 = (f32[2,8,2,8,128]{4,3,2,1,0:T(8,128)S(1)}, f32[2,8,2,8,128]{4,3,2,1,0:T(8,128)S(1)}, u32[]{:S(2)}, u32[]{:S(2)}) collective-permute-start(f32[2,8,2,8,128]{4,3,2,1,0:T(8,128)S(1)} %bitcast.35), channel_id=1, source_target_pairs={{0,6},{1,7},{2,4},{3,5},{4,2},{5,3},{6,0},{7,1},{8,14},{9,15},{10,... | collective-permute-start | bytes 393224 | tf_op jit(solution)/shard_map/ppermute | solution.py:263
  51.4 0.7 %collective-permute-start.18 = (f32[2,8,2,8,128]{4,3,2,1,0:T(8,128)S(1)}, f32[2,8,2,8,128]{4,3,2,1,0:T(8,128)S(1)}, u32[]{:S(2)}, u32[]{:S(2)}) collective-permute-start(f32[2,8,2,8,128]{4,3,2,1,0:T(8,128)S(1)} %bitcast.34), channel_id=1, source_target_pairs={{0,1},{1,2},{2,3},{3,0},{4,5},{5,6},{6,7},{7,4},{8,9},{9,10},{10,1... | collective-permute-start | bytes 393224 | tf_op jit(solution)/shard_map/ppermute | solution.py:263
  52.1 2.8 %collective-permute-start.19 = (f32[2,8,2,8,128]{4,3,2,1,0:T(8,128)S(1)}, f32[2,8,2,8,128]{4,3,2,1,0:T(8,128)S(1)}, u32[]{:S(2)}, u32[]{:S(2)}) collective-permute-start(f32[2,8,2,8,128]{4,3,2,1,0:T(8,128)S(1)} %bitcast.33), channel_id=1, source_target_pairs={{0,2},{1,3},{2,0},{3,1},{4,6},{5,7},{6,4},{7,5},{8,10},{9,11},{10,... | collective-permute-start | bytes 393224 | tf_op jit(solution)/shard_map/ppermute | solution.py:263
  54.9 0.5 collective-permute-start.20
  55.4 1.0 %collective-permute-start.21 = (f32[2,8,2,8,128]{4,3,2,1,0:T(8,128)S(1)}, f32[2,8,2,8,128]{4,3,2,1,0:T(8,128)S(1)}, u32[]{:S(2)}, u32[]{:S(2)}) collective-permute-start(f32[2,8,2,8,128]{4,3,2,1,0:T(8,128)S(1)} %bitcast.31), channel_id=1, source_target_pairs={{0,4},{1,5},{2,6},{3,7},{4,0},{5,1},{6,2},{7,3},{8,12},{9,13},{10,... | collective-permute-start | bytes 393224 | tf_op jit(solution)/shard_map/ppermute | solution.py:263
  56.3 0.0 collective-permute-done.23.refs_6_
  56.3 2.6 %collective-permute-start.22 = (f32[2,8,2,8,128]{4,3,2,1,0:T(8,128)S(1)}, f32[2,8,2,8,128]{4,3,2,1,0:T(8,128)S(1)}, u32[]{:S(2)}, u32[]{:S(2)}) collective-permute-start(f32[2,8,2,8,128]{4,3,2,1,0:T(8,128)S(1)} %bitcast.30), channel_id=1, source_target_pairs={{0,5},{1,6},{2,7},{3,4},{4,1},{5,2},{6,3},{7,0},{8,13},{9,14},{10,... | collective-permute-start | bytes 393224 | tf_op jit(solution)/shard_map/ppermute | solution.py:263
  59.0 0.3 fusion.57
  59.3 0.1 reduce-precision_convert_fusion
  59.5 0.1 reduce-precision_convert_fusion.2
  59.6 0.2 fusion.8
  59.7 0.3 collective-permute-done.18.refs_1_
  60.0 1.3 %collective-permute-start.24 = (f32[2,8,2,8,128]{4,3,2,1,0:T(8,128)S(1)}, f32[2,8,2,8,128]{4,3,2,1,0:T(8,128)S(1)}, u32[]{:S(2)}, u32[]{:S(2)}) collective-permute-start(f32[2,8,2,8,128]{4,3,2,1,0:T(8,128)S(1)} %bitcast.29), channel_id=1, source_target_pairs={{0,7},{1,4},{2,5},{3,6},{4,3},{5,0},{6,1},{7,2},{8,15},{9,12},{10,... | collective-permute-start | bytes 393224 | tf_op jit(solution)/shard_map/ppermute | solution.py:263
  61.4 2.1 %collective-permute-done.19.refs_2_ = f32[2,8,2,8,128]{4,3,2,1,0:T(8,128)S(1)} collective-permute-done((f32[2,8,2,8,128]{4,3,2,1,0:T(8,128)S(1)}, f32[2,8,2,8,128]{4,3,2,1,0:T(8,128)S(1)}, u32[]{:S(2)}, u32[]{:S(2)}) %collective-permute-start.19) | collective-permute-done | bytes 131104 | tf_op jit(solution)/shard_map/ppermute | solution.py:263
  63.5 0.8 %collective-permute-done.22.refs_5_ = f32[2,8,2,8,128]{4,3,2,1,0:T(8,128)S(1)} collective-permute-done((f32[2,8,2,8,128]{4,3,2,1,0:T(8,128)S(1)}, f32[2,8,2,8,128]{4,3,2,1,0:T(8,128)S(1)}, u32[]{:S(2)}, u32[]{:S(2)}) %collective-permute-start.22) | collective-permute-done | bytes 131104 | tf_op jit(solution)/shard_map/ppermute | solution.py:263
  64.3 1.6 %collective-permute-done.24.refs_7_ = f32[2,8,2,8,128]{4,3,2,1,0:T(8,128)S(1)} collective-permute-done((f32[2,8,2,8,128]{4,3,2,1,0:T(8,128)S(1)}, f32[2,8,2,8,128]{4,3,2,1,0:T(8,128)S(1)}, u32[]{:S(2)}, u32[]{:S(2)}) %collective-permute-start.24) | collective-permute-done | bytes 131104 | tf_op jit(solution)/shard_map/ppermute | solution.py:263
  65.9 1.8 %shard_map.20 = f32[2,8,4096]{2,1,0:T(8,128)} custom-call(f32[2,8,2,8,128]{4,3,2,1,0:T(8,128)S(1)} %bitcast.25, f32[2,8,2,8,128]{4,3,2,1,0:T(8,128)S(1)} %collective-permute-done.18.refs_1_, f32[2,8,2,8,128]{4,3,2,1,0:T(8,128)S(1)} %collective-permute-done.19.refs_2_, f32[2,8,2,8,128]{4,3,2,1,0:T(8,128)S(1)} %collective-permute-done.20.refs_3_, ...), custom_call_target="tpu_custom_call" | custom-call | tf_op jit(solution)/shard_map/pallas_call | solution.py:296
  (24 shorter events, 0.3 us)
Async XLA Ops:
  0.0 9.6 %copy-start = (f32[2,8,4096]{2,1,0:T(8,128)S(1)}, f32[2,8,4096]{2,1,0:T(8,128)}, u32[]{:S(2)}) copy-start(f32[2,8,4096]{2,1,0:T(8,128)} %orb_ref.3) | copy-start | bytes 786436
  1.0 8.6 %collective-permute-start = (f32[8,4096]{1,0:T(8,128)S(1)}, f32[8,4096]{1,0:T(8,128)S(1)}, u32[]{:S(2)}, u32[]{:S(2)}) collective-permute-start(f32[8,4096]{1,0:T(8,128)S(1)} %slice_bitcast_fusion), channel_id=1, source_target_pairs={{0,128},{8,136},{1,129},{9,137},{2,130},{10,138},{3,131},{11,139},... | collective-permute-start | bytes 393224 | tf_op jit(solution)/shard_map/ppermute | solution.py:231
  9.6 6.5 %collective-permute-start.1 = (f32[8,4096]{1,0:T(8,128)S(1)}, f32[8,4096]{1,0:T(8,128)S(1)}, u32[]{:S(2)}, u32[]{:S(2)}) collective-permute-start(f32[8,4096]{1,0:T(8,128)S(1)} %bitcast_select_fusion), channel_id=1, source_target_pairs={{0,80},{8,88},{128,208},{136,216},{1,81},{9,89},{129,209},{137,217... | collective-permute-start | bytes 393224 | tf_op jit(solution)/shard_map/ppermute | solution.py:236
  11.0 6.5 %collective-permute-start.3 = (f32[8,4096]{1,0:T(8,128)S(1)}, f32[8,4096]{1,0:T(8,128)S(1)}, u32[]{:S(2)}, u32[]{:S(2)}) collective-permute-start(f32[8,4096]{1,0:T(8,128)S(1)} %bitcast_select_fusion), channel_id=1, source_target_pairs={{0,16},{8,24},{128,144},{136,152},{1,17},{9,25},{129,145},{137,153... | collective-permute-start | bytes 393224 | tf_op jit(solution)/shard_map/ppermute | solution.py:236
  12.3 6.0 %collective-permute-start.4 = (f32[8,4096]{1,0:T(8,128)S(1)}, f32[8,4096]{1,0:T(8,128)S(1)}, u32[]{:S(2)}, u32[]{:S(2)}) collective-permute-start(f32[8,4096]{1,0:T(8,128)S(1)} %bitcast_select_fusion), channel_id=1, source_target_pairs={{0,112},{8,120},{128,240},{136,248},{1,113},{9,121},{129,241},{137... | collective-permute-start | bytes 393224 | tf_op jit(solution)/shard_map/ppermute | solution.py:236
  13.6 4.7 %collective-permute-start.5 = (f32[8,4096]{1,0:T(8,128)S(1)}, f32[8,4096]{1,0:T(8,128)S(1)}, u32[]{:S(2)}, u32[]{:S(2)}) collective-permute-start(f32[8,4096]{1,0:T(8,128)S(1)} %bitcast_select_fusion), channel_id=1, source_target_pairs={{0,32},{8,40},{128,160},{136,168},{1,33},{9,41},{129,161},{137,169... | collective-permute-start | bytes 393224 | tf_op jit(solution)/shard_map/ppermute | solution.py:236
  14.9 4.2 %collective-permute-start.6 = (f32[8,4096]{1,0:T(8,128)S(1)}, f32[8,4096]{1,0:T(8,128)S(1)}, u32[]{:S(2)}, u32[]{:S(2)}) collective-permute-start(f32[8,4096]{1,0:T(8,128)S(1)} %bitcast_select_fusion), channel_id=1, source_target_pairs={{0,96},{8,104},{128,224},{136,232},{1,97},{9,105},{129,225},{137,2... | collective-permute-start | bytes 393224 | tf_op jit(solution)/shard_map/ppermute | solution.py:236
  16.2 4.2 %collective-permute-start.7 = (f32[8,4096]{1,0:T(8,128)S(1)}, f32[8,4096]{1,0:T(8,128)S(1)}, u32[]{:S(2)}, u32[]{:S(2)}) collective-permute-start(f32[8,4096]{1,0:T(8,128)S(1)} %bitcast_select_fusion), channel_id=1, source_target_pairs={{0,48},{8,56},{128,176},{136,184},{1,49},{9,57},{129,177},{137,185... | collective-permute-start | bytes 393224 | tf_op jit(solution)/shard_map/ppermute | solution.py:236
  17.5 2.8 %collective-permute-start.2 = (f32[8,4096]{1,0:T(8,128)S(1)}, f32[8,4096]{1,0:T(8,128)S(1)}, u32[]{:S(2)}, u32[]{:S(2)}) collective-permute-start(f32[8,4096]{1,0:T(8,128)S(1)} %collective-permute-done.1), channel_id=1, source_target_pairs={{80,64},{88,72},{208,192},{216,200},{81,65},{89,73},{209,193},{217... | collective-permute-start | bytes 393224 | tf_op jit(solution)/shard_map/ppermute | solution.py:241
  20.4 6.6 %collective-permute-start.9 = (f32[8,4096]{1,0:T(8,128)S(1)}, f32[8,4096]{1,0:T(8,128)S(1)}, u32[]{:S(2)}, u32[]{:S(2)}) collective-permute-start(f32[8,4096]{1,0:T(8,128)S(1)} %select_select_fusion.refs_0_.refs_8_), channel_id=1, source_target_pairs={{0,128},{8,136},{16,144},{24,152},{32,160},{40,168},{48,176},{56,1... | collective-permute-start | bytes 393224 | tf_op jit(solution)/shard_map/ppermute | solution.py:249
  21.6 6.4 %collective-permute-start.8 = (f32[8,4096]{1,0:T(8,128)S(1)}, f32[8,4096]{1,0:T(8,128)S(1)}, u32[]{:S(2)}, u32[]{:S(2)}) collective-permute-start(f32[8,4096]{1,0:T(8,128)S(1)} %select_select_fusion.refs_0_.refs_8_), channel_id=1, source_target_pairs={{0,8},{8,0},{16,24},{24,16},{32,40},{40,32},{48,56},{56,48},{64,72... | collective-permute-start | bytes 393224 | tf_op jit(solution)/shard_map/ppermute | solution.py:251
  27.0 1.3 %collective-permute-start.10 = (f32[8,4096]{1,0:T(8,128)S(1)}, f32[8,4096]{1,0:T(8,128)S(1)}, u32[]{:S(2)}, u32[]{:S(2)}) collective-permute-start(f32[8,4096]{1,0:T(8,128)S(1)} %collective-permute-done.9.refs_1_.refs_9_), channel_id=1, source_target_pairs={{0,8},{8,0},{16,24},{24,16},{32,40},{40,32},{48,56},{56,48},{64,72... | collective-permute-start | bytes 393224 | tf_op jit(solution)/shard_map/ppermute | solution.py:251
  29.3 8.3 %collective-permute-start.16 = (f32[2,8,2,8,128]{4,3,2,1,0:T(8,128)S(1)}, f32[2,8,2,8,128]{4,3,2,1,0:T(8,128)S(1)}, u32[]{:S(2)}, u32[]{:S(2)}) collective-permute-start(f32[2,8,2,8,128]{4,3,2,1,0:T(8,128)S(1)} %get-tuple-element.51), channel_id=1, source_target_pairs={{0,6},{1,7},{2,4},{3,5},{4,2},{5,3},{6,0},{7,1},{8,14},{9,15},{10,... | collective-permute-start | bytes 393224 | tf_op jit(solution)/shard_map/ppermute | solution.py:263
  32.8 7.5 %collective-permute-start.11 = (f32[2,8,2,8,128]{4,3,2,1,0:T(8,128)S(1)}, f32[2,8,2,8,128]{4,3,2,1,0:T(8,128)S(1)}, u32[]{:S(2)}, u32[]{:S(2)}) collective-permute-start(f32[2,8,2,8,128]{4,3,2,1,0:T(8,128)S(1)} %get-tuple-element.46), channel_id=1, source_target_pairs={{0,1},{1,2},{2,3},{3,0},{4,5},{5,6},{6,7},{7,4},{8,9},{9,10},{10,1... | collective-permute-start | bytes 393224 | tf_op jit(solution)/shard_map/ppermute | solution.py:263
  33.5 11.3 %collective-permute-start.12 = (f32[2,8,2,8,128]{4,3,2,1,0:T(8,128)S(1)}, f32[2,8,2,8,128]{4,3,2,1,0:T(8,128)S(1)}, u32[]{:S(2)}, u32[]{:S(2)}) collective-permute-start(f32[2,8,2,8,128]{4,3,2,1,0:T(8,128)S(1)} %get-tuple-element.47), channel_id=1, source_target_pairs={{0,2},{1,3},{2,0},{3,1},{4,6},{5,7},{6,4},{7,5},{8,10},{9,11},{10,... | collective-permute-start | bytes 393224 | tf_op jit(solution)/shard_map/ppermute | solution.py:263
  35.3 9.4 %collective-permute-start.13 = (f32[2,8,2,8,128]{4,3,2,1,0:T(8,128)S(1)}, f32[2,8,2,8,128]{4,3,2,1,0:T(8,128)S(1)}, u32[]{:S(2)}, u32[]{:S(2)}) collective-permute-start(f32[2,8,2,8,128]{4,3,2,1,0:T(8,128)S(1)} %get-tuple-element.48), channel_id=1, source_target_pairs={{0,3},{1,0},{2,1},{3,2},{4,7},{5,4},{6,5},{7,6},{8,11},{9,8},{10,9... | collective-permute-start | bytes 393224 | tf_op jit(solution)/shard_map/ppermute | solution.py:263
  36.2 8.6 %collective-permute-start.14 = (f32[2,8,2,8,128]{4,3,2,1,0:T(8,128)S(1)}, f32[2,8,2,8,128]{4,3,2,1,0:T(8,128)S(1)}, u32[]{:S(2)}, u32[]{:S(2)}) collective-permute-start(f32[2,8,2,8,128]{4,3,2,1,0:T(8,128)S(1)} %get-tuple-element.49), channel_id=1, source_target_pairs={{0,4},{1,5},{2,6},{3,7},{4,0},{5,1},{6,2},{7,3},{8,12},{9,13},{10,... | collective-permute-start | bytes 393224 | tf_op jit(solution)/shard_map/ppermute | solution.py:263
  37.5 9.0 %collective-permute-start.15 = (f32[2,8,2,8,128]{4,3,2,1,0:T(8,128)S(1)}, f32[2,8,2,8,128]{4,3,2,1,0:T(8,128)S(1)}, u32[]{:S(2)}, u32[]{:S(2)}) collective-permute-start(f32[2,8,2,8,128]{4,3,2,1,0:T(8,128)S(1)} %get-tuple-element.50), channel_id=1, source_target_pairs={{0,5},{1,6},{2,7},{3,4},{4,1},{5,2},{6,3},{7,0},{8,13},{9,14},{10,... | collective-permute-start | bytes 393224 | tf_op jit(solution)/shard_map/ppermute | solution.py:263
  40.4 7.2 %collective-permute-start.17 = (f32[2,8,2,8,128]{4,3,2,1,0:T(8,128)S(1)}, f32[2,8,2,8,128]{4,3,2,1,0:T(8,128)S(1)}, u32[]{:S(2)}, u32[]{:S(2)}) collective-permute-start(f32[2,8,2,8,128]{4,3,2,1,0:T(8,128)S(1)} %get-tuple-element.53), channel_id=1, source_target_pairs={{0,7},{1,4},{2,5},{3,6},{4,3},{5,0},{6,1},{7,2},{8,15},{9,12},{10,... | collective-permute-start | bytes 393224 | tf_op jit(solution)/shard_map/ppermute | solution.py:263
  48.6 7.7 %collective-permute-start.23 = (f32[2,8,2,8,128]{4,3,2,1,0:T(8,128)S(1)}, f32[2,8,2,8,128]{4,3,2,1,0:T(8,128)S(1)}, u32[]{:S(2)}, u32[]{:S(2)}) collective-permute-start(f32[2,8,2,8,128]{4,3,2,1,0:T(8,128)S(1)} %bitcast.35), channel_id=1, source_target_pairs={{0,6},{1,7},{2,4},{3,5},{4,2},{5,3},{6,0},{7,1},{8,14},{9,15},{10,... | collective-permute-start | bytes 393224 | tf_op jit(solution)/shard_map/ppermute | solution.py:263
  51.4 8.7 %collective-permute-start.18 = (f32[2,8,2,8,128]{4,3,2,1,0:T(8,128)S(1)}, f32[2,8,2,8,128]{4,3,2,1,0:T(8,128)S(1)}, u32[]{:S(2)}, u32[]{:S(2)}) collective-permute-start(f32[2,8,2,8,128]{4,3,2,1,0:T(8,128)S(1)} %bitcast.34), channel_id=1, source_target_pairs={{0,1},{1,2},{2,3},{3,0},{4,5},{5,6},{6,7},{7,4},{8,9},{9,10},{10,1... | collective-permute-start | bytes 393224 | tf_op jit(solution)/shard_map/ppermute | solution.py:263
  52.1 11.4 %collective-permute-start.19 = (f32[2,8,2,8,128]{4,3,2,1,0:T(8,128)S(1)}, f32[2,8,2,8,128]{4,3,2,1,0:T(8,128)S(1)}, u32[]{:S(2)}, u32[]{:S(2)}) collective-permute-start(f32[2,8,2,8,128]{4,3,2,1,0:T(8,128)S(1)} %bitcast.33), channel_id=1, source_target_pairs={{0,2},{1,3},{2,0},{3,1},{4,6},{5,7},{6,4},{7,5},{8,10},{9,11},{10,... | collective-permute-start | bytes 393224 | tf_op jit(solution)/shard_map/ppermute | solution.py:263
  54.9 8.6 %collective-permute-start.20 = (f32[2,8,2,8,128]{4,3,2,1,0:T(8,128)S(1)}, f32[2,8,2,8,128]{4,3,2,1,0:T(8,128)S(1)}, u32[]{:S(2)}, u32[]{:S(2)}) collective-permute-start(f32[2,8,2,8,128]{4,3,2,1,0:T(8,128)S(1)} %bitcast.32), channel_id=1, source_target_pairs={{0,3},{1,0},{2,1},{3,2},{4,7},{5,4},{6,5},{7,6},{8,11},{9,8},{10,9... | collective-permute-start | bytes 393224 | tf_op jit(solution)/shard_map/ppermute | solution.py:263
  55.4 8.2 %collective-permute-start.21 = (f32[2,8,2,8,128]{4,3,2,1,0:T(8,128)S(1)}, f32[2,8,2,8,128]{4,3,2,1,0:T(8,128)S(1)}, u32[]{:S(2)}, u32[]{:S(2)}) collective-permute-start(f32[2,8,2,8,128]{4,3,2,1,0:T(8,128)S(1)} %bitcast.31), channel_id=1, source_target_pairs={{0,4},{1,5},{2,6},{3,7},{4,0},{5,1},{6,2},{7,3},{8,12},{9,13},{10,... | collective-permute-start | bytes 393224 | tf_op jit(solution)/shard_map/ppermute | solution.py:263
  56.3 8.0 %collective-permute-start.22 = (f32[2,8,2,8,128]{4,3,2,1,0:T(8,128)S(1)}, f32[2,8,2,8,128]{4,3,2,1,0:T(8,128)S(1)}, u32[]{:S(2)}, u32[]{:S(2)}) collective-permute-start(f32[2,8,2,8,128]{4,3,2,1,0:T(8,128)S(1)} %bitcast.30), channel_id=1, source_target_pairs={{0,5},{1,6},{2,7},{3,4},{4,1},{5,2},{6,3},{7,0},{8,13},{9,14},{10,... | collective-permute-start | bytes 393224 | tf_op jit(solution)/shard_map/ppermute | solution.py:263
  60.0 5.9 %collective-permute-start.24 = (f32[2,8,2,8,128]{4,3,2,1,0:T(8,128)S(1)}, f32[2,8,2,8,128]{4,3,2,1,0:T(8,128)S(1)}, u32[]{:S(2)}, u32[]{:S(2)}) collective-permute-start(f32[2,8,2,8,128]{4,3,2,1,0:T(8,128)S(1)} %bitcast.29), channel_id=1, source_target_pairs={{0,7},{1,4},{2,5},{3,6},{4,3},{5,0},{6,1},{7,2},{8,15},{9,12},{10,... | collective-permute-start | bytes 393224 | tf_op jit(solution)/shard_map/ppermute | solution.py:263
